TPU v7x, 32 devices: a whole 2x2x4 slice. The times are simulated.
32 devices in a mesh: row: 16 (over z, y, x), col: 2 (over core).
Axes of the slice: x: 2, y: 2, z: 4, core: 2. Of those that a mesh axis runs over, the one named last changes fastest.
Arguments:
- vectors: float32 [16384, 512], P('row', 'col'), may hold values from -6 to 6
- reflectors: float32 [2, 16384, 128], P('col', 'row'), may hold values from -0.375 to 0.375
- tfactors: float32 [2, 64, 128, 128], P('col', 'row'), may hold values from -0.05 to 1, as said below
- plan: int32 [2], replicated, may hold values from 0 to 1, each once
Outputs:
- result: float32 [16384, 512], P('row', 'col')
Inputs may be any that keep to these rules, and one draw needn't show every extreme that they name: `plan`: every stored group is applied exactly once. `tfactors`: each factor is upper triangular with diagonal between 0.2 and 1.
All inputs are finite; a program needn't handle non-finite values.
Results may differ from a plain program's by a relative error of at most 0.00019.
Values sent between devices are 32-bit elements; how exact they have to be, the bound alone decides.
No kernel may reach another device: no remote copies, remote signals or barrier semaphores. Data moves between devices by JAX's collectives and lax.ppermute only.
A program may use at most 64 MiB of HBM per device.

v0:
```python
import jax
import jax.numpy as jnp
from jax import lax
from jax.sharding import PartitionSpec as P


def from_behind(block, axis, distance):
    devices = range(lax.axis_size(axis))
    route = [(i - distance, i) for i in devices if i - distance in devices]
    return lax.ppermute(block, axis, route)


def product(left, right):
    return jnp.dot(left, right, precision=lax.Precision.HIGHEST, preferred_element_type=jnp.float32)


def project(left, right):
    return lax.dot_general(
        left,
        right,
        (((0,), (0,)), ((), ())),
        precision=lax.Precision.HIGHEST,
        preferred_element_type=jnp.float32,
    )


def apply_local(current, block, factor):
    count = factor.shape[0]
    width = block.shape[1]
    shaped = current.reshape(count, 2 * width, current.shape[1])
    refl = block.reshape(count, 2 * width, width)
    proj = jnp.einsum("kri,krc->kic", refl, shaped, precision=lax.Precision.HIGHEST)
    coeff = jnp.einsum("kij,kjc->kic", factor, proj, precision=lax.Precision.HIGHEST)
    update = jnp.einsum("kri,kic->krc", refl, coeff, precision=lax.Precision.HIGHEST)
    return (shaped - update).reshape(current.shape)


def local(vectors, reflectors, tfactors, plan):
    groups = plan.shape[0]
    strip = reflectors.shape[2]
    height = reflectors.shape[1]
    position = lax.axis_index("row")
    final = lax.axis_size("row") - 1
    every_refl, every_factor = (
        lax.all_gather(reflectors, "col", axis=0, tiled=True),
        lax.all_gather(tfactors, "col", axis=0, tiled=True),
    )

    def fetch(step):
        chosen = plan[step]
        block = lax.dynamic_index_in_dim(every_refl, chosen, 0, False)
        factor = lax.dynamic_index_in_dim(every_factor, chosen, 0, False)
        return (block, factor)

    def straddle(current, block, factor):
        inner = apply_local(
            current[strip : height - strip], block[strip : height - strip], factor[:-1]
        )
        edge_factor = factor[-1]
        upper_rows = current[:strip]
        lower_rows = current[height - strip :]
        upper_refl = block[:strip]
        lower_refl = block[height - strip :]
        got_rows, got_refl = from_behind((upper_rows, upper_refl), "row", -1)
        coeff = product(edge_factor, project(lower_refl, lower_rows) + project(got_refl, got_rows))
        coeff = jnp.where(position < final, coeff, 0.0)
        new_lower = lower_rows - product(lower_refl, coeff)
        next_upper = got_rows - product(got_refl, coeff)
        returned = from_behind(next_upper, "row", 1)
        new_upper = jnp.where(position > 0, returned, upper_rows)
        return jnp.concatenate([new_upper, inner, new_lower], axis=0)

    def pair_step(index, current):
        block, factor = fetch(2 * index)
        current = apply_local(current, block, factor)
        block, factor = fetch(2 * index + 1)
        return straddle(current, block, factor)

    return lax.fori_loop(0, groups // 2, pair_step, vectors)


def solution(mesh):
    return jax.shard_map(
        local,
        mesh=mesh,
        in_specs=(P("row", "col"), P("col", "row", None), P("col", "row", None, None), P()),
        out_specs=P("row", "col"),
        check_vma=False,
    )
```

profile of v0, /device:TPU:8, one launch (start us, length us, event | category | flops | bytes accessed | tf_op | source)
XLA Modules:
  0.0 53.3 jit_solution(17968065930790819953)
XLA Ops:
  6.5 0.7 %all-gather.2.cloned.1.call-update = ((f32[1,1024,128]{2,1,0:T(8,128)}), f32[2,1024,128]{2,1,0:T(8,128)}) async-update(((), (), s32[]{:S(2)}) %all-gather.2.cloned.1.call-start, f32[1,1024,128]{2,1,0:T(8,128)} %param.5) | async-update | bytes 2097176
  7.3 0.6 %fusion.11 = (s32[1]{0:T(128)}, s32[1]{0:T(128)}) fusion(s32[2]{0:T(128)S(1)} %copy-done.3), kind=kLoop, calls=%fused_computation.25 | loop fusion | bytes 16 | tf_op jit(solution)/shard_map/while/body/eval_jaxpr/dynamic_slice | solution.py:50
  11.7 2.2 %all_gather.7 = f32[2,4,128,128]{3,2,1,0:T(8,128)S(1)} all-gather(f32[1,4,128,128]{3,2,1,0:T(8,128)S(1)} %copy-done.2), channel_id=1, replica_groups=mesh['row'=16,'col'=2] {'col'}, dimensions={0}, use_global_device_ids=true | all-gather | bytes 786432 | tf_op jit(solution)/shard_map/all_gather | solution.py:46
  13.9 5.4 %all-gather.2.cloned.1.call-done = f32[2,1024,128]{2,1,0:T(8,128)} async-done(((f32[1,1024,128]{2,1,0:T(8,128)}), f32[2,1024,128]{2,1,0:T(8,128)}) %all-gather.2.cloned.1.call-update) | async-done | bytes 1048592 | tf_op jit(solution)/shard_map/all_gather | solution.py:45
  19.4 1.1 %constant_dynamic-slice_fusion.1 = f32[1,1024,128]{2,1,0:T(8,128)S(1)} fusion(f32[2,1024,128]{2,1,0:T(8,128)} %all-gather.2.cloned.1.call-done, s32[]{:T(128)S(6)} %select_n.37), kind=kLoop, calls=%fused_computation.24 | loop fusion | bytes 1048580 | tf_op jit(solution)/shard_map/while/body/eval_jaxpr/jit(dynamic_index_in_dim)/dynamic_slice | solution.py:51
  20.4 1.1 %fusion.12 = f32[4,128,256]{2,1,0:T(8,128)S(1)} fusion(f32[4,256,128]{2,1,0:T(8,128)S(1)} %bitcast.46, f32[4,256,256]{2,1,0:T(8,128)S(1)} %bitcast.48), kind=kOutput, calls=%fused_computation.26 | convolution fusion | flops 402653184 | bytes 2097152 | tf_op jit(solution)/shard_map/while/body/eval_jaxpr/kri,krc->kic/dot_general | solution.py:32
  21.5 0.6 %fusion = f32[4,128,256]{2,1,0:T(8,128)S(1)} fusion(f32[4,128,256]{2,1,0:T(8,128)S(1)} %fusion.12, f32[2,4,128,128]{3,2,1,0:T(8,128)S(1)} %all_gather.7, s32[]{:T(128)S(6)} %select_n.37), kind=kOutput, calls=%fused_computation.7 | convolution fusion | flops 201326592 | bytes 1310724 | tf_op jit(solution)/shard_map/while/body/eval_jaxpr/kij,kjc->kic/dot_general | solution.py:33
  22.1 1.0 %convolution_subtract_fusion = f32[4,256,256]{2,1,0:T(8,128)S(1)} fusion(f32[4,256,256]{2,1,0:T(8,128)S(1)} %bitcast.49, f32[4,256,128]{2,1,0:T(8,128)S(1)} %bitcast.47, f32[4,128,256]{2,1,0:T(8,128)S(1)} %fusion), kind=kOutput, calls=%fused_computation | convolution fusion | flops 402915328 | bytes 3145728 | tf_op jit(solution)/shard_map/while/body/eval_jaxpr/kri,kic->krc/dot_general | solution.py:34
  23.1 0.1 slice.58
  23.2 1.1 %copy-done.1 = f32[2,1024,128]{2,1,0:T(8,128)S(1)} copy-done((f32[2,1024,128]{2,1,0:T(8,128)S(1)}, f32[2,1024,128]{2,1,0:T(8,128)}, u32[]{:S(2)}) %copy-start.1) | copy-done | bytes 1048600
  24.3 4.3 %collective-permute-start.1 = (f32[128,128]{1,0:T(8,128)S(1)}, f32[128,128]{1,0:T(8,128)S(1)}, u32[]{:S(2)}, u32[]{:S(2)}) collective-permute-start(f32[128,128]{1,0:T(8,128)S(1)} %dynamic-slice_bitcast_fusion.5), channel_id=1, source_target_pairs={{2,0},{4,2},{6,4},{8,6},{10,8},{12,10},{14,12},{16,14},{18,16},{20... | collective-permute-start | bytes 196616 | tf_op jit(solution)/shard_map/while/body/eval_jaxpr/ppermute | solution.py:10
  28.6 2.5 %collective-permute-start = (f32[128,256]{1,0:T(8,128)S(1)}, f32[128,256]{1,0:T(8,128)S(1)}, u32[]{:S(2)}, u32[]{:S(2)}) collective-permute-start(f32[128,256]{1,0:T(8,128)S(1)} %slice.56), channel_id=1, source_target_pairs={{2,0},{4,2},{6,4},{8,6},{10,8},{12,10},{14,12},{16,14},{18,16},{20... | collective-permute-start | bytes 393224 | tf_op jit(solution)/shard_map/while/body/eval_jaxpr/ppermute | solution.py:10
  31.1 0.8 %fusion.13 = f32[3,128,256]{2,1,0:T(8,128)S(1)} fusion(f32[3,256,128]{2,1,0:T(8,128)S(1)} %bitcast.50, f32[3,256,256]{2,1,0:T(8,128)S(1)} %bitcast.39), kind=kOutput, calls=%fused_computation.27 | convolution fusion | flops 301989888 | bytes 1572864 | tf_op jit(solution)/shard_map/while/body/eval_jaxpr/kri,krc->kic/dot_general | solution.py:32
  32.0 0.5 fusion.3
  32.4 0.8 %convolution_subtract_fusion.1 = f32[3,256,256]{2,1,0:T(8,128)S(1)} fusion(f32[3,256,256]{2,1,0:T(8,128)S(1)} %bitcast.40, f32[3,256,128]{2,1,0:T(8,128)S(1)} %bitcast.51, f32[3,128,256]{2,1,0:T(8,128)S(1)} %fusion.3), kind=kOutput, calls=%fused_computation.1 | convolution fusion | flops 302186496 | bytes 2359296 | tf_op jit(solution)/shard_map/while/body/eval_jaxpr/kri,kic->krc/dot_general | solution.py:34
  33.2 0.3 fusion.4
  33.6 2.3 %collective-permute-done = f32[128,256]{1,0:T(8,128)S(1)} collective-permute-done((f32[128,256]{1,0:T(8,128)S(1)}, f32[128,256]{1,0:T(8,128)S(1)}, u32[]{:S(2)}, u32[]{:S(2)}) %collective-permute-start) | collective-permute-done | bytes 131104 | tf_op jit(solution)/shard_map/while/body/eval_jaxpr/ppermute | solution.py:10
  35.9 0.3 convolution_add_fusion
  36.2 0.3 convolution_select_fusion
  36.5 0.3 convolution_subtract_fusion.3
  36.8 2.5 %collective-permute-start.2 = (f32[128,256]{1,0:T(8,128)S(1)}, f32[128,256]{1,0:T(8,128)S(1)}, u32[]{:S(2)}, u32[]{:S(2)}) collective-permute-start(f32[128,256]{1,0:T(8,128)S(1)} %convolution_subtract_fusion.3), channel_id=1, source_target_pairs={{0,2},{2,4},{4,6},{6,8},{8,10},{10,12},{12,14},{14,16},{16,18},{18... | collective-permute-start | bytes 393224 | tf_op jit(solution)/shard_map/while/body/eval_jaxpr/ppermute | solution.py:10
  39.2 0.3 convolution_subtract_fusion.2
  39.5 5.9 %collective-permute-done.2 = f32[128,256]{1,0:T(8,128)S(1)} collective-permute-done((f32[128,256]{1,0:T(8,128)S(1)}, f32[128,256]{1,0:T(8,128)S(1)}, u32[]{:S(2)}, u32[]{:S(2)}) %collective-permute-start.2) | collective-permute-done | bytes 131104 | tf_op jit(solution)/shard_map/while/body/eval_jaxpr/ppermute | solution.py:10
  45.5 1.0 %pad_maximum_fusion = f32[1024,256]{1,0:T(8,128)} fusion(f32[128,256]{1,0:T(8,128)S(1)} %convolution_subtract_fusion.2, f32[768,256]{1,0:T(8,128)S(1)} %bitcast.52, f32[128,256]{1,0:T(8,128)S(1)} %broadcast_select_fusion), kind=kLoop, calls=%fused_computation.6 | loop fusion | flops 524288 | bytes 2097152 | tf_op jit(solution)/shard_map/while/body/eval_jaxpr/concatenate | solution.py:71
  (13 shorter events, 0.1 us)
Async XLA Ops:
  6.5 5.2 %copy-start.2 = (f32[1,4,128,128]{3,2,1,0:T(8,128)S(1)}, f32[1,4,128,128]{3,2,1,0:T(8,128)}, u32[]{:S(2)}) copy-start(f32[1,4,128,128]{3,2,1,0:T(8,128)} %param.6) | copy-start | bytes 786436
  6.5 12.8 %all-gather.2.cloned.1.call-start = ((), (), s32[]{:S(2)}) async-start(), calls=%async_computation | async-start | bytes 1572864 | tf_op jit(solution)/shard_map/all_gather | solution.py:45
  6.5 0.7 %copy-start.3 = (s32[2]{0:T(128)S(1)}, s32[2]{0:T(128)}, u32[]{:S(2)}) copy-start(s32[2]{0:T(128)} %param.7) | copy-start | bytes 28
  7.3 13.2 %copy-start = (f32[1024,256]{1,0:T(8,128)S(1)}, f32[1024,256]{1,0:T(8,128)}, u32[]{:S(2)}) copy-start(f32[1024,256]{1,0:T(8,128)} %param.4) | copy-start | bytes 3145732
  23.1 1.2 %copy-start.1 = (f32[2,1024,128]{2,1,0:T(8,128)S(1)}, f32[2,1024,128]{2,1,0:T(8,128)}, u32[]{:S(2)}) copy-start(f32[2,1024,128]{2,1,0:T(8,128)} %all-gather.2.cloned.1.call-done) | copy-start | bytes 3145732
  24.3 9.2 %collective-permute-start.1 = (f32[128,128]{1,0:T(8,128)S(1)}, f32[128,128]{1,0:T(8,128)S(1)}, u32[]{:S(2)}, u32[]{:S(2)}) collective-permute-start(f32[128,128]{1,0:T(8,128)S(1)} %dynamic-slice_bitcast_fusion.5), channel_id=1, source_target_pairs={{2,0},{4,2},{6,4},{8,6},{10,8},{12,10},{14,12},{16,14},{18,16},{20... | collective-permute-start | bytes 196616 | tf_op jit(solution)/shard_map/while/body/eval_jaxpr/ppermute | solution.py:10
  28.6 7.3 %collective-permute-start = (f32[128,256]{1,0:T(8,128)S(1)}, f32[128,256]{1,0:T(8,128)S(1)}, u32[]{:S(2)}, u32[]{:S(2)}) collective-permute-start(f32[128,256]{1,0:T(8,128)S(1)} %slice.56), channel_id=1, source_target_pairs={{2,0},{4,2},{6,4},{8,6},{10,8},{12,10},{14,12},{16,14},{18,16},{20... | collective-permute-start | bytes 393224 | tf_op jit(solution)/shard_map/while/body/eval_jaxpr/ppermute | solution.py:10
  36.8 8.7 %collective-permute-start.2 = (f32[128,256]{1,0:T(8,128)S(1)}, f32[128,256]{1,0:T(8,128)S(1)}, u32[]{:S(2)}, u32[]{:S(2)}) collective-permute-start(f32[128,256]{1,0:T(8,128)S(1)} %convolution_subtract_fusion.3), channel_id=1, source_target_pairs={{0,2},{2,4},{4,6},{6,8},{8,10},{10,12},{12,14},{14,16},{16,18},{18... | collective-permute-start | bytes 393224 | tf_op jit(solution)/shard_map/while/body/eval_jaxpr/ppermute | solution.py:10
Sparse Core Ops, SparseCore 0:
  8.9 10.4 all-gather.1
where the time goes:
time: 53.7 us; the launch traced here: 53.3 us
  between operations  17.4 us (32%)
  waiting for transfers between devices  14.4 us (27%)
  starting transfers between devices  9.18 us (17%)
  matrix products  6.15 us (11%)
  local copies, waits for them, and re-layouts  2.91 us (5%)
  blocking collectives  2.18 us (4%)
  other arithmetic  1.06 us (2%)
    ppermute x3, starting transfers between devices, from_behind(): return lax.ppermute(block, axis, route)  9.18 us
    ppermute x3, waiting for transfers between devices, from_behind(): return lax.ppermute(block, axis, route)  8.26 us
    all_gather x1, waiting for transfers between devices, local(): lax.all_gather(reflectors, 'col', axis=0, tiled=True)  5.45 us
    all_gather x1, blocking collectives, local(): lax.all_gather(tfactors, 'col', axis=0, tiled=True)  2.18 us
    dot_general x2, matrix products, apply_local(): jnp.einsum('kri,krc->kic', refl, shaped, precision=lax.Precision.HIGHEST)  1.9 us
    dot_general x2, matrix products, apply_local(): jnp.einsum('kri,kic->krc', refl, coeff, precision=lax.Precision.HIGHEST)  1.76 us
    unnamed x8, local copies, waits for them, and re-layouts  1.15 us
    dynamic_slice x1, local copies, waits for them, and re-layouts, fetch(): block = lax.dynamic_index_in_dim(every_refl, chosen, 0, False)  1.08 us
  transfers between devices with their start and end apart: 4, of which 3 were waited for; matrix products, arithmetic and copies ran while one was open for 6% of the time, Pallas kernels for 0%

commit v1 on v0

v1 whole, which is shorter than its diff:
```python
import jax
import jax.numpy as jnp
from jax import lax
from jax.experimental import pallas as pl
from jax.experimental.pallas import tpu as pltpu
from jax.sharding import PartitionSpec as P

F32 = jnp.float32
BF16 = jnp.bfloat16
VMEM = pl.BlockSpec(memory_space=pltpu.VMEM)
SMEM = pl.BlockSpec(memory_space=pltpu.SMEM)
ANY = pl.BlockSpec(memory_space=pl.ANY)


def split(a):
    high = a.astype(BF16)
    return high, (a - high.astype(F32)).astype(BF16)


def dot(a, b, over):
    return lax.dot_general(a, b, (((over,), (0,)), ((), ())), preferred_element_type=F32)


def product(a, b, over=1):
    (ah, al), (bh, bl) = a, b
    return dot(ah, bh, over) + (dot(ah, bl, over) + dot(al, bh, over))


def reflect(x, refl, factor):
    v = split(refl)
    coeff = product(split(factor), split(product(v, split(x), over=0)))
    return x - product(v, split(coeff))


def pick(kinds, step, pieces):
    value = pieces[0]
    for at, piece in enumerate(pieces[1:], 1):
        mask = jnp.broadcast_to(kinds[step : step + 1, :], value.shape) == at
        value = jnp.where(mask, piece, value)
    return value


def vmem_call(body, outs, specs, name, **rest):
    return pl.pallas_call(
        body,
        out_shape=outs,
        in_specs=specs,
        out_specs=[ANY if getattr(o, "far", False) else VMEM for o in outs],
        name=name,
        **rest,
    )


def shape(*dims, dtype=F32):
    return jax.ShapeDtypeStruct(dims, dtype)


def kinds_of(plan, columns, held, lanes):
    def body(plan_ref, out_ref):
        me = lax.axis_index("col")
        out_ref[...] = jnp.zeros_like(out_ref)
        for step in range(plan.shape[0]):
            group = plan_ref[step]
            home, slot = group // held, group % held
            piece = (me + columns - home) % columns * held + slot
            out_ref[step : step + 1, :] = jnp.full((1, lanes), piece, jnp.int32)

    rows = -(-plan.shape[0] // 8) * 8
    return vmem_call(body, [shape(rows, lanes, dtype=jnp.int32)], [SMEM], "kinds")(plan)[0]


def is_top(odd_round):
    return (lax.axis_index("row") % 2 == 1) != odd_round


def edge(x, refls, factors, kinds, step, odd_round):
    height, width = x.shape
    strip = refls[0].shape[1]
    count = height // (2 * strip)
    n = len(refls)

    def body(*refs):
        kinds_ref, x_ref, refs = refs[0], refs[1], refs[2:]
        refl_refs, factor_refs = refs[:n], refs[n : 2 * n]
        block_ref, proj_ref = refs[2 * n :]

        def work(at, outer):
            rows = pl.ds(at * 2 * strip, 2 * strip)
            side = pl.ds(at * 2 * strip + outer, strip)
            first = pick(kinds_ref, step, [r[rows, :] for r in refl_refs])
            factor = pick(kinds_ref, step, [r[at] for r in factor_refs])
            second = pick(kinds_ref, step + 1, [r[side, :] for r in refl_refs])
            new = reflect(x_ref[rows, :], first, factor)
            block_ref[...] = new
            proj_ref[...] = product(split(second), split(new[outer : outer + strip]), over=0)

        top = is_top(odd_round)
        pl.when(top)(lambda: work(0, 0))
        pl.when(jnp.logical_not(top))(lambda: work(count - 1, strip))

    return vmem_call(
        body,
        [shape(2 * strip, width), shape(strip, width)],
        [VMEM] * (2 + 2 * n),
        "edge",
    )(kinds, x, *refls, *factors)


def middle(x, refls, factors, kinds, step, even_block, odd_block):
    height, width = x.shape
    strip = refls[0].shape[1]
    count = height // (2 * strip)
    n = len(refls)

    def body(*refs):
        kinds_ref, x_ref, even_ref, odd_ref, refs = refs[0], refs[1], refs[2], refs[3], refs[4:]
        refl_refs, factor_refs = refs[:n], refs[n : 2 * n]
        out_ref, work_ref, sem = refs[2 * n :]
        top_even = is_top(False)
        head = jnp.where(top_even, even_ref[strip:, :], odd_ref[strip:, :])
        tail = jnp.where(top_even, odd_ref[:strip, :], even_ref[:strip, :])
        for at in range(1, count - 1):
            rows = pl.ds(at * 2 * strip, 2 * strip)
            refl = pick(kinds_ref, step, [r[rows, :] for r in refl_refs])
            factor = pick(kinds_ref, step, [r[at] for r in factor_refs])
            work_ref[rows, :] = reflect(x_ref[rows, :], refl, factor)
        work_ref[pl.ds(strip, strip), :] = head
        work_ref[pl.ds(height - 2 * strip, strip), :] = tail
        copies = []
        for at in range(count - 1):
            rows = pl.ds(at * 2 * strip + strip, 2 * strip)
            refl = pick(kinds_ref, step + 1, [r[rows, :] for r in refl_refs])
            factor = pick(kinds_ref, step + 1, [r[at] for r in factor_refs])
            work_ref[rows, :] = reflect(work_ref[rows, :], refl, factor)
            copy = pltpu.make_async_copy(work_ref.at[rows, :], out_ref.at[rows, :], sem.at[at])
            copy.start()
            copies.append(copy)
        for copy in copies:
            copy.wait()

    return pl.pallas_call(
        body,
        out_shape=shape(height, width),
        in_specs=[VMEM] * (4 + 2 * n),
        out_specs=ANY,
        scratch_shapes=[pltpu.VMEM((height, width), F32), pltpu.SemaphoreType.DMA((count - 1,))],
        name="middle",
    )(kinds, x, even_block, odd_block, *refls, *factors)


def prepare(refls, factors, behind, kinds, step, odd_round, block, proj):
    height, strip = refls[0].shape
    width = block.shape[1]
    count = height // (2 * strip)
    n = len(refls)

    def body(*refs):
        kinds_ref, block_ref, proj_ref, refs = refs[0], refs[1], refs[2], refs[3:]
        refl_refs, factor_refs, behind_refs = refs[:n], refs[n : 2 * n], refs[2 * n : 3 * n]
        rest_ref, high_ref, low_ref = refs[3 * n :]
        row, last = lax.axis_index("row"), lax.axis_size("row") - 1

        def work(start, outer, factor, present):
            refl = pick(kinds_ref, step + 1, [r[pl.ds(start, strip), :] for r in refl_refs])
            weight = product(split(refl), split(factor))
            weight = jnp.where(present, weight, jnp.zeros_like(weight))
            high, low = split(weight)
            high_ref[...] = high
            low_ref[...] = low
            own = product((high, low), split(proj_ref[...]))
            rest_ref[...] = block_ref[outer : outer + strip, :] - own

        top = is_top(odd_round)

        @pl.when(top)
        def _():
            work(0, 0, pick(kinds_ref, step + 1, [r[...] for r in behind_refs]), row > 0)

        @pl.when(jnp.logical_not(top))
        def _():
            factor = pick(kinds_ref, step + 1, [r[count - 1] for r in factor_refs])
            work(height - strip, strip, factor, row < last)

    return vmem_call(
        body,
        [shape(strip, width), shape(strip, strip, dtype=BF16), shape(strip, strip, dtype=BF16)],
        [VMEM] * (3 + 3 * n),
        "prepare",
    )(kinds, block, proj, *refls, *factors, *behind)


def finish(out, odd_round, rest, high, low, got):
    height, width = out.shape
    strip = rest.shape[0]

    def body(rest_ref, high_ref, low_ref, got_ref, _, out_ref, new_ref, sem):
        row, last = lax.axis_index("row"), lax.axis_size("row") - 1
        top = is_top(odd_round)
        present = jnp.where(top, row > 0, row < last)
        other = jnp.where(present, got_ref[...], jnp.zeros_like(got_ref))
        new_ref[...] = rest_ref[...] - product((high_ref[...], low_ref[...]), split(other))
        start = pl.multiple_of(jnp.where(top, 0, height - strip), strip)
        copy = pltpu.make_async_copy(new_ref, out_ref.at[pl.ds(start, strip), :], sem)
        copy.start()
        copy.wait()

    return pl.pallas_call(
        body,
        out_shape=shape(height, width),
        in_specs=[VMEM] * 4 + [ANY],
        out_specs=ANY,
        scratch_shapes=[pltpu.VMEM((strip, width), F32), pltpu.SemaphoreType.DMA],
        input_output_aliases={4: 0},
        name="finish",
    )(rest, high, low, got, out)


def local(vectors, reflectors, tfactors, plan):
    groups = plan.shape[0]
    held, height, strip = reflectors.shape
    rows, columns = lax.axis_size("row"), lax.axis_size("col")

    def around(block, shift):
        return lax.ppermute(block, "col", [(c, (c + shift) % columns) for c in range(columns)])

    def trade(block, odd_round):
        route = []
        for row in range(rows):
            for col in range(columns):
                there = row + 1 if (row % 2 == 1) == odd_round else row - 1
                there = (there, col) if 0 <= there < rows else (row, (col + 1) % columns)
                route.append((row * columns + col, there[0] * columns + there[1]))
        return lax.ppermute(block, ("row", "col"), route)

    def everyone(piece):
        return [piece] + [around(piece, shift) for shift in range(1, columns)]

    def apart(pieces):
        return [piece[slot] for piece in pieces for slot in range(held)]

    refls = apart(everyone(reflectors))
    factors = apart(everyone(tfactors))
    behind = lax.ppermute(tfactors[:, -1], "row", [(r, (r + 1) % rows) for r in range(rows)])
    behinds = apart(everyone(behind))
    kinds = kinds_of(plan, columns, held, strip)
    current = vectors
    for step in range(0, groups, 2):
        even_block, even_proj = edge(current, refls, factors, kinds, step, False)
        even_got = trade(even_proj, False)
        odd_block, odd_proj = edge(current, refls, factors, kinds, step, True)
        odd_got = trade(odd_proj, True)
        done = middle(current, refls, factors, kinds, step, even_block, odd_block)
        even = prepare(refls, factors, behinds, kinds, step, False, even_block, even_proj)
        odd = prepare(refls, factors, behinds, kinds, step, True, odd_block, odd_proj)
        done = finish(done, False, *even, even_got)
        current = finish(done, True, *odd, odd_got)
    return current


def solution(mesh):
    return jax.shard_map(
        local,
        mesh=mesh,
        in_specs=(P("row", "col"), P("col", "row", None), P("col", "row", None, None), P()),
        out_specs=P("row", "col"),
        check_vma=False,
    )
```

time: 53.7 us -> 32.5 us (0.61)
  the two profiles are of different devices: /device:TPU:8 before, /device:TPU:0 now
where the time goes in v1:
time: 32.5 us; the launch traced here: 32.2 us
  Pallas kernels  21.9 us (67%)
  starting transfers between devices  5.44 us (17%)
  local copies, waits for them, and re-layouts  3.63 us (11%)
  waiting for transfers between devices  1.15 us (4%)
    pallas_call x2, Pallas kernels, edge(): vmem_call(body, [shape(2 * strip, width), shape(strip, width)], [VMEM] *...  6.82 us
    pallas_call x2, Pallas kernels, prepare(): vmem_call(body, [shape(strip, width), shape(strip, strip, dtype=BF16), sh...  5.11 us
    pallas_call x1, Pallas kernels, middle(): pl.pallas_call(body, out_shape=shape(height, width), in_specs=[VMEM] * (4...  4.93 us
    pallas_call x2, Pallas kernels, finish(): pl.pallas_call(body, out_shape=shape(height, width), in_specs=[VMEM] * 4...  3.76 us
    ppermute x1, starting transfers between devices, local(): lax.ppermute(tfactors[:, -1], 'row', [(r, (r + 1) % rows) for r in range(...  2.97 us
    unnamed x12, local copies, waits for them, and re-layouts  2.79 us
    ppermute x2, starting transfers between devices, trade(): return lax.ppermute(block, ('row', 'col'), route)  1.47 us
    pallas_call x1, Pallas kernels, kinds_of(): vmem_call(body, [shape(rows, lanes, dtype=jnp.int32)], [SMEM], 'kinds')  1.26 us
  transfers between devices with their start and end apart: 6, of which 1 were waited for; matrix products, arithmetic and copies ran while one was open for 3% of the time, Pallas kernels for 62%

profile of v1, /device:TPU:0, one launch (start us, length us, event | category | flops | bytes accessed | tf_op | source)
XLA Modules:
  0.0 32.2 jit_solution(3896877539708425933)
XLA Ops:
  0.0 0.5 %collective-permute-start = (f32[1,1024,128]{2,1,0:T(8,128)}, f32[1,1024,128]{2,1,0:T(8,128)S(1)}, u32[]{:S(2)}, u32[]{:S(2)}) collective-permute-start(f32[1,1024,128]{2,1,0:T(8,128)} %param.5), channel_id=1, source_target_pairs={{0,1},{1,0},{2,3},{3,2},{4,5},{5,4},{6,7},{7,6},{8,9},{9,8},{10,11... | collective-permute-start | bytes 1572872 | tf_op jit(solution)/shard_map/ppermute | solution.py:224
  0.5 0.0 collective-permute-start.1
  0.5 0.8 %slice_bitcast_fusion = f32[1,128,128]{2,1,0:T(8,128)S(1)} fusion(f32[1,4,128,128]{3,2,1,0:T(8,128)} %param.6), kind=kLoop, calls=%fused_computation | loop fusion | bytes 131072 | tf_op jit(solution)/shard_map/squeeze | solution.py:243
  1.4 3.0 %collective-permute-start.2 = (f32[1,128,128]{2,1,0:T(8,128)S(1)}, f32[1,128,128]{2,1,0:T(8,128)S(1)}, u32[]{:S(2)}, u32[]{:S(2)}) collective-permute-start(f32[1,128,128]{2,1,0:T(8,128)S(1)} %slice_bitcast_fusion), channel_id=1, source_target_pairs={{0,2},{2,4},{4,6},{6,8},{8,10},{10,12},{12,14},{14,16},{16,18},{18... | collective-permute-start | bytes 196616 | tf_op jit(solution)/shard_map/ppermute | solution.py:243
  4.3 1.3 %kinds.1.refs_0_ = s32[8,128]{1,0:T(8,128)} custom-call(s32[2]{0:T(128)} %plan_ref.1), custom_call_target="tpu_custom_call" | custom-call | tf_op jit(solution)/shard_map/kinds/pallas_call | solution.py:69
  5.6 0.0 collective-permute-done.1
  5.6 0.0 collective-permute-done
  5.6 0.7 %copy-done.1 = f32[1,4,128,128]{3,2,1,0:T(8,128)} copy-done((f32[1,4,128,128]{3,2,1,0:T(8,128)}, f32[1,4,128,128]{3,2,1,0:T(8,128)S(1)}, u32[]{:S(2)}) %copy-start.1) | copy-done | bytes 262168
  6.3 0.2 copy-done
  6.5 3.4 %edge.3 = (f32[256,256]{1,0:T(8,128)}, f32[128,256]{1,0:T(8,128)}) custom-call(s32[8,128]{1,0:T(8,128)} %kinds.1.refs_0_, f32[1024,256]{1,0:T(8,128)} %refs_1_.5, f32[1024,128]{1,0:T(8,128)} %bitcast.8, f32[1024,128]{1,0:T(8,128)} %bitcast.13, f32[4,128,128]{2,1,0:T(8,128)} %bitcast.18, f32[4,128,128]{2,1,0:T(8,128)} %bitcast.23), custom_call_target="tpu_custom_call" | custom-call | tf_op jit(solution)/shard_map/edge/pallas_call | solution.py:101
  9.9 1.5 %collective-permute-start.5 = (f32[128,256]{1,0:T(8,128)}, f32[128,256]{1,0:T(8,128)S(1)}, u32[]{:S(2)}, u32[]{:S(2)}) collective-permute-start(f32[128,256]{1,0:T(8,128)} %get-tuple-element.21.refs_2_), channel_id=1, source_target_pairs={{0,2},{1,3},{2,0},{3,1},{4,6},{5,7},{6,4},{7,5},{8,10},{9,11},{10,... | collective-permute-start | bytes 393224 | tf_op jit(solution)/shard_map/ppermute | solution.py:233
  11.4 3.4 %edge.2 = (f32[256,256]{1,0:T(8,128)}, f32[128,256]{1,0:T(8,128)}) custom-call(s32[8,128]{1,0:T(8,128)} %kinds.1.refs_0_, f32[1024,256]{1,0:T(8,128)} %refs_1_.5, f32[1024,128]{1,0:T(8,128)} %bitcast.9, f32[1024,128]{1,0:T(8,128)} %bitcast.14, f32[4,128,128]{2,1,0:T(8,128)} %bitcast.19, f32[4,128,128]{2,1,0:T(8,128)} %bitcast.24), custom_call_target="tpu_custom_call" | custom-call | tf_op jit(solution)/shard_map/edge/pallas_call | solution.py:101
  14.8 0.0 collective-permute-done.2
  14.8 0.0 copy-start.2
  14.8 0.5 %collective-permute-start.3 = (f32[1,128,128]{2,1,0:T(8,128)S(1)}, f32[1,128,128]{2,1,0:T(8,128)S(1)}, u32[]{:S(2)}, u32[]{:S(2)}) collective-permute-start(f32[1,128,128]{2,1,0:T(8,128)S(1)} %collective-permute-done.2), channel_id=1, source_target_pairs={{0,1},{1,0},{2,3},{3,2},{4,5},{5,4},{6,7},{7,6},{8,9},{9,8},{10,11... | collective-permute-start | bytes 196616 | tf_op jit(solution)/shard_map/ppermute | solution.py:224
  15.3 1.1 %collective-permute-done.3 = f32[1,128,128]{2,1,0:T(8,128)S(1)} collective-permute-done((f32[1,128,128]{2,1,0:T(8,128)S(1)}, f32[1,128,128]{2,1,0:T(8,128)S(1)}, u32[]{:S(2)}, u32[]{:S(2)}) %collective-permute-start.3) | collective-permute-done | bytes 65568 | tf_op jit(solution)/shard_map/ppermute | solution.py:224
  16.4 0.6 %copy-done.3 = f32[1,128,128]{2,1,0:T(8,128)} copy-done((f32[1,128,128]{2,1,0:T(8,128)}, f32[1,128,128]{2,1,0:T(8,128)S(1)}, u32[]{:S(2)}) %copy-start.3) | copy-done | bytes 65560
  17.0 2.6 %prepare.2 = (f32[128,256]{1,0:T(8,128)}, bf16[128,128]{1,0:T(8,128)(2,1)}, bf16[128,128]{1,0:T(8,128)(2,1)}) custom-call(s32[8,128]{1,0:T(8,128)} %kinds.1.refs_0_, f32[256,256]{1,0:T(8,128)} %get-tuple-element.15.refs_1_.refs_3_, f32[128,256]{1,0:T(8,128)} %get-tuple-element.16.refs_2_, f32[1024,128]{1,0:T(8,128)} %bitcast.10, f32[1024,128]{1,0:T(8,128)} %bitcast.15, ...), custom_call_target="tpu_custom_call" | custom-call | tf_op jit(solution)/shard_map/prepare/pallas_call | solution.py:184
  19.6 2.6 %prepare.3 = (f32[128,256]{1,0:T(8,128)}, bf16[128,128]{1,0:T(8,128)(2,1)}, bf16[128,128]{1,0:T(8,128)(2,1)}) custom-call(s32[8,128]{1,0:T(8,128)} %kinds.1.refs_0_, f32[256,256]{1,0:T(8,128)} %get-tuple-element.20.refs_1_.refs_2_, f32[128,256]{1,0:T(8,128)} %get-tuple-element.21.refs_2_, f32[1024,128]{1,0:T(8,128)} %bitcast.11, f32[1024,128]{1,0:T(8,128)} %bitcast.16, ...), custom_call_target="tpu_custom_call" | custom-call | tf_op jit(solution)/shard_map/prepare/pallas_call | solution.py:184
  22.1 4.9 %middle.1._ = f32[1024,256]{1,0:T(8,128)} custom-call(s32[8,128]{1,0:T(8,128)} %kinds.1.refs_0_, f32[1024,256]{1,0:T(8,128)} %refs_1_.5, f32[256,256]{1,0:T(8,128)} %get-tuple-element.20.refs_1_.refs_2_, f32[256,256]{1,0:T(8,128)} %get-tuple-element.15.refs_1_.refs_3_, f32[1024,128]{1,0:T(8,128)} %bitcast.12, f32[1024,128]{1,0:T(8,128)} %bitcast.17, ...), custom_call_target="tpu_custom_call" | custom-call | tf_op jit(solution)/shard_map/middle/pallas_call | solution.py:141
  27.1 0.6 %copy-done.5 = f32[128,256]{1,0:T(8,128)} copy-done((f32[128,256]{1,0:T(8,128)}, f32[128,256]{1,0:T(8,128)S(1)}, u32[]{:S(2)}) %copy-start.5) | copy-done | bytes 131096
  27.7 1.9 %finish.2._ = f32[1024,256]{1,0:T(8,128)} custom-call(f32[128,256]{1,0:T(8,128)} %get-tuple-element.22.rest_ref, bf16[128,128]{1,0:T(8,128)(2,1)} %get-tuple-element.23.high_ref, bf16[128,128]{1,0:T(8,128)(2,1)} %get-tuple-element.24.low_ref, f32[128,256]{1,0:T(8,128)} %copy-done.5, f32[1024,256]{1,0:T(8,128)} %middle.1._), custom_call_target="tpu_custom_call", output_to_operand_aliasing={{}: (4, {})} | custom-call | tf_op jit(solution)/shard_map/finish/pallas_call | solution.py:207
  29.6 0.6 %copy-done.4 = f32[128,256]{1,0:T(8,128)} copy-done((f32[128,256]{1,0:T(8,128)}, f32[128,256]{1,0:T(8,128)S(1)}, u32[]{:S(2)}) %copy-start.4) | copy-done | bytes 131096
  30.3 1.9 %finish.3 = f32[1024,256]{1,0:T(8,128)} custom-call(f32[128,256]{1,0:T(8,128)} %get-tuple-element.17.rest_ref, bf16[128,128]{1,0:T(8,128)(2,1)} %get-tuple-element.18.high_ref, bf16[128,128]{1,0:T(8,128)(2,1)} %get-tuple-element.19.low_ref, f32[128,256]{1,0:T(8,128)} %copy-done.4, f32[1024,256]{1,0:T(8,128)} %finish.2._), custom_call_target="tpu_custom_call", output_to_operand_aliasing={{}: (4, {})} | custom-call | tf_op jit(solution)/shard_map/finish/pallas_call | solution.py:207
  (9 shorter events, 0.0 us)
Async XLA Ops:
  0.0 5.6 %collective-permute-start = (f32[1,1024,128]{2,1,0:T(8,128)}, f32[1,1024,128]{2,1,0:T(8,128)S(1)}, u32[]{:S(2)}, u32[]{:S(2)}) collective-permute-start(f32[1,1024,128]{2,1,0:T(8,128)} %param.5), channel_id=1, source_target_pairs={{0,1},{1,0},{2,3},{3,2},{4,5},{5,4},{6,7},{7,6},{8,9},{9,8},{10,11... | collective-permute-start | bytes 1572872 | tf_op jit(solution)/shard_map/ppermute | solution.py:224
  0.5 5.1 %collective-permute-start.1 = (f32[1,4,128,128]{3,2,1,0:T(8,128)}, f32[1,4,128,128]{3,2,1,0:T(8,128)S(1)}, u32[]{:S(2)}, u32[]{:S(2)}) collective-permute-start(f32[1,4,128,128]{3,2,1,0:T(8,128)} %param.6), channel_id=1, source_target_pairs={{0,1},{1,0},{2,3},{3,2},{4,5},{5,4},{6,7},{7,6},{8,9},{9,8},{10,11... | collective-permute-start | bytes 786440 | tf_op jit(solution)/shard_map/ppermute | solution.py:224
  1.4 13.4 %collective-permute-start.2 = (f32[1,128,128]{2,1,0:T(8,128)S(1)}, f32[1,128,128]{2,1,0:T(8,128)S(1)}, u32[]{:S(2)}, u32[]{:S(2)}) collective-permute-start(f32[1,128,128]{2,1,0:T(8,128)S(1)} %slice_bitcast_fusion), channel_id=1, source_target_pairs={{0,2},{2,4},{4,6},{6,8},{8,10},{10,12},{12,14},{14,16},{16,18},{18... | collective-permute-start | bytes 196616 | tf_op jit(solution)/shard_map/ppermute | solution.py:243
  5.6 0.7 %copy-start.1 = (f32[1,4,128,128]{3,2,1,0:T(8,128)}, f32[1,4,128,128]{3,2,1,0:T(8,128)S(1)}, u32[]{:S(2)}) copy-start(f32[1,4,128,128]{3,2,1,0:T(8,128)S(1)} %collective-permute-done.1) | copy-start | bytes 786436
  5.6 0.9 %copy-start = (f32[1,1024,128]{2,1,0:T(8,128)}, f32[1,1024,128]{2,1,0:T(8,128)S(1)}, u32[]{:S(2)}) copy-start(f32[1,1024,128]{2,1,0:T(8,128)S(1)} %collective-permute-done) | copy-start | bytes 1572868
  9.9 17.2 %collective-permute-start.5 = (f32[128,256]{1,0:T(8,128)}, f32[128,256]{1,0:T(8,128)S(1)}, u32[]{:S(2)}, u32[]{:S(2)}) collective-permute-start(f32[128,256]{1,0:T(8,128)} %get-tuple-element.21.refs_2_), channel_id=1, source_target_pairs={{0,2},{1,3},{2,0},{3,1},{4,6},{5,7},{6,4},{7,5},{8,10},{9,11},{10,... | collective-permute-start | bytes 393224 | tf_op jit(solution)/shard_map/ppermute | solution.py:233
  14.8 14.9 %collective-permute-start.4 = (f32[128,256]{1,0:T(8,128)}, f32[128,256]{1,0:T(8,128)S(1)}, u32[]{:S(2)}, u32[]{:S(2)}) collective-permute-start(f32[128,256]{1,0:T(8,128)} %get-tuple-element.16.refs_2_), channel_id=1, source_target_pairs={{0,1},{1,0},{2,4},{3,5},{4,2},{5,3},{6,8},{7,9},{8,6},{9,7},{10,12... | collective-permute-start | bytes 393224 | tf_op jit(solution)/shard_map/ppermute | solution.py:233
  14.8 1.6 %copy-start.2 = (f32[1,128,128]{2,1,0:T(8,128)}, f32[1,128,128]{2,1,0:T(8,128)S(1)}, u32[]{:S(2)}) copy-start(f32[1,128,128]{2,1,0:T(8,128)S(1)} %collective-permute-done.2) | copy-start | bytes 196612
  14.8 1.6 %collective-permute-start.3 = (f32[1,128,128]{2,1,0:T(8,128)S(1)}, f32[1,128,128]{2,1,0:T(8,128)S(1)}, u32[]{:S(2)}, u32[]{:S(2)}) collective-permute-start(f32[1,128,128]{2,1,0:T(8,128)S(1)} %collective-permute-done.2), channel_id=1, source_target_pairs={{0,1},{1,0},{2,3},{3,2},{4,5},{5,4},{6,7},{7,6},{8,9},{9,8},{10,11... | collective-permute-start | bytes 196616 | tf_op jit(solution)/shard_map/ppermute | solution.py:224
  16.4 0.6 %copy-start.3 = (f32[1,128,128]{2,1,0:T(8,128)}, f32[1,128,128]{2,1,0:T(8,128)S(1)}, u32[]{:S(2)}) copy-start(f32[1,128,128]{2,1,0:T(8,128)S(1)} %collective-permute-done.3) | copy-start | bytes 196612
  27.1 0.6 %copy-start.5 = (f32[128,256]{1,0:T(8,128)}, f32[128,256]{1,0:T(8,128)S(1)}, u32[]{:S(2)}) copy-start(f32[128,256]{1,0:T(8,128)S(1)} %collective-permute-done.5.got_ref) | copy-start | bytes 393220
  29.6 0.7 %copy-start.4 = (f32[128,256]{1,0:T(8,128)}, f32[128,256]{1,0:T(8,128)S(1)}, u32[]{:S(2)}) copy-start(f32[128,256]{1,0:T(8,128)S(1)} %collective-permute-done.4.got_ref) | copy-start | bytes 393220

commit v2 on v1

--- a/solution.py
+++ b/solution.py
@@ -10,6 +10,7 @@
 VMEM = pl.BlockSpec(memory_space=pltpu.VMEM)
 SMEM = pl.BlockSpec(memory_space=pltpu.SMEM)
 ANY = pl.BlockSpec(memory_space=pl.ANY)
+LEAN = pltpu.CompilerParams(vmem_limit_bytes=8 << 20)
 
 
 def split(a):
@@ -45,14 +46,19 @@
         body,
         out_shape=outs,
         in_specs=specs,
-        out_specs=[ANY if getattr(o, "far", False) else VMEM for o in outs],
+        out_specs=[VMEM] * len(outs),
         name=name,
+        compiler_params=LEAN,
         **rest,
     )
 
 
 def shape(*dims, dtype=F32):
-    return jax.ShapeDtypeStruct(dims, dtype)
+    return pltpu.VMEM(dims, dtype)
+
+
+def near(*values):
+    return [pltpu.with_memory_space_constraint(value, pltpu.VMEM) for value in values]
 
 
 def kinds_of(plan, columns, held, lanes):
@@ -103,7 +109,7 @@
         [shape(2 * strip, width), shape(strip, width)],
         [VMEM] * (2 + 2 * n),
         "edge",
-    )(kinds, x, *refls, *factors)
+    )(*near(kinds, x, *refls, *factors))
 
 
 def middle(x, refls, factors, kinds, step, even_block, odd_block):
@@ -140,12 +146,13 @@
 
     return pl.pallas_call(
         body,
-        out_shape=shape(height, width),
+        out_shape=jax.ShapeDtypeStruct((height, width), F32),
         in_specs=[VMEM] * (4 + 2 * n),
         out_specs=ANY,
         scratch_shapes=[pltpu.VMEM((height, width), F32), pltpu.SemaphoreType.DMA((count - 1,))],
         name="middle",
-    )(kinds, x, even_block, odd_block, *refls, *factors)
+        compiler_params=LEAN,
+    )(*near(kinds, x, even_block, odd_block, *refls, *factors))
 
 
 def prepare(refls, factors, behind, kinds, step, odd_round, block, proj):
@@ -186,7 +193,7 @@
         [shape(strip, width), shape(strip, strip, dtype=BF16), shape(strip, strip, dtype=BF16)],
         [VMEM] * (3 + 3 * n),
         "prepare",
-    )(kinds, block, proj, *refls, *factors, *behind)
+    )(*near(kinds, block, proj, *refls, *factors, *behind))
 
 
 def finish(out, odd_round, rest, high, low, got):
@@ -206,13 +213,14 @@
 
     return pl.pallas_call(
         body,
-        out_shape=shape(height, width),
+        out_shape=jax.ShapeDtypeStruct((height, width), F32),
         in_specs=[VMEM] * 4 + [ANY],
         out_specs=ANY,
         scratch_shapes=[pltpu.VMEM((strip, width), F32), pltpu.SemaphoreType.DMA],
         input_output_aliases={4: 0},
         name="finish",
-    )(rest, high, low, got, out)
+        compiler_params=LEAN,
+    )(*near(rest, high, low, got), out)
 
 
 def local(vectors, reflectors, tfactors, plan):

time: 32.5 us -> 19.3 us (0.59)
  the two profiles are of different devices: /device:TPU:0 before, /device:TPU:19 now
where the time goes in v2:
time: 19.3 us; the launch traced here: 19.1 us
  Pallas kernels  8.21 us (43%)
  starting transfers between devices  5.76 us (30%)
  local copies, waits for them, and re-layouts  4.07 us (21%)
  waiting for transfers between devices  0.92 us (5%)
    unnamed x12, local copies, waits for them, and re-layouts  3.22 us
    pallas_call x1, Pallas kernels, middle(): pl.pallas_call(body, out_shape=jax.ShapeDtypeStruct((height, width), F32)...  3.14 us
    ppermute x2, starting transfers between devices, trade(): return lax.ppermute(block, ('row', 'col'), route)  2.53 us
    ppermute x3, starting transfers between devices, around(): lax.ppermute(block, 'col', [(c, (c + shift) % columns) for c in range(col...  2.03 us
    pallas_call x2, Pallas kernels, edge(): vmem_call(body, [shape(2 * strip, width), shape(strip, width)], [VMEM] *...  1.97 us
    pallas_call x2, Pallas kernels, finish(): pl.pallas_call(body, out_shape=jax.ShapeDtypeStruct((height, width), F32)...  1.78 us
    ppermute x1, starting transfers between devices, local(): lax.ppermute(tfactors[:, -1], 'row', [(r, (r + 1) % rows) for r in range(...  1.21 us
    ppermute x3, waiting for transfers between devices, around(): lax.ppermute(block, 'col', [(c, (c + shift) % columns) for c in range(col...  0.91 us
  transfers between devices with their start and end apart: 6, of which 1 were waited for; matrix products, arithmetic and copies ran while one was open for 4% of the time, Pallas kernels for 38%

profile of v2, /device:TPU:19, one launch (start us, length us, event | category | flops | bytes accessed | tf_op | source)
XLA Modules:
  0.0 19.1 jit_solution(6601318167913881116)
XLA Ops:
  0.0 0.7 %collective-permute-start = (f32[1,1024,128]{2,1,0:T(8,128)}, f32[1,1024,128]{2,1,0:T(8,128)S(1)}, u32[]{:S(2)}, u32[]{:S(2)}) collective-permute-start(f32[1,1024,128]{2,1,0:T(8,128)} %param.5), channel_id=1, source_target_pairs={{0,1},{1,0},{2,3},{3,2},{4,5},{5,4},{6,7},{7,6},{8,9},{9,8},{10,11... | collective-permute-start | bytes 1572872 | tf_op jit(solution)/shard_map/ppermute | solution.py:232
  0.7 0.1 collective-permute-start.1
  0.7 0.8 %slice_bitcast_fusion = f32[1,128,128]{2,1,0:T(8,128)S(1)} fusion(f32[1,4,128,128]{3,2,1,0:T(8,128)} %param.6), kind=kLoop, calls=%fused_computation | loop fusion | bytes 131072 | tf_op jit(solution)/shard_map/squeeze | solution.py:251
  1.6 1.2 %collective-permute-start.2 = (f32[1,128,128]{2,1,0:T(8,128)S(1)}, f32[1,128,128]{2,1,0:T(8,128)S(1)}, u32[]{:S(2)}, u32[]{:S(2)}) collective-permute-start(f32[1,128,128]{2,1,0:T(8,128)S(1)} %slice_bitcast_fusion), channel_id=1, source_target_pairs={{0,2},{2,4},{4,6},{6,8},{8,10},{10,12},{12,14},{14,16},{16,18},{18... | collective-permute-start | bytes 196616 | tf_op jit(solution)/shard_map/ppermute | solution.py:251
  2.8 0.6 %kinds.1.refs_0_ = s32[8,128]{1,0:T(8,128)S(1)} custom-call(s32[2]{0:T(128)S(1)} %copy-done.5), custom_call_target="tpu_custom_call" | custom-call | tf_op jit(solution)/shard_map/kinds/pallas_call | solution.py:75
  3.4 0.0 collective-permute-done.1
  3.4 0.0 collective-permute-done
  3.4 0.0 copy-start
  3.4 1.0 %copy-done = f32[1,1024,128]{2,1,0:T(8,128)S(1)} copy-done((f32[1,1024,128]{2,1,0:T(8,128)S(1)}, f32[1,1024,128]{2,1,0:T(8,128)}, u32[]{:S(2)}) %copy-start) | copy-done | bytes 524312
  4.4 1.2 %copy-done.2 = f32[1024,256]{1,0:T(8,128)S(1)} copy-done((f32[1024,256]{1,0:T(8,128)S(1)}, f32[1024,256]{1,0:T(8,128)}, u32[]{:S(2)}) %copy-start.2) | copy-done | bytes 1048600
  5.7 0.9 %copy-done.3 = f32[1,4,128,128]{3,2,1,0:T(8,128)S(1)} copy-done((f32[1,4,128,128]{3,2,1,0:T(8,128)S(1)}, f32[1,4,128,128]{3,2,1,0:T(8,128)}, u32[]{:S(2)}) %copy-start.3) | copy-done | bytes 262168
  6.6 1.0 %edge.3 = (f32[256,256]{1,0:T(8,128)S(1)}, f32[128,256]{1,0:T(8,128)S(1)}) custom-call(s32[8,128]{1,0:T(8,128)S(1)} %kinds.1.refs_0_, f32[1024,256]{1,0:T(8,128)S(1)} %copy-done.2, f32[1024,128]{1,0:T(8,128)S(1)} %bitcast.8, f32[1024,128]{1,0:T(8,128)S(1)} %bitcast.13, f32[4,128,128]{2,1,0:T(8,128)S(1)} %bitcast.18, f32[4,128,128]{2,1,0:T(8,128)S(1)} %bitcast.23), custom_call_target="tpu_custom_call" | custom-call | tf_op jit(solution)/shard_map/edge/pallas_call | solution.py:107
  7.6 0.0 copy-start.1
  7.6 0.3 %collective-permute-start.5 = (f32[128,256]{1,0:T(8,128)S(1)}, f32[128,256]{1,0:T(8,128)S(1)}, u32[]{:S(2)}, u32[]{:S(2)}) collective-permute-start(f32[128,256]{1,0:T(8,128)S(1)} %get-tuple-element.21.refs_2_), channel_id=1, source_target_pairs={{0,2},{1,3},{2,0},{3,1},{4,6},{5,7},{6,4},{7,5},{8,10},{9,11},{10,... | collective-permute-start | bytes 393224 | tf_op jit(solution)/shard_map/ppermute | solution.py:241
  8.0 1.0 %edge.2 = (f32[256,256]{1,0:T(8,128)S(1)}, f32[128,256]{1,0:T(8,128)S(1)}) custom-call(s32[8,128]{1,0:T(8,128)S(1)} %kinds.1.refs_0_, f32[1024,256]{1,0:T(8,128)S(1)} %copy-done.2, f32[1024,128]{1,0:T(8,128)S(1)} %bitcast.9, f32[1024,128]{1,0:T(8,128)S(1)} %bitcast.14, f32[4,128,128]{2,1,0:T(8,128)S(1)} %bitcast.19, f32[4,128,128]{2,1,0:T(8,128)S(1)} %bitcast.24), custom_call_target="tpu_custom_call" | custom-call | tf_op jit(solution)/shard_map/edge/pallas_call | solution.py:107
  9.0 2.2 %collective-permute-start.4 = (f32[128,256]{1,0:T(8,128)S(1)}, f32[128,256]{1,0:T(8,128)S(1)}, u32[]{:S(2)}, u32[]{:S(2)}) collective-permute-start(f32[128,256]{1,0:T(8,128)S(1)} %get-tuple-element.16.refs_2_), channel_id=1, source_target_pairs={{0,1},{1,0},{2,4},{3,5},{4,2},{5,3},{6,8},{7,9},{8,6},{9,7},{10,12... | collective-permute-start | bytes 393224 | tf_op jit(solution)/shard_map/ppermute | solution.py:241
  11.1 0.0 collective-permute-done.2
  11.1 1.3 %collective-permute-start.3 = (f32[1,128,128]{2,1,0:T(8,128)S(1)}, f32[1,128,128]{2,1,0:T(8,128)S(1)}, u32[]{:S(2)}, u32[]{:S(2)}) collective-permute-start(f32[1,128,128]{2,1,0:T(8,128)S(1)} %collective-permute-done.2), channel_id=1, source_target_pairs={{0,1},{1,0},{2,3},{3,2},{4,5},{5,4},{6,7},{7,6},{8,9},{9,8},{10,11... | collective-permute-start | bytes 196616 | tf_op jit(solution)/shard_map/ppermute | solution.py:232
  12.4 0.9 %collective-permute-done.3 = f32[1,128,128]{2,1,0:T(8,128)S(1)} collective-permute-done((f32[1,128,128]{2,1,0:T(8,128)S(1)}, f32[1,128,128]{2,1,0:T(8,128)S(1)}, u32[]{:S(2)}, u32[]{:S(2)}) %collective-permute-start.3) | collective-permute-done | bytes 65568 | tf_op jit(solution)/shard_map/ppermute | solution.py:232
  13.3 0.4 %prepare.2 = (f32[128,256]{1,0:T(8,128)S(1)}, bf16[128,128]{1,0:T(8,128)(2,1)S(1)}, bf16[128,128]{1,0:T(8,128)(2,1)S(1)}) custom-call(s32[8,128]{1,0:T(8,128)S(1)} %kinds.1.refs_0_, f32[256,256]{1,0:T(8,128)S(1)} %get-tuple-element.15.refs_1_.refs_3_, f32[128,256]{1,0:T(8,128)S(1)} %get-tuple-element.16.refs_2_, f32[1024,128]{1,0:T(8,128)S(1)} %bitcast.10, ...), custom_call_target="tpu_custom_call" | custom-call | tf_op jit(solution)/shard_map/prepare/pallas_call | solution.py:191
  13.7 0.4 %prepare.3 = (f32[128,256]{1,0:T(8,128)S(1)}, bf16[128,128]{1,0:T(8,128)(2,1)S(1)}, bf16[128,128]{1,0:T(8,128)(2,1)S(1)}) custom-call(s32[8,128]{1,0:T(8,128)S(1)} %kinds.1.refs_0_, f32[256,256]{1,0:T(8,128)S(1)} %get-tuple-element.20.refs_1_.refs_2_, f32[128,256]{1,0:T(8,128)S(1)} %get-tuple-element.21.refs_2_, f32[1024,128]{1,0:T(8,128)S(1)} %bitcast.11, ...), custom_call_target="tpu_custom_call" | custom-call | tf_op jit(solution)/shard_map/prepare/pallas_call | solution.py:191
  14.1 3.1 %middle.1._ = f32[1024,256]{1,0:T(8,128)} custom-call(s32[8,128]{1,0:T(8,128)S(1)} %kinds.1.refs_0_, f32[1024,256]{1,0:T(8,128)S(1)} %copy-done.2, f32[256,256]{1,0:T(8,128)S(1)} %get-tuple-element.20.refs_1_.refs_2_, f32[256,256]{1,0:T(8,128)S(1)} %get-tuple-element.15.refs_1_.refs_3_, f32[1024,128]{1,0:T(8,128)S(1)} %bitcast.12, f32[1024,128]{1,0:T(8,128)S(1)} %bitcast.17, ...), custom_call_target="tpu_custom_call" | custom-call | tf_op jit(solution)/shard_map/middle/pallas_call | solution.py:147
  17.3 0.9 %finish.2._ = f32[1024,256]{1,0:T(8,128)} custom-call(f32[128,256]{1,0:T(8,128)S(1)} %get-tuple-element.22.rest_ref, bf16[128,128]{1,0:T(8,128)(2,1)S(1)} %get-tuple-element.23.high_ref, bf16[128,128]{1,0:T(8,128)(2,1)S(1)} %get-tuple-element.24.low_ref, f32[128,256]{1,0:T(8,128)S(1)} %collective-permute-done.5.got_ref, ...), custom_call_target="tpu_custom_call", output_to_operand_aliasing={{}: (4, {})} | custom-call | tf_op jit(solution)/shard_map/finish/pallas_call | solution.py:214
  18.2 0.9 %finish.3 = f32[1024,256]{1,0:T(8,128)} custom-call(f32[128,256]{1,0:T(8,128)S(1)} %get-tuple-element.17.rest_ref, bf16[128,128]{1,0:T(8,128)(2,1)S(1)} %get-tuple-element.18.high_ref, bf16[128,128]{1,0:T(8,128)(2,1)S(1)} %get-tuple-element.19.low_ref, f32[128,256]{1,0:T(8,128)S(1)} %collective-permute-done.4.got_ref, ...), custom_call_target="tpu_custom_call", output_to_operand_aliasing={{}: (4, {})} | custom-call | tf_op jit(solution)/shard_map/finish/pallas_call | solution.py:214
  (9 shorter events, 0.0 us)
Async XLA Ops:
  0.0 2.8 %copy-start.5 = (s32[2]{0:T(128)S(1)}, s32[2]{0:T(128)}, u32[]{:S(2)}) copy-start(s32[2]{0:T(128)} %plan_ref.1) | copy-start | bytes 28
  0.0 3.4 %collective-permute-start = (f32[1,1024,128]{2,1,0:T(8,128)}, f32[1,1024,128]{2,1,0:T(8,128)S(1)}, u32[]{:S(2)}, u32[]{:S(2)}) collective-permute-start(f32[1,1024,128]{2,1,0:T(8,128)} %param.5), channel_id=1, source_target_pairs={{0,1},{1,0},{2,3},{3,2},{4,5},{5,4},{6,7},{7,6},{8,9},{9,8},{10,11... | collective-permute-start | bytes 1572872 | tf_op jit(solution)/shard_map/ppermute | solution.py:232
  0.7 2.7 %collective-permute-start.1 = (f32[1,4,128,128]{3,2,1,0:T(8,128)}, f32[1,4,128,128]{3,2,1,0:T(8,128)S(1)}, u32[]{:S(2)}, u32[]{:S(2)}) collective-permute-start(f32[1,4,128,128]{3,2,1,0:T(8,128)} %param.6), channel_id=1, source_target_pairs={{0,1},{1,0},{2,3},{3,2},{4,5},{5,4},{6,7},{7,6},{8,9},{9,8},{10,11... | collective-permute-start | bytes 786440 | tf_op jit(solution)/shard_map/ppermute | solution.py:232
  1.6 9.6 %collective-permute-start.2 = (f32[1,128,128]{2,1,0:T(8,128)S(1)}, f32[1,128,128]{2,1,0:T(8,128)S(1)}, u32[]{:S(2)}, u32[]{:S(2)}) collective-permute-start(f32[1,128,128]{2,1,0:T(8,128)S(1)} %slice_bitcast_fusion), channel_id=1, source_target_pairs={{0,2},{2,4},{4,6},{6,8},{8,10},{10,12},{12,14},{14,16},{16,18},{18... | collective-permute-start | bytes 196616 | tf_op jit(solution)/shard_map/ppermute | solution.py:251
  3.4 1.0 %copy-start = (f32[1,1024,128]{2,1,0:T(8,128)S(1)}, f32[1,1024,128]{2,1,0:T(8,128)}, u32[]{:S(2)}) copy-start(f32[1,1024,128]{2,1,0:T(8,128)} %param.5) | copy-start | bytes 1572868
  4.4 1.2 %copy-start.2 = (f32[1024,256]{1,0:T(8,128)S(1)}, f32[1024,256]{1,0:T(8,128)}, u32[]{:S(2)}) copy-start(f32[1024,256]{1,0:T(8,128)} %refs_1_.5) | copy-start | bytes 3145732
  5.7 0.9 %copy-start.3 = (f32[1,4,128,128]{3,2,1,0:T(8,128)S(1)}, f32[1,4,128,128]{3,2,1,0:T(8,128)}, u32[]{:S(2)}) copy-start(f32[1,4,128,128]{3,2,1,0:T(8,128)} %param.6) | copy-start | bytes 786436
  6.6 1.3 %copy-start.4 = (f32[1,4,128,128]{3,2,1,0:T(8,128)S(1)}, f32[1,4,128,128]{3,2,1,0:T(8,128)}, u32[]{:S(2)}) copy-start(f32[1,4,128,128]{3,2,1,0:T(8,128)} %param.6) | copy-start | bytes 786436
  7.6 5.7 %copy-start.1 = (f32[1,1024,128]{2,1,0:T(8,128)S(1)}, f32[1,1024,128]{2,1,0:T(8,128)}, u32[]{:S(2)}) copy-start(f32[1,1024,128]{2,1,0:T(8,128)} %param.5) | copy-start | bytes 1572868
  7.6 9.7 %collective-permute-start.5 = (f32[128,256]{1,0:T(8,128)S(1)}, f32[128,256]{1,0:T(8,128)S(1)}, u32[]{:S(2)}, u32[]{:S(2)}) collective-permute-start(f32[128,256]{1,0:T(8,128)S(1)} %get-tuple-element.21.refs_2_), channel_id=1, source_target_pairs={{0,2},{1,3},{2,0},{3,1},{4,6},{5,7},{6,4},{7,5},{8,10},{9,11},{10,... | collective-permute-start | bytes 393224 | tf_op jit(solution)/shard_map/ppermute | solution.py:241
  9.0 9.2 %collective-permute-start.4 = (f32[128,256]{1,0:T(8,128)S(1)}, f32[128,256]{1,0:T(8,128)S(1)}, u32[]{:S(2)}, u32[]{:S(2)}) collective-permute-start(f32[128,256]{1,0:T(8,128)S(1)} %get-tuple-element.16.refs_2_), channel_id=1, source_target_pairs={{0,1},{1,0},{2,4},{3,5},{4,2},{5,3},{6,8},{7,9},{8,6},{9,7},{10,12... | collective-permute-start | bytes 393224 | tf_op jit(solution)/shard_map/ppermute | solution.py:241
  11.1 2.2 %collective-permute-start.3 = (f32[1,128,128]{2,1,0:T(8,128)S(1)}, f32[1,128,128]{2,1,0:T(8,128)S(1)}, u32[]{:S(2)}, u32[]{:S(2)}) collective-permute-start(f32[1,128,128]{2,1,0:T(8,128)S(1)} %collective-permute-done.2), channel_id=1, source_target_pairs={{0,1},{1,0},{2,3},{3,2},{4,5},{5,4},{6,7},{7,6},{8,9},{9,8},{10,11... | collective-permute-start | bytes 196616 | tf_op jit(solution)/shard_map/ppermute | solution.py:232

commit v3 on v2

v3 whole, which is shorter than its diff:
```python
import jax
import jax.numpy as jnp
from jax import lax
from jax.experimental import pallas as pl
from jax.experimental.pallas import tpu as pltpu
from jax.sharding import PartitionSpec as P

F32 = jnp.float32
BF16 = jnp.bfloat16
VMEM = pl.BlockSpec(memory_space=pltpu.VMEM)
HBM = pl.BlockSpec(memory_space=pltpu.HBM)
ANY = pl.BlockSpec(memory_space=pl.ANY)
LEAN = pltpu.CompilerParams(vmem_limit_bytes=8 << 20)


def split(a):
    high = a.astype(BF16)
    return high, (a - high.astype(F32)).astype(BF16)


def dot(a, b, over):
    return lax.dot_general(a, b, (((over,), (0,)), ((), ())), preferred_element_type=F32)


def product(a, b, over=1):
    (ah, al), (bh, bl) = a, b
    return dot(ah, bh, over) + (dot(ah, bl, over) + dot(al, bh, over))


def reflect(x, refl, factor):
    v = split(refl)
    coeff = product(split(factor), split(product(v, split(x), over=0)))
    return x - product(v, split(coeff))


def pick(kinds, step, pieces):
    value = pieces[0]
    for at, piece in enumerate(pieces[1:], 1):
        mask = jnp.broadcast_to(kinds[step : step + 1, :], value.shape) == at
        value = jnp.where(mask, piece, value)
    return value


def shape(*dims, dtype=F32):
    return pltpu.VMEM(dims, dtype)


def near(*values, space=pltpu.VMEM):
    return [pltpu.with_memory_space_constraint(value, space) for value in values]


def vmem_call(body, outs, name, *args):
    return pl.pallas_call(
        body,
        out_shape=outs,
        in_specs=[VMEM] * len(args),
        out_specs=[VMEM] * len(outs),
        name=name,
        compiler_params=LEAN,
    )(*near(*args))


def load(vectors, reflectors, tfactors, plan, columns):
    held, lanes = reflectors.shape[0], reflectors.shape[2]
    last = tfactors.shape[1] - 1
    groups = plan.shape[0]

    def body(plan, x, v, f, kinds_ref, x_out, v_out, f_out, end_out, plan_ref, sem):
        copies = [(plan, plan_ref), (f.at[:, last], end_out), (x, x_out), (v, v_out), (f, f_out)]
        copies = [pltpu.make_async_copy(*pair, sem.at[at]) for at, pair in enumerate(copies)]
        for copy in copies:
            copy.start()
        me = lax.axis_index("col")
        kinds_ref[...] = jnp.zeros_like(kinds_ref)
        copies[0].wait()
        for step in range(groups):
            group = plan_ref[step]
            piece = (me + columns - group // held) % columns * held + group % held
            kinds_ref[step : step + 1, :] = jnp.full((1, lanes), piece, jnp.int32)
        for copy in copies[1:]:
            copy.wait()

    return pl.pallas_call(
        body,
        out_shape=[
            shape(-(-groups // 8) * 8, lanes, dtype=jnp.int32),
            shape(*vectors.shape),
            shape(*reflectors.shape),
            shape(*tfactors.shape),
            shape(held, lanes, lanes),
        ],
        in_specs=[HBM] * 4,
        out_specs=[VMEM] * 5,
        scratch_shapes=[pltpu.SMEM((groups,), jnp.int32), pltpu.SemaphoreType.DMA((5,))],
        name="load",
        compiler_params=LEAN,
    )(*near(plan, vectors, reflectors, tfactors, space=pltpu.HBM))


def is_top(odd_round):
    return (lax.axis_index("row") % 2 == 1) != odd_round


def ordered(top, low):
    first = is_top(False)
    return jnp.where(first, top, low), jnp.where(first, low, top)


def edges(x, refls, factors, kinds, step):
    height, width = x.shape
    strip = refls[0].shape[1]
    count = height // (2 * strip)
    n = len(refls)

    def body(*refs):
        kinds_ref, x_ref, refs = refs[0], refs[1], refs[2:]
        refl_refs, factor_refs = refs[:n], refs[n : 2 * n]
        blocks, even_ref, odd_ref = refs[2 * n : 2 * n + 2], refs[2 * n + 2], refs[2 * n + 3]
        projs = []
        for at, outer, block_ref in zip((0, count - 1), (0, strip), blocks):
            rows = slice(at * 2 * strip, (at + 1) * 2 * strip)
            side = slice(rows.start + outer, rows.start + outer + strip)
            first = pick(kinds_ref, step, [r[rows, :] for r in refl_refs])
            factor = pick(kinds_ref, step, [r[at] for r in factor_refs])
            second = pick(kinds_ref, step + 1, [r[side, :] for r in refl_refs])
            new = reflect(x_ref[rows, :], first, factor)
            block_ref[...] = new
            projs.append(product(split(second), split(new[outer : outer + strip]), over=0))
        even_ref[...], odd_ref[...] = ordered(*projs)

    block, proj = shape(2 * strip, width), shape(strip, width)
    return vmem_call(body, [block, block, proj, proj], "edges", kinds, x, *refls, *factors)


def middle(x, refls, factors, kinds, step, top_block, low_block):
    height, width = x.shape
    strip = refls[0].shape[1]
    count = height // (2 * strip)
    n = len(refls)

    def body(*refs):
        kinds_ref, x_ref, top_ref, low_ref, refs = refs[0], refs[1], refs[2], refs[3], refs[4:]
        refl_refs, factor_refs = refs[:n], refs[n : 2 * n]
        out_ref, mark_ref, work_ref, sem = refs[2 * n :]
        mark_ref[...] = jnp.zeros_like(mark_ref)
        for at in range(1, count - 1):
            rows = pl.ds(at * 2 * strip, 2 * strip)
            refl = pick(kinds_ref, step, [r[rows, :] for r in refl_refs])
            factor = pick(kinds_ref, step, [r[at] for r in factor_refs])
            work_ref[rows, :] = reflect(x_ref[rows, :], refl, factor)
        work_ref[pl.ds(strip, strip), :] = top_ref[strip:, :]
        work_ref[pl.ds(height - 2 * strip, strip), :] = low_ref[:strip, :]
        copies = []
        for at in range(count - 1):
            rows = pl.ds(at * 2 * strip + strip, 2 * strip)
            refl = pick(kinds_ref, step + 1, [r[rows, :] for r in refl_refs])
            factor = pick(kinds_ref, step + 1, [r[at] for r in factor_refs])
            work_ref[rows, :] = reflect(work_ref[rows, :], refl, factor)
            copy = pltpu.make_async_copy(work_ref.at[rows, :], out_ref.at[rows, :], sem.at[at])
            copy.start()
            copies.append(copy)
        for copy in copies:
            copy.wait()

    args = near(kinds, x, top_block, low_block, *refls, *factors)
    return pl.pallas_call(
        body,
        out_shape=[jax.ShapeDtypeStruct((height, width), F32), shape(8, strip)],
        in_specs=[VMEM] * len(args),
        out_specs=[ANY, VMEM],
        scratch_shapes=[pltpu.VMEM((height, width), F32), pltpu.SemaphoreType.DMA((count - 1,))],
        name="middle",
        compiler_params=LEAN,
    )(*args)


def prepare(refls, factors, behind, kinds, step, blocks, projs, mark):
    height, strip = refls[0].shape
    width = blocks[0].shape[1]
    count = height // (2 * strip)
    n = len(refls)

    def body(_, kinds_ref, top_ref, low_ref, even_ref, odd_ref, *refs):
        refl_refs, factor_refs, behind_refs = refs[:n], refs[n : 2 * n], refs[2 * n : 3 * n]
        rests, highs, lows = refs[3 * n : 3 * n + 2], refs[3 * n + 2 : 3 * n + 4], refs[3 * n + 4 :]
        row, last = lax.axis_index("row"), lax.axis_size("row") - 1
        ends = [r[count - 1] for r in factor_refs], [r[...] for r in behind_refs]
        own = ordered(even_ref[...], odd_ref[...])

        def work(start, ends, present, strip_rows, proj):
            refl = pick(kinds_ref, step + 1, [r[start : start + strip, :] for r in refl_refs])
            weight = product(split(refl), split(pick(kinds_ref, step + 1, ends)))
            weight = jnp.where(present, weight, jnp.zeros_like(weight))
            parts = split(weight)
            return strip_rows - product(parts, split(proj)), *parts

        top = work(0, ends[1], row > 0, top_ref[:strip, :], own[0])
        low = work(height - strip, ends[0], row < last, low_ref[strip:, :], own[1])
        rests[0][...], rests[1][...] = ordered(top[0], low[0])
        for at, halves in ((1, highs), (2, lows)):
            even, odd = ordered(top[at].astype(F32), low[at].astype(F32))
            halves[0][...], halves[1][...] = even.astype(BF16), odd.astype(BF16)

    rest, half = shape(strip, width), shape(strip, strip, dtype=BF16)
    outs = vmem_call(
        body,
        [rest, rest, half, half, half, half],
        "prepare",
        *(mark, kinds, *blocks, *projs, *refls, *factors, *behind),
    )
    return outs[::2], outs[1::2]


def finish(out, odd_round, rest, high, low, got):
    height, width = out.shape
    strip = rest.shape[0]

    def body(rest_ref, high_ref, low_ref, got_ref, _, out_ref, new_ref, sem):
        row, last = lax.axis_index("row"), lax.axis_size("row") - 1
        top = is_top(odd_round)
        present = jnp.where(top, row > 0, row < last)
        other = jnp.where(present, got_ref[...], jnp.zeros_like(got_ref))
        new_ref[...] = rest_ref[...] - product((high_ref[...], low_ref[...]), split(other))
        start = pl.multiple_of(jnp.where(top, 0, height - strip), strip)
        copy = pltpu.make_async_copy(new_ref, out_ref.at[pl.ds(start, strip), :], sem)
        copy.start()
        copy.wait()

    return pl.pallas_call(
        body,
        out_shape=jax.ShapeDtypeStruct((height, width), F32),
        in_specs=[VMEM] * 4 + [ANY],
        out_specs=ANY,
        scratch_shapes=[pltpu.VMEM((strip, width), F32), pltpu.SemaphoreType.DMA],
        input_output_aliases={4: 0},
        name="finish",
        compiler_params=LEAN,
    )(*near(rest, high, low, got), out)


def local(vectors, reflectors, tfactors, plan):
    groups = plan.shape[0]
    held = reflectors.shape[0]
    rows, columns = lax.axis_size("row"), lax.axis_size("col")

    def around(block, shift):
        return lax.ppermute(block, "col", [(c, (c + shift) % columns) for c in range(columns)])

    def trade(block, odd_round):
        route = []
        for row in range(rows):
            for col in range(columns):
                there = row + 1 if (row % 2 == 1) == odd_round else row - 1
                there = (there, col) if 0 <= there < rows else (row, (col + 1) % columns)
                route.append((row * columns + col, there[0] * columns + there[1]))
        return lax.ppermute(block, ("row", "col"), route)

    def others(piece):
        return [around(piece, shift) for shift in range(1, columns)]

    def apart(pieces):
        return [piece[slot] for piece in pieces for slot in range(held)]

    far_refls, far_factors = others(reflectors), others(tfactors)
    kinds, current, refl, factor, end = load(vectors, reflectors, tfactors, plan, columns)
    behind = lax.ppermute(end, "row", [(r, (r + 1) % rows) for r in range(rows)])
    refls, factors = apart([refl, *far_refls]), apart([factor, *far_factors])
    behinds = apart([behind, *others(behind)])
    for step in range(0, groups, 2):
        top, low, even_proj, odd_proj = edges(current, refls, factors, kinds, step)
        even_got, odd_got = trade(even_proj, False), trade(odd_proj, True)
        done, mark = middle(current, refls, factors, kinds, step, top, low)
        even, odd = prepare(
            refls, factors, behinds, kinds, step, (top, low), (even_proj, odd_proj), mark
        )
        done = finish(done, False, *even, even_got)
        current = finish(done, True, *odd, odd_got)
    return current


def solution(mesh):
    return jax.shard_map(
        local,
        mesh=mesh,
        in_specs=(P("row", "col"), P("col", "row", None), P("col", "row", None, None), P()),
        out_specs=P("row", "col"),
        check_vma=False,
    )
```

time: 19.3 us -> 17 us (0.88)
  the two profiles are of different devices: /device:TPU:19 before, /device:TPU:0 now
where the time goes in v3:
time: 17 us; the launch traced here: 16.8 us
  Pallas kernels  8.7 us (51%)
  starting transfers between devices  5.09 us (30%)
  waiting for transfers between devices  2.93 us (17%)
    pallas_call x1, Pallas kernels, middle(): pl.pallas_call(body, out_shape=[jax.ShapeDtypeStruct((height, width), F32...  3.12 us
    ppermute x1, starting transfers between devices, local(): lax.ppermute(end, 'row', [(r, (r + 1) % rows) for r in range(rows)])  3.02 us
    ppermute x1, waiting for transfers between devices, local(): lax.ppermute(end, 'row', [(r, (r + 1) % rows) for r in range(rows)])  2.92 us
    pallas_call x2, Pallas kernels, vmem_call(): pl.pallas_call(body, out_shape=outs, in_specs=[VMEM] * len(args), out_spe...  2.3 us
    pallas_call x2, Pallas kernels, finish(): pl.pallas_call(body, out_shape=jax.ShapeDtypeStruct((height, width), F32)...  1.78 us
    ppermute x2, starting transfers between devices, trade(): return lax.ppermute(block, ('row', 'col'), route)  1.56 us
    pallas_call x1, Pallas kernels, load(): pl.pallas_call(body, out_shape=[shape(-(-groups // 8) * 8, lanes, dtype=j...  1.51 us
    ppermute x3, starting transfers between devices, around(): lax.ppermute(block, 'col', [(c, (c + shift) % columns) for c in range(col...  0.51 us
  transfers between devices with their start and end apart: 6, of which 1 were waited for; matrix products, arithmetic and copies ran while one was open for 0% of the time, Pallas kernels for 46%

profile of v3, /device:TPU:0, one launch (start us, length us, event | category | flops | bytes accessed | tf_op | source)
XLA Modules:
  0.0 16.8 jit_solution(15193267215010668225)
XLA Ops:
  0.0 0.5 %collective-permute-start = (f32[1,1024,128]{2,1,0:T(8,128)}, f32[1,1024,128]{2,1,0:T(8,128)S(1)}, u32[]{:S(2)}, u32[]{:S(2)}) collective-permute-start(f32[1,1024,128]{2,1,0:T(8,128)} %v.1), channel_id=1, source_target_pairs={{0,1},{1,0},{2,3},{3,2},{4,5},{5,4},{6,7},{7,6},{8,9},{9,8},{10,11... | collective-permute-start | bytes 1572872 | tf_op jit(solution)/shard_map/ppermute | solution.py:247
  0.5 0.0 collective-permute-start.1
  0.5 1.5 %load.1 = (s32[8,128]{1,0:T(8,128)S(1)}, f32[1024,256]{1,0:T(8,128)S(1)}, f32[1,1024,128]{2,1,0:T(8,128)S(1)}, f32[1,4,128,128]{3,2,1,0:T(8,128)S(1)}, f32[1,128,128]{2,1,0:T(8,128)S(1)}) custom-call(s32[2]{0:T(128)} %plan.1, f32[1024,256]{1,0:T(8,128)} %x.1, f32[1,1024,128]{2,1,0:T(8,128)} %v.1, f32[1,4,128,128]{3,2,1,0:T(8,128)} %f.1), custom_call_target="tpu_custom_call" | custom-call | tf_op jit(solution)/shard_map/load/pallas_call | solution.py:83
  2.0 3.0 %collective-permute-start.2 = (f32[1,128,128]{2,1,0:T(8,128)S(1)}, f32[1,128,128]{2,1,0:T(8,128)S(1)}, u32[]{:S(2)}, u32[]{:S(2)}) collective-permute-start(f32[1,128,128]{2,1,0:T(8,128)S(1)} %get-tuple-element.31), channel_id=1, source_target_pairs={{0,2},{2,4},{4,6},{6,8},{8,10},{10,12},{12,14},{14,16},{16,18},{18... | collective-permute-start | bytes 196616 | tf_op jit(solution)/shard_map/ppermute | solution.py:266
  5.0 0.0 collective-permute-done.1
  5.0 0.0 collective-permute-done
  5.1 1.9 %edges.1 = (f32[256,256]{1,0:T(8,128)S(1)}, f32[256,256]{1,0:T(8,128)S(1)}, f32[128,256]{1,0:T(8,128)S(1)}, f32[128,256]{1,0:T(8,128)S(1)}) custom-call(s32[8,128]{1,0:T(8,128)S(1)} %get-tuple-element.22.refs_0_.kinds_ref, f32[1024,256]{1,0:T(8,128)S(1)} %get-tuple-element.23.refs_1_, f32[1024,128]{1,0:T(8,128)S(1)} %bitcast.9, f32[1024,128]{1,0:T(8,128)S(1)} %bitcast.6, ...), custom_call_target="tpu_custom_call" | custom-call | tf_op jit(solution)/shard_map/edges/pallas_call | solution.py:53
  6.9 1.6 %collective-permute-start.5 = (f32[128,256]{1,0:T(8,128)S(1)}, f32[128,256]{1,0:T(8,128)S(1)}, u32[]{:S(2)}, u32[]{:S(2)}) collective-permute-start(f32[128,256]{1,0:T(8,128)S(1)} %get-tuple-element.29.even_ref), channel_id=1, source_target_pairs={{0,2},{1,3},{2,0},{3,1},{4,6},{5,7},{6,4},{7,5},{8,10},{9,11},{10,... | collective-permute-start | bytes 393224 | tf_op jit(solution)/shard_map/ppermute | solution.py:256
  8.5 0.0 collective-permute-start.4
  8.5 2.9 %collective-permute-done.2 = f32[1,128,128]{2,1,0:T(8,128)S(1)} collective-permute-done((f32[1,128,128]{2,1,0:T(8,128)S(1)}, f32[1,128,128]{2,1,0:T(8,128)S(1)}, u32[]{:S(2)}, u32[]{:S(2)}) %collective-permute-start.2) | collective-permute-done | bytes 65568 | tf_op jit(solution)/shard_map/ppermute | solution.py:266
  11.4 0.0 collective-permute-start.3
  11.4 3.1 %middle.1 = (f32[1024,256]{1,0:T(8,128)}, f32[8,128]{1,0:T(8,128)S(1)}) custom-call(s32[8,128]{1,0:T(8,128)S(1)} %get-tuple-element.22.refs_0_.kinds_ref, f32[1024,256]{1,0:T(8,128)S(1)} %get-tuple-element.23.refs_1_, f32[256,256]{1,0:T(8,128)S(1)} %get-tuple-element.26.refs_2_.top_ref, f32[256,256]{1,0:T(8,128)S(1)} %get-tuple-element.27.refs_3_.low_ref, ...), custom_call_target="tpu_custom_call" | custom-call | tf_op jit(solution)/shard_map/middle/pallas_call | solution.py:166
  14.5 0.0 collective-permute-done.3
  14.5 0.4 %prepare.1 = (f32[128,256]{1,0:T(8,128)S(1)}, f32[128,256]{1,0:T(8,128)S(1)}, bf16[128,128]{1,0:T(8,128)(2,1)S(1)}, bf16[128,128]{1,0:T(8,128)(2,1)S(1)}, bf16[1...) custom-call(f32[8,128]{1,0:T(8,128)S(1)} %get-tuple-element.28._, s32[8,128]{1,0:T(8,128)S(1)} %get-tuple-element.22.refs_0_.kinds_ref, ...), custom_call_target="tpu_custom_call" | custom-call | tf_op jit(solution)/shard_map/prepare/pallas_call | solution.py:53
  15.0 0.0 collective-permute-done.5.got_ref
  15.0 0.9 %finish.2._ = f32[1024,256]{1,0:T(8,128)} custom-call(f32[128,256]{1,0:T(8,128)S(1)} %get-tuple-element.35.rest_ref, bf16[128,128]{1,0:T(8,128)(2,1)S(1)} %get-tuple-element.36.high_ref, bf16[128,128]{1,0:T(8,128)(2,1)S(1)} %get-tuple-element.37.low_ref, f32[128,256]{1,0:T(8,128)S(1)} %collective-permute-done.5.got_ref, ...), custom_call_target="tpu_custom_call", output_to_operand_aliasing={{}: (4, {})} | custom-call | tf_op jit(solution)/shard_map/finish/pallas_call | solution.py:229
  15.9 0.0 collective-permute-done.4.got_ref
  15.9 0.9 %finish.3 = f32[1024,256]{1,0:T(8,128)} custom-call(f32[128,256]{1,0:T(8,128)S(1)} %get-tuple-element.32.rest_ref, bf16[128,128]{1,0:T(8,128)(2,1)S(1)} %get-tuple-element.33.high_ref, bf16[128,128]{1,0:T(8,128)(2,1)S(1)} %get-tuple-element.34.low_ref, f32[128,256]{1,0:T(8,128)S(1)} %collective-permute-done.4.got_ref, ...), custom_call_target="tpu_custom_call", output_to_operand_aliasing={{}: (4, {})} | custom-call | tf_op jit(solution)/shard_map/finish/pallas_call | solution.py:229
Async XLA Ops:
  0.0 5.0 %collective-permute-start = (f32[1,1024,128]{2,1,0:T(8,128)}, f32[1,1024,128]{2,1,0:T(8,128)S(1)}, u32[]{:S(2)}, u32[]{:S(2)}) collective-permute-start(f32[1,1024,128]{2,1,0:T(8,128)} %v.1), channel_id=1, source_target_pairs={{0,1},{1,0},{2,3},{3,2},{4,5},{5,4},{6,7},{7,6},{8,9},{9,8},{10,11... | collective-permute-start | bytes 1572872 | tf_op jit(solution)/shard_map/ppermute | solution.py:247
  0.5 4.6 %collective-permute-start.1 = (f32[1,4,128,128]{3,2,1,0:T(8,128)}, f32[1,4,128,128]{3,2,1,0:T(8,128)S(1)}, u32[]{:S(2)}, u32[]{:S(2)}) collective-permute-start(f32[1,4,128,128]{3,2,1,0:T(8,128)} %f.1), channel_id=1, source_target_pairs={{0,1},{1,0},{2,3},{3,2},{4,5},{5,4},{6,7},{7,6},{8,9},{9,8},{10,11... | collective-permute-start | bytes 786440 | tf_op jit(solution)/shard_map/ppermute | solution.py:247
  2.0 9.4 %collective-permute-start.2 = (f32[1,128,128]{2,1,0:T(8,128)S(1)}, f32[1,128,128]{2,1,0:T(8,128)S(1)}, u32[]{:S(2)}, u32[]{:S(2)}) collective-permute-start(f32[1,128,128]{2,1,0:T(8,128)S(1)} %get-tuple-element.31), channel_id=1, source_target_pairs={{0,2},{2,4},{4,6},{6,8},{8,10},{10,12},{12,14},{14,16},{16,18},{18... | collective-permute-start | bytes 196616 | tf_op jit(solution)/shard_map/ppermute | solution.py:266
  6.9 8.1 %collective-permute-start.5 = (f32[128,256]{1,0:T(8,128)S(1)}, f32[128,256]{1,0:T(8,128)S(1)}, u32[]{:S(2)}, u32[]{:S(2)}) collective-permute-start(f32[128,256]{1,0:T(8,128)S(1)} %get-tuple-element.29.even_ref), channel_id=1, source_target_pairs={{0,2},{1,3},{2,0},{3,1},{4,6},{5,7},{6,4},{7,5},{8,10},{9,11},{10,... | collective-permute-start | bytes 393224 | tf_op jit(solution)/shard_map/ppermute | solution.py:256
  8.5 7.4 %collective-permute-start.4 = (f32[128,256]{1,0:T(8,128)S(1)}, f32[128,256]{1,0:T(8,128)S(1)}, u32[]{:S(2)}, u32[]{:S(2)}) collective-permute-start(f32[128,256]{1,0:T(8,128)S(1)} %get-tuple-element.30.odd_ref), channel_id=1, source_target_pairs={{0,1},{1,0},{2,4},{3,5},{4,2},{5,3},{6,8},{7,9},{8,6},{9,7},{10,12... | collective-permute-start | bytes 393224 | tf_op jit(solution)/shard_map/ppermute | solution.py:256
  11.4 3.1 %collective-permute-start.3 = (f32[1,128,128]{2,1,0:T(8,128)S(1)}, f32[1,128,128]{2,1,0:T(8,128)S(1)}, u32[]{:S(2)}, u32[]{:S(2)}) collective-permute-start(f32[1,128,128]{2,1,0:T(8,128)S(1)} %collective-permute-done.2), channel_id=1, source_target_pairs={{0,1},{1,0},{2,3},{3,2},{4,5},{5,4},{6,7},{7,6},{8,9},{9,8},{10,11... | collective-permute-start | bytes 196616 | tf_op jit(solution)/shard_map/ppermute | solution.py:247

commit v4 on v3

--- a/solution.py
+++ b/solution.py
@@ -7,6 +7,7 @@
 
 F32 = jnp.float32
 BF16 = jnp.bfloat16
+LANES = 128
 VMEM = pl.BlockSpec(memory_space=pltpu.VMEM)
 HBM = pl.BlockSpec(memory_space=pltpu.HBM)
 ANY = pl.BlockSpec(memory_space=pl.ANY)
@@ -24,7 +25,11 @@
 
 def product(a, b, over=1):
     (ah, al), (bh, bl) = a, b
-    return dot(ah, bh, over) + (dot(ah, bl, over) + dot(al, bh, over))
+    if ah.shape[over] > LANES:
+        both = dot(jnp.concatenate([ah, al], 1 - over), bh, over)
+        rows = ah.shape[1 - over]
+        return both[:rows] + (both[rows:] + dot(ah, bl, over))
+    return dot(jnp.concatenate([ah, al], over), jnp.concatenate([bh, bh], 0), over) + dot(ah, bl, over)
 
 
 def reflect(x, refl, factor):
@@ -115,41 +120,62 @@
     def body(*refs):
         kinds_ref, x_ref, refs = refs[0], refs[1], refs[2:]
         refl_refs, factor_refs = refs[:n], refs[n : 2 * n]
-        blocks, even_ref, odd_ref = refs[2 * n : 2 * n + 2], refs[2 * n + 2], refs[2 * n + 3]
-        projs = []
-        for at, outer, block_ref in zip((0, count - 1), (0, strip), blocks):
+        coeffs, even_ref, odd_ref = refs[2 * n : 2 * n + 2], refs[2 * n + 2], refs[2 * n + 3]
+        firsts, seconds, crosses, weights, projs = [], [], [], [], []
+        places = [(0, 0), (count - 1, strip)]
+        for at, outer in places:
+            start = at * 2 * strip
+            rows = slice(start, start + 2 * strip)
+            side = slice(start + outer, start + outer + strip)
+            firsts.append(split(pick(kinds_ref, step, [r[rows, :] for r in refl_refs])))
+            seconds.append(split(pick(kinds_ref, step + 1, [r[side, :] for r in refl_refs])))
+        for (at, outer), first, second in zip(places, firsts, seconds):
+            crosses.append(product(second, [v[outer : outer + strip] for v in first], over=0))
+        for (at, outer), first, second, coeff_ref in zip(places, firsts, seconds, coeffs):
             rows = slice(at * 2 * strip, (at + 1) * 2 * strip)
-            side = slice(rows.start + outer, rows.start + outer + strip)
-            first = pick(kinds_ref, step, [r[rows, :] for r in refl_refs])
+            blank = jnp.zeros((strip, strip), BF16)
+            second = [jnp.concatenate([v, blank] if outer == 0 else [blank, v], 0) for v in second]
+            high, low = split(x_ref[rows, :])
+            all_high = dot(jnp.concatenate([*first, *second], 1), high, 0)
+            all_low = dot(jnp.concatenate([first[0], second[0]], 1), low, 0)
+            parts = [all_high[i * strip : (i + 1) * strip] for i in range(4)]
+            coeff_ref[...] = parts[0] + (parts[1] + all_low[:strip])
+            projs.append(parts[2] + (parts[3] + all_low[strip:]))
+        for (at, outer), cross in zip(places, crosses):
             factor = pick(kinds_ref, step, [r[at] for r in factor_refs])
-            second = pick(kinds_ref, step + 1, [r[side, :] for r in refl_refs])
-            new = reflect(x_ref[rows, :], first, factor)
-            block_ref[...] = new
-            projs.append(product(split(second), split(new[outer : outer + strip]), over=0))
+            weights.append(product(split(cross), split(factor)))
+        for at, (weight, coeff_ref) in enumerate(zip(weights, coeffs)):
+            projs[at] = projs[at] - product(split(weight), split(coeff_ref[...]))
         even_ref[...], odd_ref[...] = ordered(*projs)
 
-    block, proj = shape(2 * strip, width), shape(strip, width)
-    return vmem_call(body, [block, block, proj, proj], "edges", kinds, x, *refls, *factors)
-
-
-def middle(x, refls, factors, kinds, step, top_block, low_block):
+    return vmem_call(body, [shape(strip, width)] * 4, "edges", kinds, x, *refls, *factors)
+
+
+def middle(x, refls, factors, kinds, step, coeffs):
     height, width = x.shape
     strip = refls[0].shape[1]
     count = height // (2 * strip)
     n = len(refls)
 
     def body(*refs):
-        kinds_ref, x_ref, top_ref, low_ref, refs = refs[0], refs[1], refs[2], refs[3], refs[4:]
+        kinds_ref, x_ref, coeff_refs, refs = refs[0], refs[1], refs[2:4], refs[4:]
         refl_refs, factor_refs = refs[:n], refs[n : 2 * n]
-        out_ref, mark_ref, work_ref, sem = refs[2 * n :]
-        mark_ref[...] = jnp.zeros_like(mark_ref)
-        for at in range(1, count - 1):
-            rows = pl.ds(at * 2 * strip, 2 * strip)
-            refl = pick(kinds_ref, step, [r[rows, :] for r in refl_refs])
-            factor = pick(kinds_ref, step, [r[at] for r in factor_refs])
-            work_ref[rows, :] = reflect(x_ref[rows, :], refl, factor)
-        work_ref[pl.ds(strip, strip), :] = top_ref[strip:, :]
-        work_ref[pl.ds(height - 2 * strip, strip), :] = low_ref[:strip, :]
+        out_ref, top_ref, low_ref, work_ref, sem = refs[2 * n :]
+        for at in range(count):
+            rows = slice(at * 2 * strip, (at + 1) * 2 * strip)
+            refl = split(pick(kinds_ref, step, [r[rows, :] for r in refl_refs]))
+            factor = split(pick(kinds_ref, step, [r[at] for r in factor_refs]))
+            block = x_ref[rows, :]
+            if at in (0, count - 1):
+                coeff = coeff_refs[at // (count - 1)][...]
+            else:
+                coeff = product(refl, split(block), over=0)
+            new = block - product(refl, split(product(factor, split(coeff))))
+            work_ref[rows, :] = new
+            if at == 0:
+                top_ref[...] = new[:strip]
+            if at == count - 1:
+                low_ref[...] = new[strip:]
         copies = []
         for at in range(count - 1):
             rows = pl.ds(at * 2 * strip + strip, 2 * strip)
@@ -162,25 +188,25 @@
         for copy in copies:
             copy.wait()
 
-    args = near(kinds, x, top_block, low_block, *refls, *factors)
+    args = near(kinds, x, *coeffs, *refls, *factors)
     return pl.pallas_call(
         body,
-        out_shape=[jax.ShapeDtypeStruct((height, width), F32), shape(8, strip)],
+        out_shape=[jax.ShapeDtypeStruct((height, width), F32)] + [shape(strip, width)] * 2,
         in_specs=[VMEM] * len(args),
-        out_specs=[ANY, VMEM],
+        out_specs=[ANY, VMEM, VMEM],
         scratch_shapes=[pltpu.VMEM((height, width), F32), pltpu.SemaphoreType.DMA((count - 1,))],
         name="middle",
         compiler_params=LEAN,
     )(*args)
 
 
-def prepare(refls, factors, behind, kinds, step, blocks, projs, mark):
+def prepare(refls, factors, behind, kinds, step, strips, projs):
     height, strip = refls[0].shape
-    width = blocks[0].shape[1]
+    width = strips[0].shape[1]
     count = height // (2 * strip)
     n = len(refls)
 
-    def body(_, kinds_ref, top_ref, low_ref, even_ref, odd_ref, *refs):
+    def body(kinds_ref, top_ref, low_ref, even_ref, odd_ref, *refs):
         refl_refs, factor_refs, behind_refs = refs[:n], refs[n : 2 * n], refs[2 * n : 3 * n]
         rests, highs, lows = refs[3 * n : 3 * n + 2], refs[3 * n + 2 : 3 * n + 4], refs[3 * n + 4 :]
         row, last = lax.axis_index("row"), lax.axis_size("row") - 1
@@ -194,8 +220,8 @@
             parts = split(weight)
             return strip_rows - product(parts, split(proj)), *parts
 
-        top = work(0, ends[1], row > 0, top_ref[:strip, :], own[0])
-        low = work(height - strip, ends[0], row < last, low_ref[strip:, :], own[1])
+        top = work(0, ends[1], row > 0, top_ref[...], own[0])
+        low = work(height - strip, ends[0], row < last, low_ref[...], own[1])
         rests[0][...], rests[1][...] = ordered(top[0], low[0])
         for at, halves in ((1, highs), (2, lows)):
             even, odd = ordered(top[at].astype(F32), low[at].astype(F32))
@@ -206,7 +232,7 @@
         body,
         [rest, rest, half, half, half, half],
         "prepare",
-        *(mark, kinds, *blocks, *projs, *refls, *factors, *behind),
+        *(kinds, *strips, *projs, *refls, *factors, *behind),
     )
     return outs[::2], outs[1::2]
 
@@ -265,13 +291,16 @@
     kinds, current, refl, factor, end = load(vectors, reflectors, tfactors, plan, columns)
     behind = lax.ppermute(end, "row", [(r, (r + 1) % rows) for r in range(rows)])
     refls, factors = apart([refl, *far_refls]), apart([factor, *far_factors])
-    behinds = apart([behind, *others(behind)])
+    behinds = None
     for step in range(0, groups, 2):
-        top, low, even_proj, odd_proj = edges(current, refls, factors, kinds, step)
+        *coeffs, even_proj, odd_proj = edges(current, refls, factors, kinds, step)
         even_got, odd_got = trade(even_proj, False), trade(odd_proj, True)
-        done, mark = middle(current, refls, factors, kinds, step, top, low)
+        done, *strips = middle(current, refls, factors, kinds, step, coeffs)
+        if behinds is None:
+            behind, strips[0] = lax.optimization_barrier((behind, strips[0]))
+            behinds = apart([behind, *others(behind)])
         even, odd = prepare(
-            refls, factors, behinds, kinds, step, (top, low), (even_proj, odd_proj), mark
+            refls, factors, behinds, kinds, step, strips, (even_proj, odd_proj)
         )
         done = finish(done, False, *even, even_got)
         current = finish(done, True, *odd, odd_got)

time: 17 us -> 15.1 us (0.89)
  Pallas kernels: 8.7 us -> 7.71 us
  waiting for transfers between devices: 2.93 us -> 2.09 us
    ppermute x1, waiting for transfers between devices: 2.92 us -> 0.83 us  [local(): lax.ppermute(end, 'row', [(r, (r + 1) % rows) for r in range(rows)])]
    ppermute x3, waiting for transfers between devices: 0.01 us -> 1.26 us  [around(): lax.ppermute(block, 'col', [(c, (c + shift) % columns) for c in range(col...]
    pallas_call x2, Pallas kernels: 2.3 us -> 1.23 us  [vmem_call(): pl.pallas_call(body, out_shape=outs, in_specs=[VMEM] * len(args), out_spe...]
  transfers between devices with their start and end apart: 6 -> 6, of which waited for: 1 -> 2; matrix products, arithmetic and copies ran while one was open for 0% -> 0% of each run, Pallas kernels for 46% -> 46%
where the time goes in v4:
time: 15.1 us; the launch traced here: 15 us
  Pallas kernels  7.71 us (51%)
  starting transfers between devices  5.09 us (34%)
  waiting for transfers between devices  2.09 us (14%)
    pallas_call x1, Pallas kernels, middle(): pl.pallas_call(body, out_shape=[jax.ShapeDtypeStruct((height, width), F32...  3.24 us
    ppermute x1, starting transfers between devices, local(): lax.ppermute(end, 'row', [(r, (r + 1) % rows) for r in range(rows)])  3.02 us
    pallas_call x2, Pallas kernels, finish(): pl.pallas_call(body, out_shape=jax.ShapeDtypeStruct((height, width), F32)...  1.74 us
    ppermute x2, starting transfers between devices, trade(): return lax.ppermute(block, ('row', 'col'), route)  1.56 us
    pallas_call x1, Pallas kernels, load(): pl.pallas_call(body, out_shape=[shape(-(-groups // 8) * 8, lanes, dtype=j...  1.51 us
    ppermute x3, waiting for transfers between devices, around(): lax.ppermute(block, 'col', [(c, (c + shift) % columns) for c in range(col...  1.26 us
    pallas_call x2, Pallas kernels, vmem_call(): pl.pallas_call(body, out_shape=outs, in_specs=[VMEM] * len(args), out_spe...  1.23 us
    ppermute x1, waiting for transfers between devices, local(): lax.ppermute(end, 'row', [(r, (r + 1) % rows) for r in range(rows)])  0.83 us
  transfers between devices with their start and end apart: 6, of which 2 were waited for; matrix products, arithmetic and copies ran while one was open for 0% of the time, Pallas kernels for 46%

profile of v4, /device:TPU:0, one launch (start us, length us, event | category | flops | bytes accessed | tf_op | source)
XLA Modules:
  0.0 15.0 jit_solution(5754248083355405742)
XLA Ops:
  0.0 0.5 %collective-permute-start.1 = (f32[1,1024,128]{2,1,0:T(8,128)}, f32[1,1024,128]{2,1,0:T(8,128)S(1)}, u32[]{:S(2)}, u32[]{:S(2)}) collective-permute-start(f32[1,1024,128]{2,1,0:T(8,128)} %v.1), channel_id=1, source_target_pairs={{0,1},{1,0},{2,3},{3,2},{4,5},{5,4},{6,7},{7,6},{8,9},{9,8},{10,11... | collective-permute-start | bytes 1572872 | tf_op jit(solution)/shard_map/ppermute | solution.py:273
  0.5 0.0 collective-permute-start.2
  0.5 1.5 %load.1 = (s32[8,128]{1,0:T(8,128)S(1)}, f32[1024,256]{1,0:T(8,128)S(1)}, f32[1,1024,128]{2,1,0:T(8,128)S(1)}, f32[1,4,128,128]{3,2,1,0:T(8,128)S(1)}, f32[1,128,128]{2,1,0:T(8,128)S(1)}) custom-call(s32[2]{0:T(128)} %plan.1, f32[1024,256]{1,0:T(8,128)} %x.1, f32[1,1024,128]{2,1,0:T(8,128)} %v.1, f32[1,4,128,128]{3,2,1,0:T(8,128)} %f.1), custom_call_target="tpu_custom_call" | custom-call | tf_op jit(solution)/shard_map/load/pallas_call | solution.py:88
  2.0 3.0 %collective-permute-start = (f32[1,128,128]{2,1,0:T(8,128)S(1)}, f32[1,128,128]{2,1,0:T(8,128)S(1)}, u32[]{:S(2)}, u32[]{:S(2)}) collective-permute-start(f32[1,128,128]{2,1,0:T(8,128)S(1)} %get-tuple-element.26), channel_id=1, source_target_pairs={{0,2},{2,4},{4,6},{6,8},{8,10},{10,12},{12,14},{14,16},{16,18},{18... | collective-permute-start | bytes 196616 | tf_op jit(solution)/shard_map/ppermute | solution.py:292
  5.0 0.0 collective-permute-done.2
  5.0 0.0 collective-permute-done.1
  5.1 0.7 %edges.1 = (f32[128,256]{1,0:T(8,128)S(1)}, f32[128,256]{1,0:T(8,128)S(1)}, f32[128,256]{1,0:T(8,128)S(1)}, f32[128,256]{1,0:T(8,128)S(1)}) custom-call(s32[8,128]{1,0:T(8,128)S(1)} %get-tuple-element.25.refs_0_.kinds_ref, f32[1024,256]{1,0:T(8,128)S(1)} %get-tuple-element.27.refs_1_, f32[1024,128]{1,0:T(8,128)S(1)} %bitcast.9, f32[1024,128]{1,0:T(8,128)S(1)} %bitcast.6, ...), custom_call_target="tpu_custom_call" | custom-call | tf_op jit(solution)/shard_map/edges/pallas_call | solution.py:58
  5.8 1.6 %collective-permute-start.5 = (f32[128,256]{1,0:T(8,128)S(1)}, f32[128,256]{1,0:T(8,128)S(1)}, u32[]{:S(2)}, u32[]{:S(2)}) collective-permute-start(f32[128,256]{1,0:T(8,128)S(1)} %get-tuple-element.35.even_ref), channel_id=1, source_target_pairs={{0,2},{1,3},{2,0},{3,1},{4,6},{5,7},{6,4},{7,5},{8,10},{9,11},{10,... | collective-permute-start | bytes 393224 | tf_op jit(solution)/shard_map/ppermute | solution.py:282
  7.3 0.0 collective-permute-start.4
  7.3 3.2 %middle.1 = (f32[1024,256]{1,0:T(8,128)}, f32[128,256]{1,0:T(8,128)S(1)}, f32[128,256]{1,0:T(8,128)S(1)}) custom-call(s32[8,128]{1,0:T(8,128)S(1)} %get-tuple-element.25.refs_0_.kinds_ref, f32[1024,256]{1,0:T(8,128)S(1)} %get-tuple-element.27.refs_1_, f32[128,256]{1,0:T(8,128)S(1)} %get-tuple-element.30.refs_2_, f32[128,256]{1,0:T(8,128)S(1)} %get-tuple-element.31.refs_3_, ...), custom_call_target="tpu_custom_call" | custom-call | tf_op jit(solution)/shard_map/middle/pallas_call | solution.py:192
  10.6 0.8 %collective-permute-done = f32[1,128,128]{2,1,0:T(8,128)S(1)} collective-permute-done((f32[1,128,128]{2,1,0:T(8,128)S(1)}, f32[1,128,128]{2,1,0:T(8,128)S(1)}, u32[]{:S(2)}, u32[]{:S(2)}) %collective-permute-start) | collective-permute-done | bytes 65568 | tf_op jit(solution)/shard_map/ppermute | solution.py:292
  11.4 0.0 collective-permute-start.3
  11.4 1.3 %collective-permute-done.3 = f32[1,128,128]{2,1,0:T(8,128)S(1)} collective-permute-done((f32[1,128,128]{2,1,0:T(8,128)S(1)}, f32[1,128,128]{2,1,0:T(8,128)S(1)}, u32[]{:S(2)}, u32[]{:S(2)}) %collective-permute-start.3) | collective-permute-done | bytes 65568 | tf_op jit(solution)/shard_map/ppermute | solution.py:273
  12.7 0.5 %prepare.1 = (f32[128,256]{1,0:T(8,128)S(1)}, f32[128,256]{1,0:T(8,128)S(1)}, bf16[128,128]{1,0:T(8,128)(2,1)S(1)}, bf16[128,128]{1,0:T(8,128)(2,1)S(1)}, bf16[1...) custom-call(s32[8,128]{1,0:T(8,128)S(1)} %get-tuple-element.25.refs_0_.kinds_ref, ...), custom_call_target="tpu_custom_call" | custom-call | tf_op jit(solution)/shard_map/prepare/pallas_call | solution.py:58
  13.2 0.0 collective-permute-done.5.got_ref
  13.2 0.9 %finish.2._ = f32[1024,256]{1,0:T(8,128)} custom-call(f32[128,256]{1,0:T(8,128)S(1)} %get-tuple-element.41.rest_ref, bf16[128,128]{1,0:T(8,128)(2,1)S(1)} %get-tuple-element.42.high_ref, bf16[128,128]{1,0:T(8,128)(2,1)S(1)} %get-tuple-element.43.low_ref, f32[128,256]{1,0:T(8,128)S(1)} %collective-permute-done.5.got_ref, ...), custom_call_target="tpu_custom_call", output_to_operand_aliasing={{}: (4, {})} | custom-call | tf_op jit(solution)/shard_map/finish/pallas_call | solution.py:255
  14.1 0.0 collective-permute-done.4.got_ref
  14.1 0.9 %finish.3 = f32[1024,256]{1,0:T(8,128)} custom-call(f32[128,256]{1,0:T(8,128)S(1)} %get-tuple-element.38.rest_ref, bf16[128,128]{1,0:T(8,128)(2,1)S(1)} %get-tuple-element.39.high_ref, bf16[128,128]{1,0:T(8,128)(2,1)S(1)} %get-tuple-element.40.low_ref, f32[128,256]{1,0:T(8,128)S(1)} %collective-permute-done.4.got_ref, ...), custom_call_target="tpu_custom_call", output_to_operand_aliasing={{}: (4, {})} | custom-call | tf_op jit(solution)/shard_map/finish/pallas_call | solution.py:255
Async XLA Ops:
  0.0 5.0 %collective-permute-start.1 = (f32[1,1024,128]{2,1,0:T(8,128)}, f32[1,1024,128]{2,1,0:T(8,128)S(1)}, u32[]{:S(2)}, u32[]{:S(2)}) collective-permute-start(f32[1,1024,128]{2,1,0:T(8,128)} %v.1), channel_id=1, source_target_pairs={{0,1},{1,0},{2,3},{3,2},{4,5},{5,4},{6,7},{7,6},{8,9},{9,8},{10,11... | collective-permute-start | bytes 1572872 | tf_op jit(solution)/shard_map/ppermute | solution.py:273
  0.5 4.6 %collective-permute-start.2 = (f32[1,4,128,128]{3,2,1,0:T(8,128)}, f32[1,4,128,128]{3,2,1,0:T(8,128)S(1)}, u32[]{:S(2)}, u32[]{:S(2)}) collective-permute-start(f32[1,4,128,128]{3,2,1,0:T(8,128)} %f.1), channel_id=1, source_target_pairs={{0,1},{1,0},{2,3},{3,2},{4,5},{5,4},{6,7},{7,6},{8,9},{9,8},{10,11... | collective-permute-start | bytes 786440 | tf_op jit(solution)/shard_map/ppermute | solution.py:273
  2.0 9.4 %collective-permute-start = (f32[1,128,128]{2,1,0:T(8,128)S(1)}, f32[1,128,128]{2,1,0:T(8,128)S(1)}, u32[]{:S(2)}, u32[]{:S(2)}) collective-permute-start(f32[1,128,128]{2,1,0:T(8,128)S(1)} %get-tuple-element.26), channel_id=1, source_target_pairs={{0,2},{2,4},{4,6},{6,8},{8,10},{10,12},{12,14},{14,16},{16,18},{18... | collective-permute-start | bytes 196616 | tf_op jit(solution)/shard_map/ppermute | solution.py:292
  5.8 7.4 %collective-permute-start.5 = (f32[128,256]{1,0:T(8,128)S(1)}, f32[128,256]{1,0:T(8,128)S(1)}, u32[]{:S(2)}, u32[]{:S(2)}) collective-permute-start(f32[128,256]{1,0:T(8,128)S(1)} %get-tuple-element.35.even_ref), channel_id=1, source_target_pairs={{0,2},{1,3},{2,0},{3,1},{4,6},{5,7},{6,4},{7,5},{8,10},{9,11},{10,... | collective-permute-start | bytes 393224 | tf_op jit(solution)/shard_map/ppermute | solution.py:282
  7.3 6.8 %collective-permute-start.4 = (f32[128,256]{1,0:T(8,128)S(1)}, f32[128,256]{1,0:T(8,128)S(1)}, u32[]{:S(2)}, u32[]{:S(2)}) collective-permute-start(f32[128,256]{1,0:T(8,128)S(1)} %get-tuple-element.36.odd_ref), channel_id=1, source_target_pairs={{0,1},{1,0},{2,4},{3,5},{4,2},{5,3},{6,8},{7,9},{8,6},{9,7},{10,12... | collective-permute-start | bytes 393224 | tf_op jit(solution)/shard_map/ppermute | solution.py:282
  11.4 1.3 %collective-permute-start.3 = (f32[1,128,128]{2,1,0:T(8,128)S(1)}, f32[1,128,128]{2,1,0:T(8,128)S(1)}, u32[]{:S(2)}, u32[]{:S(2)}) collective-permute-start(f32[1,128,128]{2,1,0:T(8,128)S(1)} %collective-permute-done), channel_id=1, source_target_pairs={{0,1},{1,0},{2,3},{3,2},{4,5},{5,4},{6,7},{7,6},{8,9},{9,8},{10,11... | collective-permute-start | bytes 196616 | tf_op jit(solution)/shard_map/ppermute | solution.py:273

commit v5 on v4

v5 whole, which is shorter than its diff:
```python
import jax
import jax.numpy as jnp
from jax import lax
from jax.experimental import pallas as pl
from jax.experimental.pallas import tpu as pltpu
from jax.sharding import PartitionSpec as P

F32 = jnp.float32
BF16 = jnp.bfloat16
LANES = 128
VMEM = pl.BlockSpec(memory_space=pltpu.VMEM)
HBM = pl.BlockSpec(memory_space=pltpu.HBM)
ANY = pl.BlockSpec(memory_space=pl.ANY)
LEAN = pltpu.CompilerParams(vmem_limit_bytes=8 << 20)


def split(a):
    high = a.astype(BF16)
    return high, (a - high.astype(F32)).astype(BF16)


def dot(a, b, over):
    return lax.dot_general(a, b, (((over,), (0,)), ((), ())), preferred_element_type=F32)


def product(a, b, over=1):
    (ah, al), (bh, bl) = a, b
    if ah.shape[over] > LANES:
        both = dot(jnp.concatenate([ah, al], 1 - over), bh, over)
        rows = ah.shape[1 - over]
        return both[:rows] + (both[rows:] + dot(ah, bl, over))
    return dot(jnp.concatenate([ah, al], over), jnp.concatenate([bh, bh], 0), over) + dot(ah, bl, over)


def pick(kinds, step, pieces):
    value = pieces[0]
    for at, piece in enumerate(pieces[1:], 1):
        mask = jnp.broadcast_to(kinds[step : step + 1, :], value.shape) == at
        value = jnp.where(mask, piece, value)
    return value


def shape(*dims, dtype=F32):
    return pltpu.VMEM(dims, dtype)


def near(*values, space=pltpu.VMEM):
    return [pltpu.with_memory_space_constraint(value, space) for value in values]


def vmem_call(body, outs, name, *args):
    return pl.pallas_call(
        body,
        out_shape=outs,
        in_specs=[VMEM] * len(args),
        out_specs=[VMEM] * len(outs),
        name=name,
        compiler_params=LEAN,
    )(*near(*args))


def load(vectors, reflectors, tfactors, plan, columns):
    held, height, lanes = reflectors.shape
    block, last = 2 * lanes, tfactors.shape[1] - 1
    groups = plan.shape[0]

    def body(plan, x, v, f, kinds_ref, x_out, v_out, f_out, end_out, plan_ref, sem):
        copies = [(plan, plan_ref), (f.at[:, last], end_out)]
        for at, place in enumerate((0, last)):
            rows = pl.ds(place * block, block)
            copies.append((v.at[:, rows], v_out.at[:, pl.ds(at * block, block)]))
            copies.append((x.at[rows], x_out.at[pl.ds(at * block, block)]))
            copies.append((f.at[:, place], f_out.at[:, at]))
        copies = [pltpu.make_async_copy(*pair, sem.at[at]) for at, pair in enumerate(copies)]
        for copy in copies:
            copy.start()
        me = lax.axis_index("col")
        kinds_ref[...] = jnp.zeros_like(kinds_ref)
        copies[0].wait()
        for step in range(groups):
            group = plan_ref[step]
            piece = (me + columns - group // held) % columns * held + group % held
            kinds_ref[step : step + 1, :] = jnp.full((1, lanes), piece, jnp.int32)
        for copy in copies[1:]:
            copy.wait()

    return pl.pallas_call(
        body,
        out_shape=[
            shape(-(-groups // 8) * 8, lanes, dtype=jnp.int32),
            shape(2 * block, vectors.shape[1]),
            shape(held, 2 * block, lanes),
            shape(held, 2, lanes, lanes),
            shape(held, lanes, lanes),
        ],
        in_specs=[HBM] * 4,
        out_specs=[VMEM] * 5,
        scratch_shapes=[pltpu.SMEM((groups,), jnp.int32), pltpu.SemaphoreType.DMA((8,))],
        name="load",
        compiler_params=LEAN,
    )(*near(plan, vectors, reflectors, tfactors, space=pltpu.HBM))


def is_top(odd_round):
    return (lax.axis_index("row") % 2 == 1) != odd_round


def ordered(top, low):
    first = is_top(False)
    return jnp.where(first, top, low), jnp.where(first, low, top)


def apart(pieces):
    return [piece.at[slot] for piece in pieces for slot in range(piece.shape[0])]


def edges(x, own, others, kinds, step):
    width = x.shape[1]
    strip = own[0].shape[2]
    count = others[0][1].shape[1]
    held = own[0].shape[0]

    def body(kinds_ref, x_ref, own_refl, own_factor, *refs):
        far_refls, far_factors = refs[: len(others)], refs[len(others) : 2 * len(others)]
        coeffs, even_ref, odd_ref = refs[-4:-2], refs[-2], refs[-1]
        firsts, seconds, crosses, weights, projs = [], [], [], [], []
        places = [(0, 0, 0), (1, count - 1, strip)]

        def refl(step, near_row, far_row, rows):
            pieces = [own_refl[slot, near_row : near_row + rows, :] for slot in range(held)]
            pieces += [r[far_row : far_row + rows, :] for r in apart(far_refls)]
            return split(pick(kinds_ref, step, pieces))

        for at, place, outer in places:
            near_row, far_row = at * 2 * strip, place * 2 * strip
            firsts.append(refl(step, near_row, far_row, 2 * strip))
            seconds.append(refl(step + 1, near_row + outer, far_row + outer, strip))
        for (_, _, outer), first, second in zip(places, firsts, seconds):
            crosses.append(product(second, [v[outer : outer + strip] for v in first], over=0))
        for (at, _, outer), first, second in zip(places, firsts, seconds):
            blank = jnp.zeros((strip, strip), BF16)
            second = [jnp.concatenate([v, blank] if outer == 0 else [blank, v], 0) for v in second]
            high, low = split(x_ref[at * 2 * strip : (at + 1) * 2 * strip, :])
            all_high = dot(jnp.concatenate([*first, *second], 1), high, 0)
            all_low = dot(jnp.concatenate([first[0], second[0]], 1), low, 0)
            parts = [all_high[i * strip : (i + 1) * strip] for i in range(4)]
            coeffs[at][...] = parts[0] + (parts[1] + all_low[:strip])
            projs.append(parts[2] + (parts[3] + all_low[strip:]))
        for (at, place, _), cross in zip(places, crosses):
            pieces = [own_factor[slot, at] for slot in range(held)]
            factor = pick(kinds_ref, step, pieces + [r[place] for r in apart(far_factors)])
            weights.append(product(split(cross), split(factor)))
        for at, weight in enumerate(weights):
            projs[at] = projs[at] - product(split(weight), split(coeffs[at][...]))
        even_ref[...], odd_ref[...] = ordered(*projs)

    far = [piece for pair in zip(*others) for piece in pair]
    return vmem_call(body, [shape(strip, width)] * 4, "edges", kinds, x, *own, *far)


def middle(x, edge_rows, own, others, kinds, step, coeffs):
    height, width = x.shape
    held, _, strip = own[0].shape
    block = 2 * strip
    count = height // block

    def body(kinds_ref, edge_ref, top_coeff, low_coeff, *refs):
        far_refls, refs = refs[: len(others)], refs[len(others) :]
        far_factors, refs = refs[: len(others)], refs[len(others) :]
        x_hbm, v_hbm, f_hbm, work_ref, top_ref, low_ref, v_own, f_own, coeff_ref, sem = refs
        inner = pl.ds(block, height - 2 * block)
        copies = [(v_hbm, v_own), (f_hbm, f_own), (x_hbm.at[inner, :], work_ref.at[inner, :])]
        copies = [pltpu.make_async_copy(*pair, sem.at[at]) for at, pair in enumerate(copies)]
        for copy in copies:
            copy.start()
        work_ref[:block, :] = edge_ref[:block, :]
        work_ref[height - block :, :] = edge_ref[block:, :]
        refls, factors = apart([v_own, *far_refls]), apart([f_own, *far_factors])
        coeff_ref[0] = top_coeff[...]
        coeff_ref[count - 1] = low_coeff[...]
        for copy in copies:
            copy.wait()

        def run(step, blocks, offset, known):
            def rows(at):
                return slice(at * block + offset, (at + 1) * block + offset)

            def refl(at):
                return split(pick(kinds_ref, step, [r[rows(at), :] for r in refls]))

            for at in blocks:
                if at not in known:
                    coeff_ref[at] = product(refl(at), split(work_ref[rows(at), :]), over=0)
            for at in blocks:
                factor = split(pick(kinds_ref, step, [r[at] for r in factors]))
                coeff_ref[at] = product(factor, split(coeff_ref[at]))
            for at in blocks:
                change = product(refl(at), split(coeff_ref[at]))
                work_ref[rows(at), :] = work_ref[rows(at), :] - change

        run(step, range(count), 0, (0, count - 1))
        top_ref[...] = work_ref[:strip, :]
        low_ref[...] = work_ref[height - strip :, :]
        run(step + 1, range(count - 1), strip, ())

    far = [piece for pair in zip(*others) for piece in pair]
    args = near(kinds, edge_rows, *coeffs, *far)
    args, specs = args + near(x, *own, space=pltpu.HBM), [VMEM] * len(args) + [HBM] * 3
    return pl.pallas_call(
        body,
        out_shape=[shape(height, width)] + [shape(strip, width)] * 2,
        in_specs=specs,
        out_specs=[VMEM] * 3,
        scratch_shapes=[
            pltpu.VMEM(own[0].shape, F32),
            pltpu.VMEM(own[1].shape, F32),
            pltpu.VMEM((count, strip, width), F32),
            pltpu.SemaphoreType.DMA((3,)),
        ],
        name="middle",
        compiler_params=LEAN,
    )(*args)


def store(work, strip):
    height, width = work.shape

    def body(work_ref, out_ref, sem):
        inner = pl.ds(strip, height - 2 * strip)
        copy = pltpu.make_async_copy(work_ref.at[inner, :], out_ref.at[inner, :], sem)
        copy.start()
        copy.wait()

    return pl.pallas_call(
        body,
        out_shape=jax.ShapeDtypeStruct((height, width), F32),
        in_specs=[VMEM],
        out_specs=ANY,
        scratch_shapes=[pltpu.SemaphoreType.DMA],
        name="store",
        compiler_params=LEAN,
    )(*near(work))


def prepare(own, others, behind, kinds, step, strips, projs):
    strip, width = strips[0].shape
    count = others[0][1].shape[1]
    height = others[0][0].shape[1]
    held = own[0].shape[0]
    far = [piece for pair in zip(*others) for piece in pair]

    def body(kinds_ref, top_ref, low_ref, even_ref, odd_ref, own_refl, own_factor, *refs):
        far_refls, refs = refs[: len(others)], refs[len(others) :]
        far_factors, refs = refs[: len(others)], refs[len(others) :]
        behinds, refs = apart(refs[: len(behind)]), refs[len(behind) :]
        rests, highs, lows = refs[:2], refs[2:4], refs[4:]
        row, last = lax.axis_index("row"), lax.axis_size("row") - 1
        projs = ordered(even_ref[...], odd_ref[...])

        def weight(near_row, far_row, ends, present):
            pieces = [own_refl[slot, near_row : near_row + strip, :] for slot in range(held)]
            pieces += [r[far_row : far_row + strip, :] for r in apart(far_refls)]
            refl = split(pick(kinds_ref, step + 1, pieces))
            value = product(refl, split(pick(kinds_ref, step + 1, ends)))
            return jnp.where(present, value, jnp.zeros_like(value))

        ends = [own_factor[slot, 1] for slot in range(held)]
        ends += [r[count - 1] for r in apart(far_factors)]
        top = weight(0, 0, [r[...] for r in behinds], row > 0)
        low = weight(3 * strip, height - strip, ends, row < last)
        even, odd = ordered(top, low)
        highs[0][...], lows[0][...] = split(even)
        highs[1][...], lows[1][...] = split(odd)
        top = top_ref[...] - product(split(top), split(projs[0]))
        low = low_ref[...] - product(split(low), split(projs[1]))
        rests[0][...], rests[1][...] = ordered(top, low)

    rest, half = shape(strip, width), shape(strip, strip, dtype=BF16)
    return vmem_call(
        body,
        [rest, rest, half, half, half, half],
        "prepare",
        *(kinds, *strips, *projs, *own, *far, *behind),
    )


def finish(out, prepared, gots):
    height, width = out.shape
    strip = gots[0].shape[0]

    def body(*refs):
        rests, highs, lows, gots = refs[:2], refs[2:4], refs[4:6], refs[6:8]
        out_ref, new_ref, sem = refs[9:]
        row, last = lax.axis_index("row"), lax.axis_size("row") - 1
        copies = []
        for at in range(2):
            top = is_top(at == 1)
            present = jnp.where(top, row > 0, row < last)
            other = jnp.where(present, gots[at][...], jnp.zeros_like(gots[at]))
            weight = highs[at][...], lows[at][...]
            new_ref[at] = rests[at][...] - product(weight, split(other))
            start = pl.multiple_of(jnp.where(top, 0, height - strip), strip)
            rows = out_ref.at[pl.ds(start, strip), :]
            copies.append(pltpu.make_async_copy(new_ref.at[at], rows, sem.at[at]))
            copies[-1].start()
        for copy in copies:
            copy.wait()

    return pl.pallas_call(
        body,
        out_shape=jax.ShapeDtypeStruct((height, width), F32),
        in_specs=[VMEM] * 8 + [ANY],
        out_specs=ANY,
        scratch_shapes=[pltpu.VMEM((2, strip, width), F32), pltpu.SemaphoreType.DMA((2,))],
        input_output_aliases={8: 0},
        name="finish",
        compiler_params=LEAN,
    )(*near(*prepared, *gots), out)


def local(vectors, reflectors, tfactors, plan):
    groups, strip = plan.shape[0], reflectors.shape[2]
    rows, columns = lax.axis_size("row"), lax.axis_size("col")

    def around(block, shift):
        return lax.ppermute(block, "col", [(c, (c + shift) % columns) for c in range(columns)])

    def trade(block, odd_round):
        route = []
        for row in range(rows):
            for col in range(columns):
                there = row + 1 if (row % 2 == 1) == odd_round else row - 1
                there = (there, col) if 0 <= there < rows else (row, (col + 1) % columns)
                route.append((row * columns + col, there[0] * columns + there[1]))
        return lax.ppermute(block, ("row", "col"), route)

    shifts = range(1, columns)
    others = [(around(reflectors, shift), around(tfactors, shift)) for shift in shifts]
    current, behinds = vectors, None
    for step in range(0, groups, 2):
        kinds, edge_rows, *own, end = load(current, reflectors, tfactors, plan, columns)
        if behinds is None:
            behind = lax.ppermute(end, "row", [(r, (r + 1) % rows) for r in range(rows)])
        *coeffs, even_proj, odd_proj = edges(edge_rows, own, others, kinds, step)
        gots = trade(even_proj, False), trade(odd_proj, True)
        work, *strips = middle(
            current, edge_rows, (reflectors, tfactors), others, kinds, step, coeffs
        )
        if behinds is None:
            behind, strips[0] = lax.optimization_barrier((behind, strips[0]))
            behinds = [behind, *(around(behind, shift) for shift in shifts)]
        out = store(work, strip)
        prepared = prepare(own, others, behinds, kinds, step, strips, (even_proj, odd_proj))
        current = finish(out, prepared, gots)
    return current


def solution(mesh):
    return jax.shard_map(
        local,
        mesh=mesh,
        in_specs=(P("row", "col"), P("col", "row", None), P("col", "row", None, None), P()),
        out_specs=P("row", "col"),
        check_vma=False,
    )
```

time: 15.1 us -> 14.1 us (0.934)
  the two profiles are of different devices: /device:TPU:0 before, /device:TPU:2 now
where the time goes in v5:
time: 14.1 us; the launch traced here: 14 us
  Pallas kernels  7.23 us (51%)
  starting transfers between devices  5.17 us (37%)
  waiting for transfers between devices  1.51 us (11%)
    ppermute x2, starting transfers between devices, trade(): return lax.ppermute(block, ('row', 'col'), route)  3.05 us
    pallas_call x1, Pallas kernels, middle(): pl.pallas_call(body, out_shape=[shape(height, width)] + [shape(strip, wid...  3.02 us
    ppermute x1, starting transfers between devices, local(): lax.ppermute(end, 'row', [(r, (r + 1) % rows) for r in range(rows)])  1.54 us
    pallas_call x1, Pallas kernels, load(): pl.pallas_call(body, out_shape=[shape(-(-groups // 8) * 8, lanes, dtype=j...  1.27 us
    ppermute x2, waiting for transfers between devices, trade(): return lax.ppermute(block, ('row', 'col'), route)  1.16 us
    pallas_call x2, Pallas kernels, vmem_call(): pl.pallas_call(body, out_shape=outs, in_specs=[VMEM] * len(args), out_spe...  1.09 us
    pallas_call x1, Pallas kernels, finish(): pl.pallas_call(body, out_shape=jax.ShapeDtypeStruct((height, width), F32)...  0.95 us
    pallas_call x1, Pallas kernels, store(): pl.pallas_call(body, out_shape=jax.ShapeDtypeStruct((height, width), F32)...  0.89 us
  transfers between devices with their start and end apart: 6, of which 3 were waited for; matrix products, arithmetic and copies ran while one was open for 0% of the time, Pallas kernels for 45%

profile of v5, /device:TPU:2, one launch (start us, length us, event | category | flops | bytes accessed | tf_op | source)
XLA Modules:
  0.0 14.0 jit_solution(1504929728276191864)
XLA Ops:
  0.0 0.0 collective-permute-start.1
  0.0 0.5 %collective-permute-start.2 = (f32[1,4,128,128]{3,2,1,0:T(8,128)}, f32[1,4,128,128]{3,2,1,0:T(8,128)S(1)}, u32[]{:S(2)}, u32[]{:S(2)}) collective-permute-start(f32[1,4,128,128]{3,2,1,0:T(8,128)} %refs_4_.1), channel_id=1, source_target_pairs={{0,1},{1,0},{2,3},{3,2},{4,5},{5,4},{6,7},{7,6},{8,9},{9,8},{10,11... | collective-permute-start | bytes 786440 | tf_op jit(solution)/shard_map/ppermute | solution.py:326
  0.5 1.3 %load.1 = (s32[8,128]{1,0:T(8,128)S(1)}, f32[512,256]{1,0:T(8,128)S(1)}, f32[1,512,128]{2,1,0:T(8,128)S(1)}, f32[1,2,128,128]{3,2,1,0:T(8,128)S(1)}, f32[1,128,128]{2,1,0:T(8,128)S(1)}) custom-call(s32[2]{0:T(128)} %plan.1, f32[1024,256]{1,0:T(8,128)} %refs_2_.1, f32[1,1024,128]{2,1,0:T(8,128)} %refs_3_.1, f32[1,4,128,128]{3,2,1,0:T(8,128)} %refs_4_.1), custom_call_target="tpu_custom_call" | custom-call | tf_op jit(solution)/shard_map/load/pallas_call | solution.py:87
  1.8 1.5 %collective-permute-start = (f32[1,128,128]{2,1,0:T(8,128)S(1)}, f32[1,128,128]{2,1,0:T(8,128)S(1)}, u32[]{:S(2)}, u32[]{:S(2)}) collective-permute-start(f32[1,128,128]{2,1,0:T(8,128)S(1)} %get-tuple-element.26), channel_id=1, source_target_pairs={{0,2},{2,4},{4,6},{6,8},{8,10},{10,12},{12,14},{14,16},{16,18},{18... | collective-permute-start | bytes 196616 | tf_op jit(solution)/shard_map/ppermute | solution.py:343
  3.3 0.0 collective-permute-done.2.refs_1_
  3.3 0.0 collective-permute-done.1.refs_0_
  3.3 0.7 %edges.1 = (f32[128,256]{1,0:T(8,128)S(1)}, f32[128,256]{1,0:T(8,128)S(1)}, f32[128,256]{1,0:T(8,128)S(1)}, f32[128,256]{1,0:T(8,128)S(1)}) custom-call(s32[8,128]{1,0:T(8,128)S(1)} %get-tuple-element.25.kinds_ref, f32[512,256]{1,0:T(8,128)S(1)} %get-tuple-element.27.x_ref.edge_ref, f32[1,512,128]{2,1,0:T(8,128)S(1)} %get-tuple-element.28.own_refl, ...), custom_call_target="tpu_custom_call" | custom-call | tf_op jit(solution)/shard_map/edges/pallas_call | solution.py:52
  4.1 0.6 %collective-permute-start.4 = (f32[128,256]{1,0:T(8,128)S(1)}, f32[128,256]{1,0:T(8,128)S(1)}, u32[]{:S(2)}, u32[]{:S(2)}) collective-permute-start(f32[128,256]{1,0:T(8,128)S(1)} %get-tuple-element.35.even_ref), channel_id=1, source_target_pairs={{0,2},{1,3},{2,0},{3,1},{4,6},{5,7},{6,4},{7,5},{8,10},{9,11},{10,... | collective-permute-start | bytes 393224 | tf_op jit(solution)/shard_map/ppermute | solution.py:335
  4.7 2.4 %collective-permute-start.5 = (f32[128,256]{1,0:T(8,128)S(1)}, f32[128,256]{1,0:T(8,128)S(1)}, u32[]{:S(2)}, u32[]{:S(2)}) collective-permute-start(f32[128,256]{1,0:T(8,128)S(1)} %get-tuple-element.36.odd_ref), channel_id=1, source_target_pairs={{0,1},{1,0},{2,4},{3,5},{4,2},{5,3},{6,8},{7,9},{8,6},{9,7},{10,12... | collective-permute-start | bytes 393224 | tf_op jit(solution)/shard_map/ppermute | solution.py:335
  7.1 3.0 %middle.1 = (f32[1024,256]{1,0:T(8,128)S(1)}, f32[128,256]{1,0:T(8,128)S(1)}, f32[128,256]{1,0:T(8,128)S(1)}) custom-call(s32[8,128]{1,0:T(8,128)S(1)} %get-tuple-element.25.kinds_ref, f32[512,256]{1,0:T(8,128)S(1)} %get-tuple-element.27.x_ref.edge_ref, f32[128,256]{1,0:T(8,128)S(1)} %get-tuple-element.30.top_coeff, ...), custom_call_target="tpu_custom_call" | custom-call | tf_op jit(solution)/shard_map/middle/pallas_call | solution.py:209
  10.1 0.0 collective-permute-done.refs_2_
  10.1 0.1 collective-permute-start.3
  10.2 0.9 %store.1.refs_8_ = f32[1024,256]{1,0:T(8,128)} custom-call(f32[1024,256]{1,0:T(8,128)S(1)} %get-tuple-element.44.work_ref), custom_call_target="tpu_custom_call" | custom-call | tf_op jit(solution)/shard_map/store/pallas_call | solution.py:234
  11.1 0.3 %collective-permute-done.3.refs_3_ = f32[1,128,128]{2,1,0:T(8,128)S(1)} collective-permute-done((f32[1,128,128]{2,1,0:T(8,128)S(1)}, f32[1,128,128]{2,1,0:T(8,128)S(1)}, u32[]{:S(2)}, u32[]{:S(2)}) %collective-permute-start.3) | collective-permute-done | bytes 65568 | tf_op jit(solution)/shard_map/ppermute | solution.py:326
  11.5 0.4 %prepare.1 = (f32[128,256]{1,0:T(8,128)S(1)}, f32[128,256]{1,0:T(8,128)S(1)}, bf16[128,128]{1,0:T(8,128)(2,1)S(1)}, bf16[128,128]{1,0:T(8,128)(2,1)S(1)}, bf16[1...) custom-call(s32[8,128]{1,0:T(8,128)S(1)} %get-tuple-element.25.kinds_ref, f32[128,256]{1,0:T(8,128)S(1)} %get-tuple-element.33.top_ref, ...), custom_call_target="tpu_custom_call" | custom-call | tf_op jit(solution)/shard_map/prepare/pallas_call | solution.py:52
  11.9 0.2 %collective-permute-done.4.refs_6_ = f32[128,256]{1,0:T(8,128)S(1)} collective-permute-done((f32[128,256]{1,0:T(8,128)S(1)}, f32[128,256]{1,0:T(8,128)S(1)}, u32[]{:S(2)}, u32[]{:S(2)}) %collective-permute-start.4) | collective-permute-done | bytes 131104 | tf_op jit(solution)/shard_map/ppermute | solution.py:335
  12.1 1.0 %collective-permute-done.5.refs_7_ = f32[128,256]{1,0:T(8,128)S(1)} collective-permute-done((f32[128,256]{1,0:T(8,128)S(1)}, f32[128,256]{1,0:T(8,128)S(1)}, u32[]{:S(2)}, u32[]{:S(2)}) %collective-permute-start.5) | collective-permute-done | bytes 131104 | tf_op jit(solution)/shard_map/ppermute | solution.py:335
  13.0 1.0 %finish.1 = f32[1024,256]{1,0:T(8,128)} custom-call(f32[128,256]{1,0:T(8,128)S(1)} %get-tuple-element.38.refs_0_, f32[128,256]{1,0:T(8,128)S(1)} %get-tuple-element.39.refs_1_, bf16[128,128]{1,0:T(8,128)(2,1)S(1)} %get-tuple-element.40.refs_2_, bf16[128,128]{1,0:T(8,128)(2,1)S(1)} %get-tuple-element.41.refs_3_, ...), custom_call_target="tpu_custom_call", output_to_operand_aliasing={{}: (8, {})} | custom-call | tf_op jit(solution)/shard_map/finish/pallas_call | solution.py:309
Async XLA Ops:
  0.0 3.3 %collective-permute-start.1 = (f32[1,1024,128]{2,1,0:T(8,128)}, f32[1,1024,128]{2,1,0:T(8,128)S(1)}, u32[]{:S(2)}, u32[]{:S(2)}) collective-permute-start(f32[1,1024,128]{2,1,0:T(8,128)} %refs_3_.1), channel_id=1, source_target_pairs={{0,1},{1,0},{2,3},{3,2},{4,5},{5,4},{6,7},{7,6},{8,9},{9,8},{10,11... | collective-permute-start | bytes 1572872 | tf_op jit(solution)/shard_map/ppermute | solution.py:326
  0.0 3.3 %collective-permute-start.2 = (f32[1,4,128,128]{3,2,1,0:T(8,128)}, f32[1,4,128,128]{3,2,1,0:T(8,128)S(1)}, u32[]{:S(2)}, u32[]{:S(2)}) collective-permute-start(f32[1,4,128,128]{3,2,1,0:T(8,128)} %refs_4_.1), channel_id=1, source_target_pairs={{0,1},{1,0},{2,3},{3,2},{4,5},{5,4},{6,7},{7,6},{8,9},{9,8},{10,11... | collective-permute-start | bytes 786440 | tf_op jit(solution)/shard_map/ppermute | solution.py:326
  1.8 8.3 %collective-permute-start = (f32[1,128,128]{2,1,0:T(8,128)S(1)}, f32[1,128,128]{2,1,0:T(8,128)S(1)}, u32[]{:S(2)}, u32[]{:S(2)}) collective-permute-start(f32[1,128,128]{2,1,0:T(8,128)S(1)} %get-tuple-element.26), channel_id=1, source_target_pairs={{0,2},{2,4},{4,6},{6,8},{8,10},{10,12},{12,14},{14,16},{16,18},{18... | collective-permute-start | bytes 196616 | tf_op jit(solution)/shard_map/ppermute | solution.py:343
  4.1 8.0 %collective-permute-start.4 = (f32[128,256]{1,0:T(8,128)S(1)}, f32[128,256]{1,0:T(8,128)S(1)}, u32[]{:S(2)}, u32[]{:S(2)}) collective-permute-start(f32[128,256]{1,0:T(8,128)S(1)} %get-tuple-element.35.even_ref), channel_id=1, source_target_pairs={{0,2},{1,3},{2,0},{3,1},{4,6},{5,7},{6,4},{7,5},{8,10},{9,11},{10,... | collective-permute-start | bytes 393224 | tf_op jit(solution)/shard_map/ppermute | solution.py:335
  4.7 8.4 %collective-permute-start.5 = (f32[128,256]{1,0:T(8,128)S(1)}, f32[128,256]{1,0:T(8,128)S(1)}, u32[]{:S(2)}, u32[]{:S(2)}) collective-permute-start(f32[128,256]{1,0:T(8,128)S(1)} %get-tuple-element.36.odd_ref), channel_id=1, source_target_pairs={{0,1},{1,0},{2,4},{3,5},{4,2},{5,3},{6,8},{7,9},{8,6},{9,7},{10,12... | collective-permute-start | bytes 393224 | tf_op jit(solution)/shard_map/ppermute | solution.py:335
  10.1 1.3 %collective-permute-start.3 = (f32[1,128,128]{2,1,0:T(8,128)S(1)}, f32[1,128,128]{2,1,0:T(8,128)S(1)}, u32[]{:S(2)}, u32[]{:S(2)}) collective-permute-start(f32[1,128,128]{2,1,0:T(8,128)S(1)} %collective-permute-done.refs_2_), channel_id=1, source_target_pairs={{0,1},{1,0},{2,3},{3,2},{4,5},{5,4},{6,7},{7,6},{8,9},{9,8},{10,11... | collective-permute-start | bytes 196616 | tf_op jit(solution)/shard_map/ppermute | solution.py:326

commit v6 on v5

--- a/solution.py
+++ b/solution.py
@@ -114,48 +114,42 @@
     return [piece.at[slot] for piece in pieces for slot in range(piece.shape[0])]
 
 
-def edges(x, own, others, kinds, step):
+def edge(x, own, others, kinds, step, odd_round):
     width = x.shape[1]
-    strip = own[0].shape[2]
-    count = others[0][1].shape[1]
-    held = own[0].shape[0]
+    held, _, strip = own[0].shape
+    block = 2 * strip
+    height, count = others[0][0].shape[1], others[0][1].shape[1]
 
     def body(kinds_ref, x_ref, own_refl, own_factor, *refs):
-        far_refls, far_factors = refs[: len(others)], refs[len(others) : 2 * len(others)]
-        coeffs, even_ref, odd_ref = refs[-4:-2], refs[-2], refs[-1]
-        firsts, seconds, crosses, weights, projs = [], [], [], [], []
-        places = [(0, 0, 0), (1, count - 1, strip)]
-
-        def refl(step, near_row, far_row, rows):
-            pieces = [own_refl[slot, near_row : near_row + rows, :] for slot in range(held)]
-            pieces += [r[far_row : far_row + rows, :] for r in apart(far_refls)]
-            return split(pick(kinds_ref, step, pieces))
-
-        for at, place, outer in places:
-            near_row, far_row = at * 2 * strip, place * 2 * strip
-            firsts.append(refl(step, near_row, far_row, 2 * strip))
-            seconds.append(refl(step + 1, near_row + outer, far_row + outer, strip))
-        for (_, _, outer), first, second in zip(places, firsts, seconds):
-            crosses.append(product(second, [v[outer : outer + strip] for v in first], over=0))
-        for (at, _, outer), first, second in zip(places, firsts, seconds):
-            blank = jnp.zeros((strip, strip), BF16)
-            second = [jnp.concatenate([v, blank] if outer == 0 else [blank, v], 0) for v in second]
-            high, low = split(x_ref[at * 2 * strip : (at + 1) * 2 * strip, :])
-            all_high = dot(jnp.concatenate([*first, *second], 1), high, 0)
-            all_low = dot(jnp.concatenate([first[0], second[0]], 1), low, 0)
-            parts = [all_high[i * strip : (i + 1) * strip] for i in range(4)]
-            coeffs[at][...] = parts[0] + (parts[1] + all_low[:strip])
-            projs.append(parts[2] + (parts[3] + all_low[strip:]))
-        for (at, place, _), cross in zip(places, crosses):
-            pieces = [own_factor[slot, at] for slot in range(held)]
-            factor = pick(kinds_ref, step, pieces + [r[place] for r in apart(far_factors)])
-            weights.append(product(split(cross), split(factor)))
-        for at, weight in enumerate(weights):
-            projs[at] = projs[at] - product(split(weight), split(coeffs[at][...]))
-        even_ref[...], odd_ref[...] = ordered(*projs)
+        far_refls, far_factors = refs[: len(others)], refs[len(others) : -2]
+        coeff_ref, proj_ref = refs[-2:]
+        top = is_top(odd_round)
+        near_rows = pl.ds(pl.multiple_of(jnp.where(top, 0, block), block), block)
+        far_rows = pl.ds(pl.multiple_of(jnp.where(top, 0, height - block), block), block)
+        slots = range(held)
+
+        def refl(step):
+            pieces = [own_refl[slot, near_rows, :] for slot in slots]
+            return pick(kinds_ref, step, pieces + [r[far_rows, :] for r in apart(far_refls)])
+
+        row = lax.broadcasted_iota(jnp.int32, (block, strip), 0) - jnp.where(top, 0, strip)
+        second = jnp.where((row >= 0) & (row < strip), refl(step + 1), 0.0)
+        first, second = split(refl(step)), split(second)
+        high, low = split(x_ref[near_rows, :])
+        cross = product(second, first, over=0)
+        all_high = dot(jnp.concatenate([*first, *second], 1), high, 0)
+        all_low = dot(jnp.concatenate([first[0], second[0]], 1), low, 0)
+        pieces = [own_factor[slot, jnp.where(top, 0, 1)] for slot in slots]
+        pieces += [r[jnp.where(top, 0, count - 1)] for r in apart(far_factors)]
+        weight = product(split(cross), split(pick(kinds_ref, step, pieces)))
+        parts = [all_high[i * strip : (i + 1) * strip] for i in range(4)]
+        coeff = parts[0] + (parts[1] + all_low[:strip])
+        coeff_ref[...] = coeff
+        rest = product(split(weight), split(coeff))
+        proj_ref[...] = parts[2] + (parts[3] + all_low[strip:]) - rest
 
     far = [piece for pair in zip(*others) for piece in pair]
-    return vmem_call(body, [shape(strip, width)] * 4, "edges", kinds, x, *own, *far)
+    return vmem_call(body, [shape(strip, width)] * 2, "edge", kinds, x, *own, *far)
 
 
 def middle(x, edge_rows, own, others, kinds, step, coeffs):
@@ -164,7 +158,7 @@
     block = 2 * strip
     count = height // block
 
-    def body(kinds_ref, edge_ref, top_coeff, low_coeff, *refs):
+    def body(kinds_ref, edge_ref, even_coeff, odd_coeff, *refs):
         far_refls, refs = refs[: len(others)], refs[len(others) :]
         far_factors, refs = refs[: len(others)], refs[len(others) :]
         x_hbm, v_hbm, f_hbm, work_ref, top_ref, low_ref, v_own, f_own, coeff_ref, sem = refs
@@ -176,8 +170,7 @@
         work_ref[:block, :] = edge_ref[:block, :]
         work_ref[height - block :, :] = edge_ref[block:, :]
         refls, factors = apart([v_own, *far_refls]), apart([f_own, *far_factors])
-        coeff_ref[0] = top_coeff[...]
-        coeff_ref[count - 1] = low_coeff[...]
+        coeff_ref[0], coeff_ref[count - 1] = ordered(even_coeff[...], odd_coeff[...])
         for copy in copies:
             copy.wait()
 
@@ -341,8 +334,12 @@
         kinds, edge_rows, *own, end = load(current, reflectors, tfactors, plan, columns)
         if behinds is None:
             behind = lax.ppermute(end, "row", [(r, (r + 1) % rows) for r in range(rows)])
-        *coeffs, even_proj, odd_proj = edges(edge_rows, own, others, kinds, step)
-        gots = trade(even_proj, False), trade(odd_proj, True)
+        coeffs, projs, gots = [], [], []
+        for odd_round in (False, True):
+            coeff, proj = edge(edge_rows, own, others, kinds, step, odd_round)
+            coeffs.append(coeff)
+            projs.append(proj)
+            gots.append(trade(proj, odd_round))
         work, *strips = middle(
             current, edge_rows, (reflectors, tfactors), others, kinds, step, coeffs
         )
@@ -350,7 +347,7 @@
             behind, strips[0] = lax.optimization_barrier((behind, strips[0]))
             behinds = [behind, *(around(behind, shift) for shift in shifts)]
         out = store(work, strip)
-        prepared = prepare(own, others, behinds, kinds, step, strips, (even_proj, odd_proj))
+        prepared = prepare(own, others, behinds, kinds, step, strips, projs)
         current = finish(out, prepared, gots)
     return current
 

time: 14.1 us -> 14.1 us (level)
  the two profiles are of different devices: /device:TPU:2 before, /device:TPU:0 now
where the time goes in v6:
time: 14.1 us; the launch traced here: 13.8 us
  Pallas kernels  7.74 us (55%)
  starting transfers between devices  5.25 us (37%)
  waiting for transfers between devices  0.75 us (5%)
    ppermute x1, starting transfers between devices, local(): lax.ppermute(end, 'row', [(r, (r + 1) % rows) for r in range(rows)])  3.02 us
    pallas_call x1, Pallas kernels, middle(): pl.pallas_call(body, out_shape=[shape(height, width)] + [shape(strip, wid...  3.02 us
    ppermute x2, starting transfers between devices, trade(): return lax.ppermute(block, ('row', 'col'), route)  1.63 us
    pallas_call x3, Pallas kernels, vmem_call(): pl.pallas_call(body, out_shape=outs, in_specs=[VMEM] * len(args), out_spe...  1.59 us
    pallas_call x1, Pallas kernels, load(): pl.pallas_call(body, out_shape=[shape(-(-groups // 8) * 8, lanes, dtype=j...  1.27 us
    pallas_call x1, Pallas kernels, finish(): pl.pallas_call(body, out_shape=jax.ShapeDtypeStruct((height, width), F32)...  0.98 us
    pallas_call x1, Pallas kernels, store(): pl.pallas_call(body, out_shape=jax.ShapeDtypeStruct((height, width), F32)...  0.89 us
    ppermute x3, starting transfers between devices, around(): lax.ppermute(block, 'col', [(c, (c + shift) % columns) for c in range(col...  0.6 us
  transfers between devices with their start and end apart: 6, of which 2 were waited for; matrix products, arithmetic and copies ran while one was open for 0% of the time, Pallas kernels for 49%

profile of v6, /device:TPU:0, one launch (start us, length us, event | category | flops | bytes accessed | tf_op | source)
XLA Modules:
  0.0 13.8 jit_solution(5639024178417941642)
XLA Ops:
  0.0 0.5 %collective-permute-start.1 = (f32[1,1024,128]{2,1,0:T(8,128)}, f32[1,1024,128]{2,1,0:T(8,128)S(1)}, u32[]{:S(2)}, u32[]{:S(2)}) collective-permute-start(f32[1,1024,128]{2,1,0:T(8,128)} %refs_3_.1), channel_id=1, source_target_pairs={{0,1},{1,0},{2,3},{3,2},{4,5},{5,4},{6,7},{7,6},{8,9},{9,8},{10,11... | collective-permute-start | bytes 1572872 | tf_op jit(solution)/shard_map/ppermute | solution.py:319
  0.5 0.0 collective-permute-start.2
  0.5 1.3 %load.1 = (s32[8,128]{1,0:T(8,128)S(1)}, f32[512,256]{1,0:T(8,128)S(1)}, f32[1,512,128]{2,1,0:T(8,128)S(1)}, f32[1,2,128,128]{3,2,1,0:T(8,128)S(1)}, f32[1,128,128]{2,1,0:T(8,128)S(1)}) custom-call(s32[2]{0:T(128)} %plan.1, f32[1024,256]{1,0:T(8,128)} %refs_2_.1, f32[1,1024,128]{2,1,0:T(8,128)} %refs_3_.1, f32[1,4,128,128]{3,2,1,0:T(8,128)} %refs_4_.1), custom_call_target="tpu_custom_call" | custom-call | tf_op jit(solution)/shard_map/load/pallas_call | solution.py:87
  1.8 3.0 %collective-permute-start = (f32[1,128,128]{2,1,0:T(8,128)S(1)}, f32[1,128,128]{2,1,0:T(8,128)S(1)}, u32[]{:S(2)}, u32[]{:S(2)}) collective-permute-start(f32[1,128,128]{2,1,0:T(8,128)S(1)} %get-tuple-element.26), channel_id=1, source_target_pairs={{0,2},{2,4},{4,6},{6,8},{8,10},{10,12},{12,14},{14,16},{16,18},{18... | collective-permute-start | bytes 196616 | tf_op jit(solution)/shard_map/ppermute | solution.py:336
  4.8 0.0 collective-permute-done.2.refs_1_
  4.8 0.0 collective-permute-done.1.refs_0_
  4.8 0.6 %edge.2 = (f32[128,256]{1,0:T(8,128)S(1)}, f32[128,256]{1,0:T(8,128)S(1)}) custom-call(s32[8,128]{1,0:T(8,128)S(1)} %get-tuple-element.25.kinds_ref, f32[512,256]{1,0:T(8,128)S(1)} %get-tuple-element.27.x_ref.edge_ref, f32[1,512,128]{2,1,0:T(8,128)S(1)} %get-tuple-element.28.own_refl, f32[1,2,128,128]{3,2,1,0:T(8,128)S(1)} %get-tuple-element.29.own_factor, ...), custom_call_target="tpu_custom_call" | custom-call | tf_op jit(solution)/shard_map/edge/pallas_call | solution.py:52
  5.4 1.6 %collective-permute-start.4 = (f32[128,256]{1,0:T(8,128)S(1)}, f32[128,256]{1,0:T(8,128)S(1)}, u32[]{:S(2)}, u32[]{:S(2)}) collective-permute-start(f32[128,256]{1,0:T(8,128)S(1)} %get-tuple-element.35.even_ref), channel_id=1, source_target_pairs={{0,2},{1,3},{2,0},{3,1},{4,6},{5,7},{6,4},{7,5},{8,10},{9,11},{10,... | collective-permute-start | bytes 393224 | tf_op jit(solution)/shard_map/ppermute | solution.py:328
  7.0 0.6 %edge.3 = (f32[128,256]{1,0:T(8,128)S(1)}, f32[128,256]{1,0:T(8,128)S(1)}) custom-call(s32[8,128]{1,0:T(8,128)S(1)} %get-tuple-element.25.kinds_ref, f32[512,256]{1,0:T(8,128)S(1)} %get-tuple-element.27.x_ref.edge_ref, f32[1,512,128]{2,1,0:T(8,128)S(1)} %get-tuple-element.28.own_refl, f32[1,2,128,128]{3,2,1,0:T(8,128)S(1)} %get-tuple-element.29.own_factor, ...), custom_call_target="tpu_custom_call" | custom-call | tf_op jit(solution)/shard_map/edge/pallas_call | solution.py:52
  7.6 0.1 collective-permute-start.5
  7.7 3.0 %middle.1 = (f32[1024,256]{1,0:T(8,128)S(1)}, f32[128,256]{1,0:T(8,128)S(1)}, f32[128,256]{1,0:T(8,128)S(1)}) custom-call(s32[8,128]{1,0:T(8,128)S(1)} %get-tuple-element.25.kinds_ref, f32[512,256]{1,0:T(8,128)S(1)} %get-tuple-element.27.x_ref.edge_ref, f32[128,256]{1,0:T(8,128)S(1)} %get-tuple-element.30.even_coeff, ...), custom_call_target="tpu_custom_call" | custom-call | tf_op jit(solution)/shard_map/middle/pallas_call | solution.py:202
  10.7 0.5 %collective-permute-done.refs_2_ = f32[1,128,128]{2,1,0:T(8,128)S(1)} collective-permute-done((f32[1,128,128]{2,1,0:T(8,128)S(1)}, f32[1,128,128]{2,1,0:T(8,128)S(1)}, u32[]{:S(2)}, u32[]{:S(2)}) %collective-permute-start) | collective-permute-done | bytes 65568 | tf_op jit(solution)/shard_map/ppermute | solution.py:336
  11.2 0.1 collective-permute-start.3
  11.3 0.9 %store.1.refs_8_ = f32[1024,256]{1,0:T(8,128)} custom-call(f32[1024,256]{1,0:T(8,128)S(1)} %get-tuple-element.44.work_ref), custom_call_target="tpu_custom_call" | custom-call | tf_op jit(solution)/shard_map/store/pallas_call | solution.py:227
  12.2 0.3 %collective-permute-done.3.refs_3_ = f32[1,128,128]{2,1,0:T(8,128)S(1)} collective-permute-done((f32[1,128,128]{2,1,0:T(8,128)S(1)}, f32[1,128,128]{2,1,0:T(8,128)S(1)}, u32[]{:S(2)}, u32[]{:S(2)}) %collective-permute-start.3) | collective-permute-done | bytes 65568 | tf_op jit(solution)/shard_map/ppermute | solution.py:319
  12.4 0.4 %prepare.1 = (f32[128,256]{1,0:T(8,128)S(1)}, f32[128,256]{1,0:T(8,128)S(1)}, bf16[128,128]{1,0:T(8,128)(2,1)S(1)}, bf16[128,128]{1,0:T(8,128)(2,1)S(1)}, bf16[1...) custom-call(s32[8,128]{1,0:T(8,128)S(1)} %get-tuple-element.25.kinds_ref, f32[128,256]{1,0:T(8,128)S(1)} %get-tuple-element.33.top_ref, ...), custom_call_target="tpu_custom_call" | custom-call | tf_op jit(solution)/shard_map/prepare/pallas_call | solution.py:52
  12.8 0.0 collective-permute-done.4.refs_6_
  12.8 0.0 collective-permute-done.5.refs_7_
  12.8 1.0 %finish.1 = f32[1024,256]{1,0:T(8,128)} custom-call(f32[128,256]{1,0:T(8,128)S(1)} %get-tuple-element.38.refs_0_, f32[128,256]{1,0:T(8,128)S(1)} %get-tuple-element.39.refs_1_, bf16[128,128]{1,0:T(8,128)(2,1)S(1)} %get-tuple-element.40.refs_2_, bf16[128,128]{1,0:T(8,128)(2,1)S(1)} %get-tuple-element.41.refs_3_, ...), custom_call_target="tpu_custom_call", output_to_operand_aliasing={{}: (8, {})} | custom-call | tf_op jit(solution)/shard_map/finish/pallas_call | solution.py:302
Async XLA Ops:
  0.0 4.8 %collective-permute-start.1 = (f32[1,1024,128]{2,1,0:T(8,128)}, f32[1,1024,128]{2,1,0:T(8,128)S(1)}, u32[]{:S(2)}, u32[]{:S(2)}) collective-permute-start(f32[1,1024,128]{2,1,0:T(8,128)} %refs_3_.1), channel_id=1, source_target_pairs={{0,1},{1,0},{2,3},{3,2},{4,5},{5,4},{6,7},{7,6},{8,9},{9,8},{10,11... | collective-permute-start | bytes 1572872 | tf_op jit(solution)/shard_map/ppermute | solution.py:319
  0.5 4.3 %collective-permute-start.2 = (f32[1,4,128,128]{3,2,1,0:T(8,128)}, f32[1,4,128,128]{3,2,1,0:T(8,128)S(1)}, u32[]{:S(2)}, u32[]{:S(2)}) collective-permute-start(f32[1,4,128,128]{3,2,1,0:T(8,128)} %refs_4_.1), channel_id=1, source_target_pairs={{0,1},{1,0},{2,3},{3,2},{4,5},{5,4},{6,7},{7,6},{8,9},{9,8},{10,11... | collective-permute-start | bytes 786440 | tf_op jit(solution)/shard_map/ppermute | solution.py:319
  1.8 9.4 %collective-permute-start = (f32[1,128,128]{2,1,0:T(8,128)S(1)}, f32[1,128,128]{2,1,0:T(8,128)S(1)}, u32[]{:S(2)}, u32[]{:S(2)}) collective-permute-start(f32[1,128,128]{2,1,0:T(8,128)S(1)} %get-tuple-element.26), channel_id=1, source_target_pairs={{0,2},{2,4},{4,6},{6,8},{8,10},{10,12},{12,14},{14,16},{16,18},{18... | collective-permute-start | bytes 196616 | tf_op jit(solution)/shard_map/ppermute | solution.py:336
  5.4 7.4 %collective-permute-start.4 = (f32[128,256]{1,0:T(8,128)S(1)}, f32[128,256]{1,0:T(8,128)S(1)}, u32[]{:S(2)}, u32[]{:S(2)}) collective-permute-start(f32[128,256]{1,0:T(8,128)S(1)} %get-tuple-element.35.even_ref), channel_id=1, source_target_pairs={{0,2},{1,3},{2,0},{3,1},{4,6},{5,7},{6,4},{7,5},{8,10},{9,11},{10,... | collective-permute-start | bytes 393224 | tf_op jit(solution)/shard_map/ppermute | solution.py:328
  7.6 5.2 %collective-permute-start.5 = (f32[128,256]{1,0:T(8,128)S(1)}, f32[128,256]{1,0:T(8,128)S(1)}, u32[]{:S(2)}, u32[]{:S(2)}) collective-permute-start(f32[128,256]{1,0:T(8,128)S(1)} %get-tuple-element.36.odd_ref), channel_id=1, source_target_pairs={{0,1},{1,0},{2,4},{3,5},{4,2},{5,3},{6,8},{7,9},{8,6},{9,7},{10,12... | collective-permute-start | bytes 393224 | tf_op jit(solution)/shard_map/ppermute | solution.py:328
  11.2 1.3 %collective-permute-start.3 = (f32[1,128,128]{2,1,0:T(8,128)S(1)}, f32[1,128,128]{2,1,0:T(8,128)S(1)}, u32[]{:S(2)}, u32[]{:S(2)}) collective-permute-start(f32[1,128,128]{2,1,0:T(8,128)S(1)} %collective-permute-done.refs_2_), channel_id=1, source_target_pairs={{0,1},{1,0},{2,3},{3,2},{4,5},{5,4},{6,7},{7,6},{8,9},{9,8},{10,11... | collective-permute-start | bytes 196616 | tf_op jit(solution)/shard_map/ppermute | solution.py:319

commit v7 on v6

v7 whole, which is shorter than its diff:
```python
import jax
import jax.numpy as jnp
from jax import lax
from jax.experimental import pallas as pl
from jax.experimental.pallas import tpu as pltpu
from jax.sharding import PartitionSpec as P

F32 = jnp.float32
BF16 = jnp.bfloat16
LANES = 128
VMEM = pl.BlockSpec(memory_space=pltpu.VMEM)
HBM = pl.BlockSpec(memory_space=pltpu.HBM)
ANY = pl.BlockSpec(memory_space=pl.ANY)
LEAN = pltpu.CompilerParams(vmem_limit_bytes=8 << 20)


def split(a):
    high = a.astype(BF16)
    return high, (a - high.astype(F32)).astype(BF16)


def dot(a, b, over):
    return lax.dot_general(a, b, (((over,), (0,)), ((), ())), preferred_element_type=F32)


def product(a, b, over=1):
    (ah, al), (bh, bl) = a, b
    if ah.shape[over] > LANES:
        both = dot(jnp.concatenate([ah, al], 1 - over), bh, over)
        rows = ah.shape[1 - over]
        return both[:rows] + (both[rows:] + dot(ah, bl, over))
    return dot(jnp.concatenate([ah, al], over), jnp.concatenate([bh, bh], 0), over) + dot(ah, bl, over)


def pick(kinds, step, pieces):
    value = pieces[0]
    for at, piece in enumerate(pieces[1:], 1):
        mask = jnp.broadcast_to(kinds[step : step + 1, :], value.shape) == at
        value = jnp.where(mask, piece, value)
    return value


def shape(*dims, dtype=F32):
    return pltpu.VMEM(dims, dtype)


def near(*values, space=pltpu.VMEM):
    return [pltpu.with_memory_space_constraint(value, space) for value in values]


def vmem_call(body, outs, name, *args):
    return pl.pallas_call(
        body,
        out_shape=outs,
        in_specs=[VMEM] * len(args),
        out_specs=[VMEM] * len(outs),
        name=name,
        compiler_params=LEAN,
    )(*near(*args))


def load(vectors, reflectors, tfactors, plan, columns):
    held, count, lanes = tfactors.shape[:3]
    groups = plan.shape[0]

    def body(plan, x, v, f, kinds_ref, f_out, end_out, plan_ref, sem):
        copies = [(plan, plan_ref), (f.at[:, count - 1], end_out), (f, f_out)]
        copies = [pltpu.make_async_copy(*pair, sem.at[at]) for at, pair in enumerate(copies)]
        for copy in copies:
            copy.start()
        me = lax.axis_index("col")
        kinds_ref[...] = jnp.zeros_like(kinds_ref)
        copies[0].wait()
        for step in range(groups):
            group = plan_ref[step]
            piece = (me + columns - group // held) % columns * held + group % held
            kinds_ref[step : step + 1, :] = jnp.full((1, lanes), piece, jnp.int32)
        for copy in copies[1:]:
            copy.wait()

    return pl.pallas_call(
        body,
        out_shape=[
            shape(-(-groups // 8) * 8, lanes, dtype=jnp.int32),
            shape(*tfactors.shape),
            shape(held, lanes, lanes),
        ],
        in_specs=[HBM] * 4,
        out_specs=[VMEM] * 3,
        scratch_shapes=[pltpu.SMEM((groups,), jnp.int32), pltpu.SemaphoreType.DMA((3,))],
        name="load",
        compiler_params=LEAN,
    )(*near(plan, vectors, reflectors, tfactors, space=pltpu.HBM))


def is_top(odd_round):
    return (lax.axis_index("row") % 2 == 1) != odd_round


def ordered(top, low):
    first = is_top(False)
    return jnp.where(first, top, low), jnp.where(first, low, top)


def apart(pieces):
    return [piece.at[slot] for piece in pieces for slot in range(piece.shape[0])]


def edge(x, refls, factors, kinds, step, odd_round):
    width, strip = x.shape[1], refls[0].shape[2]
    block = 2 * strip
    count = factors[0].shape[1]
    n = len(refls)

    def body(kinds_ref, x_ref, *refs):
        refl_refs, factor_refs = apart(refs[:n]), apart(refs[n : 2 * n])
        coeff_ref, proj_ref = refs[-2:]

        def work(at, outer):
            start = at * block
            rows, side = slice(start, start + block), slice(start + outer, start + outer + strip)
            first = split(pick(kinds_ref, step, [r[rows, :] for r in refl_refs]))
            second = split(pick(kinds_ref, step + 1, [r[side, :] for r in refl_refs]))
            high, low = split(x_ref[rows, :])
            cross = product(second, [v[outer : outer + strip] for v in first], over=0)
            blank = jnp.zeros((strip, strip), BF16)
            second = [jnp.concatenate([v, blank] if outer == 0 else [blank, v], 0) for v in second]
            all_high = dot(jnp.concatenate([*first, *second], 1), high, 0)
            all_low = dot(jnp.concatenate([first[0], second[0]], 1), low, 0)
            factor = pick(kinds_ref, step, [r[at] for r in factor_refs])
            weight = product(split(cross), split(factor))
            parts = [all_high[i * strip : (i + 1) * strip] for i in range(4)]
            coeff = parts[0] + (parts[1] + all_low[:strip])
            coeff_ref[...] = coeff
            rest = product(split(weight), split(coeff))
            proj_ref[...] = parts[2] + (parts[3] + all_low[strip:]) - rest

        top = is_top(odd_round)
        pl.when(top)(lambda: work(0, 0))
        pl.when(jnp.logical_not(top))(lambda: work(count - 1, strip))

    args = (kinds, x, *refls, *factors)
    return vmem_call(body, [shape(strip, width)] * 2, "edge", *args)


def middle(x, refls, factors, kinds, step, coeffs):
    height, width = x.shape
    strip = refls[0].shape[2]
    block = 2 * strip
    count = height // block
    n = len(refls)

    def body(kinds_ref, x_ref, even_coeff, odd_coeff, *refs):
        refl_refs, factor_refs = apart(refs[:n]), apart(refs[n : 2 * n])
        work_ref, top_ref, low_ref, coeff_ref = refs[2 * n :]
        coeff_ref[0], coeff_ref[count - 1] = ordered(even_coeff[...], odd_coeff[...])

        def run(step, source, blocks, offset, known):
            def rows(at):
                return slice(at * block + offset, (at + 1) * block + offset)

            def refl(at):
                return split(pick(kinds_ref, step, [r[rows(at), :] for r in refl_refs]))

            for at in blocks:
                if at not in known:
                    coeff_ref[at] = product(refl(at), split(source[rows(at), :]), over=0)
            for at in blocks:
                factor = split(pick(kinds_ref, step, [r[at] for r in factor_refs]))
                coeff_ref[at] = product(factor, split(coeff_ref[at]))
            for at in blocks:
                change = product(refl(at), split(coeff_ref[at]))
                work_ref[rows(at), :] = source[rows(at), :] - change

        run(step, x_ref, range(count), 0, (0, count - 1))
        top_ref[...] = work_ref[:strip, :]
        low_ref[...] = work_ref[height - strip :, :]
        run(step + 1, work_ref, range(count - 1), strip, ())

    args = near(kinds, x, *coeffs, *refls, *factors)
    return pl.pallas_call(
        body,
        out_shape=[shape(height, width)] + [shape(strip, width)] * 2,
        in_specs=[VMEM] * len(args),
        out_specs=[VMEM] * 3,
        scratch_shapes=[pltpu.VMEM((count, strip, width), F32)],
        name="middle",
        compiler_params=LEAN,
    )(*args)


def store(work, strip):
    height, width = work.shape

    def body(work_ref, out_ref, sem):
        inner = pl.ds(strip, height - 2 * strip)
        copy = pltpu.make_async_copy(work_ref.at[inner, :], out_ref.at[inner, :], sem)
        copy.start()
        copy.wait()

    return pl.pallas_call(
        body,
        out_shape=jax.ShapeDtypeStruct((height, width), F32),
        in_specs=[VMEM],
        out_specs=ANY,
        scratch_shapes=[pltpu.SemaphoreType.DMA],
        name="store",
        compiler_params=LEAN,
    )(*near(work))


def prepare(refls, factors, behind, kinds, step, strips, projs):
    strip, width = strips[0].shape
    height, count = refls[0].shape[1], factors[0].shape[1]
    n = len(refls)

    def body(kinds_ref, top_ref, low_ref, even_ref, odd_ref, *refs):
        refl_refs, factor_refs = apart(refs[:n]), apart(refs[n : 2 * n])
        behind_refs, refs = apart(refs[2 * n : 3 * n]), refs[3 * n :]
        rests, highs, lows = refs[:2], refs[2:4], refs[4:]
        row, last = lax.axis_index("row"), lax.axis_size("row") - 1
        projs = ordered(even_ref[...], odd_ref[...])

        def weight(start, ends, present):
            refl = pick(kinds_ref, step + 1, [r[start : start + strip, :] for r in refl_refs])
            value = product(split(refl), split(pick(kinds_ref, step + 1, ends)))
            return jnp.where(present, value, jnp.zeros_like(value))

        top = weight(0, [r[...] for r in behind_refs], row > 0)
        low = weight(height - strip, [r[count - 1] for r in factor_refs], row < last)
        even, odd = ordered(top, low)
        highs[0][...], lows[0][...] = split(even)
        highs[1][...], lows[1][...] = split(odd)
        top = top_ref[...] - product(split(top), split(projs[0]))
        low = low_ref[...] - product(split(low), split(projs[1]))
        rests[0][...], rests[1][...] = ordered(top, low)

    rest, half = shape(strip, width), shape(strip, strip, dtype=BF16)
    return vmem_call(
        body,
        [rest, rest, half, half, half, half],
        "prepare",
        *(kinds, *strips, *projs, *refls, *factors, *behind),
    )


def finish(out, prepared, gots):
    height, width = out.shape
    strip = gots[0].shape[0]

    def body(*refs):
        rests, highs, lows, gots = refs[:2], refs[2:4], refs[4:6], refs[6:8]
        out_ref, new_ref, sem = refs[9:]
        row, last = lax.axis_index("row"), lax.axis_size("row") - 1
        copies = []
        for at in range(2):
            top = is_top(at == 1)
            present = jnp.where(top, row > 0, row < last)
            other = jnp.where(present, gots[at][...], jnp.zeros_like(gots[at]))
            weight = highs[at][...], lows[at][...]
            new_ref[at] = rests[at][...] - product(weight, split(other))
            start = pl.multiple_of(jnp.where(top, 0, height - strip), strip)
            rows = out_ref.at[pl.ds(start, strip), :]
            copies.append(pltpu.make_async_copy(new_ref.at[at], rows, sem.at[at]))
            copies[-1].start()
        for copy in copies:
            copy.wait()

    return pl.pallas_call(
        body,
        out_shape=jax.ShapeDtypeStruct((height, width), F32),
        in_specs=[VMEM] * 8 + [ANY],
        out_specs=ANY,
        scratch_shapes=[pltpu.VMEM((2, strip, width), F32), pltpu.SemaphoreType.DMA((2,))],
        input_output_aliases={8: 0},
        name="finish",
        compiler_params=LEAN,
    )(*near(*prepared, *gots), out)


def local(vectors, reflectors, tfactors, plan):
    groups, strip = plan.shape[0], reflectors.shape[2]
    rows, columns = lax.axis_size("row"), lax.axis_size("col")

    def around(block, shift):
        return lax.ppermute(block, "col", [(c, (c + shift) % columns) for c in range(columns)])

    def trade(block, odd_round):
        route = []
        for row in range(rows):
            for col in range(columns):
                there = row + 1 if (row % 2 == 1) == odd_round else row - 1
                there = (there, col) if 0 <= there < rows else (row, (col + 1) % columns)
                route.append((row * columns + col, there[0] * columns + there[1]))
        return lax.ppermute(block, ("row", "col"), route)

    def everyone(mine, sent):
        return [mine, *(around(sent, shift) for shift in range(1, columns))]

    kinds, factor, end = load(vectors, reflectors, tfactors, plan, columns)
    refls, factors = everyone(reflectors, reflectors), everyone(factor, tfactors)
    behind = lax.ppermute(end, "row", [(r, (r + 1) % rows) for r in range(rows)])
    current, behinds = vectors, None
    for step in range(0, groups, 2):
        coeffs, projs, gots = [], [], []
        for odd_round in (False, True):
            coeff, proj = edge(current, refls, factors, kinds, step, odd_round)
            coeffs.append(coeff)
            projs.append(proj)
            gots.append(trade(proj, odd_round))
        work, *strips = middle(current, refls, factors, kinds, step, coeffs)
        if behinds is None:
            behind, strips[0] = lax.optimization_barrier((behind, strips[0]))
            behinds = everyone(behind, behind)
        out = store(work, strip)
        prepared = prepare(refls, factors, behinds, kinds, step, strips, projs)
        current = finish(out, prepared, gots)
    return current


def solution(mesh):
    return jax.shard_map(
        local,
        mesh=mesh,
        in_specs=(P("row", "col"), P("col", "row", None), P("col", "row", None, None), P()),
        out_specs=P("row", "col"),
        check_vma=False,
    )
```

time: 14.1 us -> 13.8 us (0.979); the launches traced: 13.8 us -> 13.7 us
  Pallas kernels: 7.74 us -> 6.05 us
  waiting for transfers between devices: 0.75 us -> 2.37 us
    ppermute x1, waiting for transfers between devices: 0.47 us -> 2.01 us  [local(): lax.ppermute(end, 'row', [(r, (r + 1) % rows) for r in range(rows)])]
    pallas_call x1, Pallas kernels: 3.02 us -> 1.65 us  [middle(): pl.pallas_call(body, out_shape=[shape(height, width)] + [shape(strip, wid...]
    pallas_call x1, Pallas kernels: 1.27 us -> 1.06 us  [load(): pl.pallas_call(body, out_shape=[shape(-(-groups // 8) * 8, lanes, dtype=j...]
  transfers between devices with their start and end apart: 6 -> 6, of which waited for: 2 -> 2; matrix products, arithmetic and copies ran while one was open for 0% -> 0% of each run, Pallas kernels for 49% -> 37%
where the time goes in v7:
time: 13.8 us; the launch traced here: 13.7 us
  Pallas kernels  6.05 us (44%)
  starting transfers between devices  5.16 us (37%)
  waiting for transfers between devices  2.37 us (17%)
    ppermute x1, starting transfers between devices, local(): lax.ppermute(end, 'row', [(r, (r + 1) % rows) for r in range(rows)])  2.96 us
    ppermute x1, waiting for transfers between devices, local(): lax.ppermute(end, 'row', [(r, (r + 1) % rows) for r in range(rows)])  2.01 us
    pallas_call x1, Pallas kernels, middle(): pl.pallas_call(body, out_shape=[shape(height, width)] + [shape(strip, wid...  1.65 us
    ppermute x2, starting transfers between devices, trade(): return lax.ppermute(block, ('row', 'col'), route)  1.63 us
    pallas_call x3, Pallas kernels, vmem_call(): pl.pallas_call(body, out_shape=outs, in_specs=[VMEM] * len(args), out_spe...  1.47 us
    pallas_call x1, Pallas kernels, load(): pl.pallas_call(body, out_shape=[shape(-(-groups // 8) * 8, lanes, dtype=j...  1.06 us
    pallas_call x1, Pallas kernels, finish(): pl.pallas_call(body, out_shape=jax.ShapeDtypeStruct((height, width), F32)...  0.97 us
    pallas_call x1, Pallas kernels, store(): pl.pallas_call(body, out_shape=jax.ShapeDtypeStruct((height, width), F32)...  0.89 us
  transfers between devices with their start and end apart: 6, of which 2 were waited for; matrix products, arithmetic and copies ran while one was open for 0% of the time, Pallas kernels for 37%

profile of v7, /device:TPU:0, one launch (start us, length us, event | category | flops | bytes accessed | tf_op | source)
XLA Modules:
  0.0 13.7 jit_solution(813032652102015232)
XLA Ops:
  0.0 0.0 copy-start.1
  0.0 0.0 copy-start
  0.0 0.5 %collective-permute-start.1 = (f32[1,1024,128]{2,1,0:T(8,128)}, f32[1,1024,128]{2,1,0:T(8,128)S(1)}, u32[]{:S(2)}, u32[]{:S(2)}) collective-permute-start(f32[1,1024,128]{2,1,0:T(8,128)} %refs_0_.7), channel_id=1, source_target_pairs={{0,1},{1,0},{2,3},{3,2},{4,5},{5,4},{6,7},{7,6},{8,9},{9,8},{10,11... | collective-permute-start | bytes 1572872 | tf_op jit(solution)/shard_map/ppermute | solution.py:286
  0.5 0.1 collective-permute-start.2
  0.6 1.1 %load.1 = (s32[8,128]{1,0:T(8,128)S(1)}, f32[1,4,128,128]{3,2,1,0:T(8,128)S(1)}, f32[1,128,128]{2,1,0:T(8,128)S(1)}) custom-call(s32[2]{0:T(128)} %plan.1, f32[1024,256]{1,0:T(8,128)} %x_ref.5, f32[1,1024,128]{2,1,0:T(8,128)} %refs_0_.7, f32[1,4,128,128]{3,2,1,0:T(8,128)} %f.1), custom_call_target="tpu_custom_call" | custom-call | tf_op jit(solution)/shard_map/load/pallas_call | solution.py:81
  1.6 3.0 %collective-permute-start = (f32[1,128,128]{2,1,0:T(8,128)S(1)}, f32[1,128,128]{2,1,0:T(8,128)S(1)}, u32[]{:S(2)}, u32[]{:S(2)}) collective-permute-start(f32[1,128,128]{2,1,0:T(8,128)S(1)} %get-tuple-element.24), channel_id=1, source_target_pairs={{0,2},{2,4},{4,6},{6,8},{8,10},{10,12},{12,14},{14,16},{16,18},{18... | collective-permute-start | bytes 196616 | tf_op jit(solution)/shard_map/ppermute | solution.py:302
  4.6 0.0 collective-permute-done.2.refs_3_
  4.6 0.0 collective-permute-done.1.refs_1_
  4.6 0.0 copy-done.1
  4.6 0.0 copy-done
  4.6 0.6 %edge.2 = (f32[128,256]{1,0:T(8,128)S(1)}, f32[128,256]{1,0:T(8,128)S(1)}) custom-call(s32[8,128]{1,0:T(8,128)S(1)} %get-tuple-element.23.kinds_ref, f32[1024,256]{1,0:T(8,128)S(1)} %copy-done, f32[1,1024,128]{2,1,0:T(8,128)S(1)} %copy-done.1, f32[1,1024,128]{2,1,0:T(8,128)S(1)} %collective-permute-done.1.refs_1_, ...), custom_call_target="tpu_custom_call" | custom-call | tf_op jit(solution)/shard_map/edge/pallas_call | solution.py:52
  5.2 1.6 %collective-permute-start.4 = (f32[128,256]{1,0:T(8,128)S(1)}, f32[128,256]{1,0:T(8,128)S(1)}, u32[]{:S(2)}, u32[]{:S(2)}) collective-permute-start(f32[128,256]{1,0:T(8,128)S(1)} %get-tuple-element.31.even_ref), channel_id=1, source_target_pairs={{0,2},{1,3},{2,0},{3,1},{4,6},{5,7},{6,4},{7,5},{8,10},{9,11},{10,... | collective-permute-start | bytes 393224 | tf_op jit(solution)/shard_map/ppermute | solution.py:295
  6.7 0.5 %edge.3 = (f32[128,256]{1,0:T(8,128)S(1)}, f32[128,256]{1,0:T(8,128)S(1)}) custom-call(s32[8,128]{1,0:T(8,128)S(1)} %get-tuple-element.23.kinds_ref, f32[1024,256]{1,0:T(8,128)S(1)} %copy-done, f32[1,1024,128]{2,1,0:T(8,128)S(1)} %copy-done.1, f32[1,1024,128]{2,1,0:T(8,128)S(1)} %collective-permute-done.1.refs_1_, ...), custom_call_target="tpu_custom_call" | custom-call | tf_op jit(solution)/shard_map/edge/pallas_call | solution.py:52
  7.3 0.1 collective-permute-start.5
  7.4 1.7 %middle.1 = (f32[1024,256]{1,0:T(8,128)S(1)}, f32[128,256]{1,0:T(8,128)S(1)}, f32[128,256]{1,0:T(8,128)S(1)}) custom-call(s32[8,128]{1,0:T(8,128)S(1)} %get-tuple-element.23.kinds_ref, f32[1024,256]{1,0:T(8,128)S(1)} %copy-done, f32[128,256]{1,0:T(8,128)S(1)} %get-tuple-element.26.even_coeff, f32[128,256]{1,0:T(8,128)S(1)} %get-tuple-element.27.odd_coeff, ...), custom_call_target="tpu_custom_call" | custom-call | tf_op jit(solution)/shard_map/middle/pallas_call | solution.py:181
  9.0 2.0 %collective-permute-done.refs_4_ = f32[1,128,128]{2,1,0:T(8,128)S(1)} collective-permute-done((f32[1,128,128]{2,1,0:T(8,128)S(1)}, f32[1,128,128]{2,1,0:T(8,128)S(1)}, u32[]{:S(2)}, u32[]{:S(2)}) %collective-permute-start) | collective-permute-done | bytes 65568 | tf_op jit(solution)/shard_map/ppermute | solution.py:302
  11.0 0.0 collective-permute-start.3
  11.0 0.9 %store.1.refs_8_ = f32[1024,256]{1,0:T(8,128)} custom-call(f32[1024,256]{1,0:T(8,128)S(1)} %get-tuple-element.40.work_ref), custom_call_target="tpu_custom_call" | custom-call | tf_op jit(solution)/shard_map/store/pallas_call | solution.py:201
  11.9 0.4 %collective-permute-done.3.refs_5_ = f32[1,128,128]{2,1,0:T(8,128)S(1)} collective-permute-done((f32[1,128,128]{2,1,0:T(8,128)S(1)}, f32[1,128,128]{2,1,0:T(8,128)S(1)}, u32[]{:S(2)}, u32[]{:S(2)}) %collective-permute-start.3) | collective-permute-done | bytes 65568 | tf_op jit(solution)/shard_map/ppermute | solution.py:286
  12.3 0.4 %prepare.1 = (f32[128,256]{1,0:T(8,128)S(1)}, f32[128,256]{1,0:T(8,128)S(1)}, bf16[128,128]{1,0:T(8,128)(2,1)S(1)}, bf16[128,128]{1,0:T(8,128)(2,1)S(1)}, bf16[1...) custom-call(s32[8,128]{1,0:T(8,128)S(1)} %get-tuple-element.23.kinds_ref, f32[128,256]{1,0:T(8,128)S(1)} %get-tuple-element.29.top_ref, ...), custom_call_target="tpu_custom_call" | custom-call | tf_op jit(solution)/shard_map/prepare/pallas_call | solution.py:52
  12.7 0.0 collective-permute-done.4.refs_6_
  12.7 0.0 collective-permute-done.5.refs_7_
  12.7 1.0 %finish.1 = f32[1024,256]{1,0:T(8,128)} custom-call(f32[128,256]{1,0:T(8,128)S(1)} %get-tuple-element.34.refs_0_, f32[128,256]{1,0:T(8,128)S(1)} %get-tuple-element.35.refs_1_, bf16[128,128]{1,0:T(8,128)(2,1)S(1)} %get-tuple-element.36.refs_2_, bf16[128,128]{1,0:T(8,128)(2,1)S(1)} %get-tuple-element.37.refs_3_, ...), custom_call_target="tpu_custom_call", output_to_operand_aliasing={{}: (8, {})} | custom-call | tf_op jit(solution)/shard_map/finish/pallas_call | solution.py:269
Async XLA Ops:
  0.0 4.6 %copy-start.1 = (f32[1,1024,128]{2,1,0:T(8,128)S(1)}, f32[1,1024,128]{2,1,0:T(8,128)}, u32[]{:S(2)}) copy-start(f32[1,1024,128]{2,1,0:T(8,128)} %refs_0_.7) | copy-start | bytes 1572868
  0.0 4.6 %copy-start = (f32[1024,256]{1,0:T(8,128)S(1)}, f32[1024,256]{1,0:T(8,128)}, u32[]{:S(2)}) copy-start(f32[1024,256]{1,0:T(8,128)} %x_ref.5) | copy-start | bytes 3145732
  0.0 4.6 %collective-permute-start.1 = (f32[1,1024,128]{2,1,0:T(8,128)}, f32[1,1024,128]{2,1,0:T(8,128)S(1)}, u32[]{:S(2)}, u32[]{:S(2)}) collective-permute-start(f32[1,1024,128]{2,1,0:T(8,128)} %refs_0_.7), channel_id=1, source_target_pairs={{0,1},{1,0},{2,3},{3,2},{4,5},{5,4},{6,7},{7,6},{8,9},{9,8},{10,11... | collective-permute-start | bytes 1572872 | tf_op jit(solution)/shard_map/ppermute | solution.py:286
  0.5 4.1 %collective-permute-start.2 = (f32[1,4,128,128]{3,2,1,0:T(8,128)}, f32[1,4,128,128]{3,2,1,0:T(8,128)S(1)}, u32[]{:S(2)}, u32[]{:S(2)}) collective-permute-start(f32[1,4,128,128]{3,2,1,0:T(8,128)} %f.1), channel_id=1, source_target_pairs={{0,1},{1,0},{2,3},{3,2},{4,5},{5,4},{6,7},{7,6},{8,9},{9,8},{10,11... | collective-permute-start | bytes 786440 | tf_op jit(solution)/shard_map/ppermute | solution.py:286
  1.6 9.4 %collective-permute-start = (f32[1,128,128]{2,1,0:T(8,128)S(1)}, f32[1,128,128]{2,1,0:T(8,128)S(1)}, u32[]{:S(2)}, u32[]{:S(2)}) collective-permute-start(f32[1,128,128]{2,1,0:T(8,128)S(1)} %get-tuple-element.24), channel_id=1, source_target_pairs={{0,2},{2,4},{4,6},{6,8},{8,10},{10,12},{12,14},{14,16},{16,18},{18... | collective-permute-start | bytes 196616 | tf_op jit(solution)/shard_map/ppermute | solution.py:302
  5.2 7.5 %collective-permute-start.4 = (f32[128,256]{1,0:T(8,128)S(1)}, f32[128,256]{1,0:T(8,128)S(1)}, u32[]{:S(2)}, u32[]{:S(2)}) collective-permute-start(f32[128,256]{1,0:T(8,128)S(1)} %get-tuple-element.31.even_ref), channel_id=1, source_target_pairs={{0,2},{1,3},{2,0},{3,1},{4,6},{5,7},{6,4},{7,5},{8,10},{9,11},{10,... | collective-permute-start | bytes 393224 | tf_op jit(solution)/shard_map/ppermute | solution.py:295
  7.3 5.4 %collective-permute-start.5 = (f32[128,256]{1,0:T(8,128)S(1)}, f32[128,256]{1,0:T(8,128)S(1)}, u32[]{:S(2)}, u32[]{:S(2)}) collective-permute-start(f32[128,256]{1,0:T(8,128)S(1)} %get-tuple-element.32.odd_ref), channel_id=1, source_target_pairs={{0,1},{1,0},{2,4},{3,5},{4,2},{5,3},{6,8},{7,9},{8,6},{9,7},{10,12... | collective-permute-start | bytes 393224 | tf_op jit(solution)/shard_map/ppermute | solution.py:295
  11.0 1.3 %collective-permute-start.3 = (f32[1,128,128]{2,1,0:T(8,128)S(1)}, f32[1,128,128]{2,1,0:T(8,128)S(1)}, u32[]{:S(2)}, u32[]{:S(2)}) collective-permute-start(f32[1,128,128]{2,1,0:T(8,128)S(1)} %collective-permute-done.refs_4_), channel_id=1, source_target_pairs={{0,1},{1,0},{2,3},{3,2},{4,5},{5,4},{6,7},{7,6},{8,9},{9,8},{10,11... | collective-permute-start | bytes 196616 | tf_op jit(solution)/shard_map/ppermute | solution.py:286

commit v8 on v7

--- a/solution.py
+++ b/solution.py
@@ -59,38 +59,39 @@
     )(*near(*args))
 
 
-def load(vectors, reflectors, tfactors, plan, columns):
+def entry(*arrays):
+    lanes = (8, LANES)
+
+    def body(*refs):
+        refs[-1][...] = jnp.zeros(lanes, F32)
+
+    return pl.pallas_call(
+        body,
+        out_shape=shape(*lanes),
+        in_specs=[HBM] * len(arrays),
+        out_specs=VMEM,
+        name="entry",
+        compiler_params=LEAN,
+    )(*near(*arrays, space=pltpu.HBM))
+
+
+def tables(mark, tfactors, plan, columns):
     held, count, lanes = tfactors.shape[:3]
-    groups = plan.shape[0]
-
-    def body(plan, x, v, f, kinds_ref, f_out, end_out, plan_ref, sem):
-        copies = [(plan, plan_ref), (f.at[:, count - 1], end_out), (f, f_out)]
-        copies = [pltpu.make_async_copy(*pair, sem.at[at]) for at, pair in enumerate(copies)]
-        for copy in copies:
-            copy.start()
+    groups = plan.shape[1]
+
+    def body(_, plan_ref, f_ref, kinds_ref, end_ref):
+        end_ref[...] = f_ref[:, count - 1]
         me = lax.axis_index("col")
         kinds_ref[...] = jnp.zeros_like(kinds_ref)
-        copies[0].wait()
         for step in range(groups):
-            group = plan_ref[step]
-            piece = (me + columns - group // held) % columns * held + group % held
-            kinds_ref[step : step + 1, :] = jnp.full((1, lanes), piece, jnp.int32)
-        for copy in copies[1:]:
-            copy.wait()
-
-    return pl.pallas_call(
-        body,
-        out_shape=[
-            shape(-(-groups // 8) * 8, lanes, dtype=jnp.int32),
-            shape(*tfactors.shape),
-            shape(held, lanes, lanes),
-        ],
-        in_specs=[HBM] * 4,
-        out_specs=[VMEM] * 3,
-        scratch_shapes=[pltpu.SMEM((groups,), jnp.int32), pltpu.SemaphoreType.DMA((3,))],
-        name="load",
-        compiler_params=LEAN,
-    )(*near(plan, vectors, reflectors, tfactors, space=pltpu.HBM))
+            group = jnp.broadcast_to(plan_ref[:, step : step + 1], (1, lanes))
+            home = group // held if held > 1 else group
+            gap = me - home
+            gap = jnp.where(gap < 0, gap + columns, gap)
+            kinds_ref[step : step + 1, :] = gap * held + (group - home * held)
+
+    table = shape(-(-groups // 8) * 8, lanes, dtype=jnp.int32)
+    return vmem_call(body, [table, shape(held, lanes, lanes)], "tables", mark, plan, tfactors)
 
 
 def is_top(odd_round):
@@ -294,11 +295,13 @@
                 route.append((row * columns + col, there[0] * columns + there[1]))
         return lax.ppermute(block, ("row", "col"), route)
 
-    def everyone(mine, sent):
-        return [mine, *(around(sent, shift) for shift in range(1, columns))]
-
-    kinds, factor, end = load(vectors, reflectors, tfactors, plan, columns)
-    refls, factors = everyone(reflectors, reflectors), everyone(factor, tfactors)
+    def everyone(piece):
+        return [piece, *(around(piece, shift) for shift in range(1, columns))]
+
+    refls, factors = everyone(reflectors), everyone(tfactors)
+    plan = plan.reshape(1, groups)
+    mark = entry(plan, vectors, reflectors, tfactors)
+    kinds, end = tables(mark, tfactors, plan, columns)
     behind = lax.ppermute(end, "row", [(r, (r + 1) % rows) for r in range(rows)])
     current, behinds = vectors, None
     for step in range(0, groups, 2):
@@ -311,7 +314,7 @@
         work, *strips = middle(current, refls, factors, kinds, step, coeffs)
         if behinds is None:
             behind, strips[0] = lax.optimization_barrier((behind, strips[0]))
-            behinds = everyone(behind, behind)
+            behinds = everyone(behind)
         out = store(work, strip)
         prepared = prepare(refls, factors, behinds, kinds, step, strips, projs)
         current = finish(out, prepared, gots)

time: 13.8 us -> 13.7 us (level)
  Pallas kernels: 6.05 us -> 5.07 us
  local copies, waits for them, and re-layouts: 0.01 us -> 0.94 us
    pallas_call x1, Pallas kernels: 1.06 us -> 0.01 us  [entry(): pl.pallas_call(body, out_shape=shape(*lanes), in_specs=[HBM] * len(arrays...]
    unnamed x4 -> x8, local copies, waits for them, and re-layouts: 0.01 us -> 0.94 us
    pallas_call x3 -> x4, Pallas kernels: 1.47 us -> 1.55 us  [vmem_call(): pl.pallas_call(body, out_shape=outs, in_specs=[VMEM] * len(args), out_spe...]
  transfers between devices with their start and end apart: 6 -> 6, of which waited for: 2 -> 2; matrix products, arithmetic and copies ran while one was open for 0% -> 0% of each run, Pallas kernels for 37% -> 30%
where the time goes in v8:
time: 13.7 us; the launch traced here: 13.5 us
  starting transfers between devices  5.11 us (37%)
  Pallas kernels  5.07 us (37%)
  waiting for transfers between devices  2.29 us (17%)
  local copies, waits for them, and re-layouts  0.94 us (7%)
    ppermute x1, starting transfers between devices, local(): lax.ppermute(end, 'row', [(r, (r + 1) % rows) for r in range(rows)])  2.97 us
    ppermute x1, waiting for transfers between devices, local(): lax.ppermute(end, 'row', [(r, (r + 1) % rows) for r in range(rows)])  1.92 us
    pallas_call x1, Pallas kernels, middle(): pl.pallas_call(body, out_shape=[shape(height, width)] + [shape(strip, wid...  1.66 us
    ppermute x2, starting transfers between devices, trade(): return lax.ppermute(block, ('row', 'col'), route)  1.63 us
    pallas_call x4, Pallas kernels, vmem_call(): pl.pallas_call(body, out_shape=outs, in_specs=[VMEM] * len(args), out_spe...  1.55 us
    pallas_call x1, Pallas kernels, finish(): pl.pallas_call(body, out_shape=jax.ShapeDtypeStruct((height, width), F32)...  0.97 us
    unnamed x8, local copies, waits for them, and re-layouts  0.94 us
    pallas_call x1, Pallas kernels, store(): pl.pallas_call(body, out_shape=jax.ShapeDtypeStruct((height, width), F32)...  0.89 us
  transfers between devices with their start and end apart: 6, of which 2 were waited for; matrix products, arithmetic and copies ran while one was open for 0% of the time, Pallas kernels for 30%

profile of v8, /device:TPU:0, one launch (start us, length us, event | category | flops | bytes accessed | tf_op | source)
XLA Modules:
  0.0 13.5 jit_solution(721233141900723723)
XLA Ops:
  0.0 0.5 %collective-permute-start.1 = (f32[1,1024,128]{2,1,0:T(8,128)}, f32[1,1024,128]{2,1,0:T(8,128)S(1)}, u32[]{:S(2)}, u32[]{:S(2)}) collective-permute-start(f32[1,1024,128]{2,1,0:T(8,128)} %refs_0_.7), channel_id=1, source_target_pairs={{0,1},{1,0},{2,3},{3,2},{4,5},{5,4},{6,7},{7,6},{8,9},{9,8},{10,11... | collective-permute-start | bytes 1572872 | tf_op jit(solution)/shard_map/ppermute | solution.py:287
  0.5 0.0 collective-permute-start.2
  0.5 0.0 copy-start.2
  0.5 0.9 %copy-done.2 = f32[1,4,128,128]{3,2,1,0:T(8,128)S(1)} copy-done((f32[1,4,128,128]{3,2,1,0:T(8,128)S(1)}, f32[1,4,128,128]{3,2,1,0:T(8,128)}, u32[]{:S(2)}) %copy-start.2) | copy-done | bytes 262168
  1.5 0.0 copy-done.3
  1.5 0.1 tables.1
  1.5 3.0 %collective-permute-start = (f32[1,128,128]{2,1,0:T(8,128)S(1)}, f32[1,128,128]{2,1,0:T(8,128)S(1)}, u32[]{:S(2)}, u32[]{:S(2)}) collective-permute-start(f32[1,128,128]{2,1,0:T(8,128)S(1)} %get-tuple-element.23), channel_id=1, source_target_pairs={{0,2},{2,4},{4,6},{6,8},{8,10},{10,12},{12,14},{14,16},{16,18},{18... | collective-permute-start | bytes 196616 | tf_op jit(solution)/shard_map/ppermute | solution.py:305
  4.5 0.0 collective-permute-done.2.refs_3_
  4.5 0.0 collective-permute-done.1.refs_1_
  4.5 0.0 copy-done
  4.5 0.0 copy-done.1
  4.5 0.6 %edge.2 = (f32[128,256]{1,0:T(8,128)S(1)}, f32[128,256]{1,0:T(8,128)S(1)}) custom-call(s32[8,128]{1,0:T(8,128)S(1)} %get-tuple-element.22.kinds_ref, f32[1024,256]{1,0:T(8,128)S(1)} %copy-done, f32[1,1024,128]{2,1,0:T(8,128)S(1)} %copy-done.1, f32[1,1024,128]{2,1,0:T(8,128)S(1)} %collective-permute-done.1.refs_1_, f32[1,4,128,128]{3,2,1,0:T(8,128)S(1)} %copy-done.2, ...), custom_call_target="tpu_custom_call" | custom-call | tf_op jit(solution)/shard_map/edge/pallas_call | solution.py:52
  5.1 1.6 %collective-permute-start.4 = (f32[128,256]{1,0:T(8,128)S(1)}, f32[128,256]{1,0:T(8,128)S(1)}, u32[]{:S(2)}, u32[]{:S(2)}) collective-permute-start(f32[128,256]{1,0:T(8,128)S(1)} %get-tuple-element.29.even_ref), channel_id=1, source_target_pairs={{0,2},{1,3},{2,0},{3,1},{4,6},{5,7},{6,4},{7,5},{8,10},{9,11},{10,... | collective-permute-start | bytes 393224 | tf_op jit(solution)/shard_map/ppermute | solution.py:296
  6.6 0.5 %edge.3 = (f32[128,256]{1,0:T(8,128)S(1)}, f32[128,256]{1,0:T(8,128)S(1)}) custom-call(s32[8,128]{1,0:T(8,128)S(1)} %get-tuple-element.22.kinds_ref, f32[1024,256]{1,0:T(8,128)S(1)} %copy-done, f32[1,1024,128]{2,1,0:T(8,128)S(1)} %copy-done.1, f32[1,1024,128]{2,1,0:T(8,128)S(1)} %collective-permute-done.1.refs_1_, f32[1,4,128,128]{3,2,1,0:T(8,128)S(1)} %copy-done.2, ...), custom_call_target="tpu_custom_call" | custom-call | tf_op jit(solution)/shard_map/edge/pallas_call | solution.py:52
  7.2 0.1 collective-permute-start.5
  7.3 1.7 %middle.1 = (f32[1024,256]{1,0:T(8,128)S(1)}, f32[128,256]{1,0:T(8,128)S(1)}, f32[128,256]{1,0:T(8,128)S(1)}) custom-call(s32[8,128]{1,0:T(8,128)S(1)} %get-tuple-element.22.kinds_ref, f32[1024,256]{1,0:T(8,128)S(1)} %copy-done, f32[128,256]{1,0:T(8,128)S(1)} %get-tuple-element.24.even_coeff, f32[128,256]{1,0:T(8,128)S(1)} %get-tuple-element.25.odd_coeff, ...), custom_call_target="tpu_custom_call" | custom-call | tf_op jit(solution)/shard_map/middle/pallas_call | solution.py:182
  8.9 1.9 %collective-permute-done.refs_4_ = f32[1,128,128]{2,1,0:T(8,128)S(1)} collective-permute-done((f32[1,128,128]{2,1,0:T(8,128)S(1)}, f32[1,128,128]{2,1,0:T(8,128)S(1)}, u32[]{:S(2)}, u32[]{:S(2)}) %collective-permute-start) | collective-permute-done | bytes 65568 | tf_op jit(solution)/shard_map/ppermute | solution.py:305
  10.9 0.0 collective-permute-start.3
  10.9 0.9 %store.1.refs_8_ = f32[1024,256]{1,0:T(8,128)} custom-call(f32[1024,256]{1,0:T(8,128)S(1)} %get-tuple-element.38.work_ref), custom_call_target="tpu_custom_call" | custom-call | tf_op jit(solution)/shard_map/store/pallas_call | solution.py:202
  11.8 0.4 %collective-permute-done.3.refs_5_ = f32[1,128,128]{2,1,0:T(8,128)S(1)} collective-permute-done((f32[1,128,128]{2,1,0:T(8,128)S(1)}, f32[1,128,128]{2,1,0:T(8,128)S(1)}, u32[]{:S(2)}, u32[]{:S(2)}) %collective-permute-start.3) | collective-permute-done | bytes 65568 | tf_op jit(solution)/shard_map/ppermute | solution.py:287
  12.1 0.4 %prepare.1 = (f32[128,256]{1,0:T(8,128)S(1)}, f32[128,256]{1,0:T(8,128)S(1)}, bf16[128,128]{1,0:T(8,128)(2,1)S(1)}, bf16[128,128]{1,0:T(8,128)(2,1)S(1)}, bf16[1...) custom-call(s32[8,128]{1,0:T(8,128)S(1)} %get-tuple-element.22.kinds_ref, f32[128,256]{1,0:T(8,128)S(1)} %get-tuple-element.27.top_ref, ...), custom_call_target="tpu_custom_call" | custom-call | tf_op jit(solution)/shard_map/prepare/pallas_call | solution.py:52
  12.5 0.0 collective-permute-done.4.refs_6_
  12.5 0.0 collective-permute-done.5.refs_7_
  12.5 1.0 %finish.1 = f32[1024,256]{1,0:T(8,128)} custom-call(f32[128,256]{1,0:T(8,128)S(1)} %get-tuple-element.32.refs_0_, f32[128,256]{1,0:T(8,128)S(1)} %get-tuple-element.33.refs_1_, bf16[128,128]{1,0:T(8,128)(2,1)S(1)} %get-tuple-element.34.refs_2_, bf16[128,128]{1,0:T(8,128)(2,1)S(1)} %get-tuple-element.35.refs_3_, ...), custom_call_target="tpu_custom_call", output_to_operand_aliasing={{}: (8, {})} | custom-call | tf_op jit(solution)/shard_map/finish/pallas_call | solution.py:270
  (4 shorter events, 0.0 us)
Async XLA Ops:
  0.0 4.5 %collective-permute-start.1 = (f32[1,1024,128]{2,1,0:T(8,128)}, f32[1,1024,128]{2,1,0:T(8,128)S(1)}, u32[]{:S(2)}, u32[]{:S(2)}) collective-permute-start(f32[1,1024,128]{2,1,0:T(8,128)} %refs_0_.7), channel_id=1, source_target_pairs={{0,1},{1,0},{2,3},{3,2},{4,5},{5,4},{6,7},{7,6},{8,9},{9,8},{10,11... | collective-permute-start | bytes 1572872 | tf_op jit(solution)/shard_map/ppermute | solution.py:287
  0.5 4.0 %collective-permute-start.2 = (f32[1,4,128,128]{3,2,1,0:T(8,128)}, f32[1,4,128,128]{3,2,1,0:T(8,128)S(1)}, u32[]{:S(2)}, u32[]{:S(2)}) collective-permute-start(f32[1,4,128,128]{3,2,1,0:T(8,128)} %refs_2_.9), channel_id=1, source_target_pairs={{0,1},{1,0},{2,3},{3,2},{4,5},{5,4},{6,7},{7,6},{8,9},{9,8},{10,11... | collective-permute-start | bytes 786440 | tf_op jit(solution)/shard_map/ppermute | solution.py:287
  0.5 0.9 %copy-start.2 = (f32[1,4,128,128]{3,2,1,0:T(8,128)S(1)}, f32[1,4,128,128]{3,2,1,0:T(8,128)}, u32[]{:S(2)}) copy-start(f32[1,4,128,128]{3,2,1,0:T(8,128)} %refs_2_.9) | copy-start | bytes 786436
  0.5 1.0 %copy-start.3 = (s32[2]{0:T(128)S(1)}, s32[2]{0:T(128)}, u32[]{:S(2)}) copy-start(s32[2]{0:T(128)} %param.7) | copy-start | bytes 28
  0.5 4.0 %copy-start = (f32[1024,256]{1,0:T(8,128)S(1)}, f32[1024,256]{1,0:T(8,128)}, u32[]{:S(2)}) copy-start(f32[1024,256]{1,0:T(8,128)} %x_ref.5) | copy-start | bytes 3145732
  0.5 4.0 %copy-start.1 = (f32[1,1024,128]{2,1,0:T(8,128)S(1)}, f32[1,1024,128]{2,1,0:T(8,128)}, u32[]{:S(2)}) copy-start(f32[1,1024,128]{2,1,0:T(8,128)} %refs_0_.7) | copy-start | bytes 1572868
  1.5 9.3 %collective-permute-start = (f32[1,128,128]{2,1,0:T(8,128)S(1)}, f32[1,128,128]{2,1,0:T(8,128)S(1)}, u32[]{:S(2)}, u32[]{:S(2)}) collective-permute-start(f32[1,128,128]{2,1,0:T(8,128)S(1)} %get-tuple-element.23), channel_id=1, source_target_pairs={{0,2},{2,4},{4,6},{6,8},{8,10},{10,12},{12,14},{14,16},{16,18},{18... | collective-permute-start | bytes 196616 | tf_op jit(solution)/shard_map/ppermute | solution.py:305
  5.1 7.4 %collective-permute-start.4 = (f32[128,256]{1,0:T(8,128)S(1)}, f32[128,256]{1,0:T(8,128)S(1)}, u32[]{:S(2)}, u32[]{:S(2)}) collective-permute-start(f32[128,256]{1,0:T(8,128)S(1)} %get-tuple-element.29.even_ref), channel_id=1, source_target_pairs={{0,2},{1,3},{2,0},{3,1},{4,6},{5,7},{6,4},{7,5},{8,10},{9,11},{10,... | collective-permute-start | bytes 393224 | tf_op jit(solution)/shard_map/ppermute | solution.py:296
  7.2 5.3 %collective-permute-start.5 = (f32[128,256]{1,0:T(8,128)S(1)}, f32[128,256]{1,0:T(8,128)S(1)}, u32[]{:S(2)}, u32[]{:S(2)}) collective-permute-start(f32[128,256]{1,0:T(8,128)S(1)} %get-tuple-element.30.odd_ref), channel_id=1, source_target_pairs={{0,1},{1,0},{2,4},{3,5},{4,2},{5,3},{6,8},{7,9},{8,6},{9,7},{10,12... | collective-permute-start | bytes 393224 | tf_op jit(solution)/shard_map/ppermute | solution.py:296
  10.9 1.3 %collective-permute-start.3 = (f32[1,128,128]{2,1,0:T(8,128)S(1)}, f32[1,128,128]{2,1,0:T(8,128)S(1)}, u32[]{:S(2)}, u32[]{:S(2)}) collective-permute-start(f32[1,128,128]{2,1,0:T(8,128)S(1)} %collective-permute-done.refs_4_), channel_id=1, source_target_pairs={{0,1},{1,0},{2,3},{3,2},{4,5},{5,4},{6,7},{7,6},{8,9},{9,8},{10,11... | collective-permute-start | bytes 196616 | tf_op jit(solution)/shard_map/ppermute | solution.py:287

commit v9 on v8

--- a/solution.py
+++ b/solution.py
@@ -295,12 +295,13 @@
                 route.append((row * columns + col, there[0] * columns + there[1]))
         return lax.ppermute(block, ("row", "col"), route)
 
-    def everyone(piece):
-        return [piece, *(around(piece, shift) for shift in range(1, columns))]
-
-    refls, factors = everyone(reflectors), everyone(tfactors)
+    def everyone(piece, sent):
+        return [piece, *(around(sent, shift) for shift in range(1, columns))]
+
     plan = plan.reshape(1, groups)
     mark = entry(plan, vectors, reflectors, tfactors)
+    later, mark = lax.optimization_barrier((tfactors, mark))
+    refls, factors = everyone(reflectors, reflectors), everyone(tfactors, later)
     kinds, end = tables(mark, tfactors, plan, columns)
     behind = lax.ppermute(end, "row", [(r, (r + 1) % rows) for r in range(rows)])
     current, behinds = vectors, None
@@ -314,7 +315,7 @@
         work, *strips = middle(current, refls, factors, kinds, step, coeffs)
         if behinds is None:
             behind, strips[0] = lax.optimization_barrier((behind, strips[0]))
-            behinds = everyone(behind)
+            behinds = everyone(behind, behind)
         out = store(work, strip)
         prepared = prepare(refls, factors, behinds, kinds, step, strips, projs)
         current = finish(out, prepared, gots)

time: 13.7 us -> 13.9 us (1.015)
  the two profiles are of different devices: /device:TPU:0 before, /device:TPU:18 now
where the time goes in v9:
time: 13.9 us; the launch traced here: 13.8 us
  starting transfers between devices  5.18 us (37%)
  Pallas kernels  5.05 us (36%)
  waiting for transfers between devices  2.49 us (18%)
  local copies, waits for them, and re-layouts  0.93 us (7%)
    ppermute x2, starting transfers between devices, trade(): return lax.ppermute(block, ('row', 'col'), route)  3.11 us
    ppermute x2, waiting for transfers between devices, trade(): return lax.ppermute(block, ('row', 'col'), route)  2.14 us
    pallas_call x1, Pallas kernels, middle(): pl.pallas_call(body, out_shape=[shape(height, width)] + [shape(strip, wid...  1.65 us
    pallas_call x4, Pallas kernels, vmem_call(): pl.pallas_call(body, out_shape=outs, in_specs=[VMEM] * len(args), out_spe...  1.55 us
    ppermute x1, starting transfers between devices, local(): lax.ppermute(end, 'row', [(r, (r + 1) % rows) for r in range(rows)])  1.49 us
    pallas_call x1, Pallas kernels, finish(): pl.pallas_call(body, out_shape=jax.ShapeDtypeStruct((height, width), F32)...  0.95 us
    unnamed x8, local copies, waits for them, and re-layouts  0.93 us
    pallas_call x1, Pallas kernels, store(): pl.pallas_call(body, out_shape=jax.ShapeDtypeStruct((height, width), F32)...  0.89 us
  transfers between devices with their start and end apart: 6, of which 2 were waited for; matrix products, arithmetic and copies ran while one was open for 0% of the time, Pallas kernels for 30%

profile of v9, /device:TPU:18, one launch (start us, length us, event | category | flops | bytes accessed | tf_op | source)
XLA Modules:
  0.0 13.8 jit_solution(9525976880074734887)
XLA Ops:
  0.0 0.0 collective-permute-start.1
  0.0 0.0 copy-start
  0.0 0.0 copy-start.1
  0.0 0.9 %copy-done.2 = f32[1,4,128,128]{3,2,1,0:T(8,128)S(1)} copy-done((f32[1,4,128,128]{3,2,1,0:T(8,128)S(1)}, f32[1,4,128,128]{3,2,1,0:T(8,128)}, u32[]{:S(2)}) %copy-start.2) | copy-done | bytes 262168
  1.0 0.5 %collective-permute-start.2 = (f32[1,4,128,128]{3,2,1,0:T(8,128)S(1)}, f32[1,4,128,128]{3,2,1,0:T(8,128)S(1)}, u32[]{:S(2)}, u32[]{:S(2)}) collective-permute-start(f32[1,4,128,128]{3,2,1,0:T(8,128)S(1)} %copy-done.2), channel_id=1, source_target_pairs={{0,1},{1,0},{2,3},{3,2},{4,5},{5,4},{6,7},{7,6},{8,9},{9,8},{10,11... | collective-permute-start | bytes 786440 | tf_op jit(solution)/shard_map/ppermute | solution.py:287
  1.5 0.0 copy-done.3
  1.5 0.1 tables.1
  1.5 1.5 %collective-permute-start = (f32[1,128,128]{2,1,0:T(8,128)S(1)}, f32[1,128,128]{2,1,0:T(8,128)S(1)}, u32[]{:S(2)}, u32[]{:S(2)}) collective-permute-start(f32[1,128,128]{2,1,0:T(8,128)S(1)} %get-tuple-element.26), channel_id=1, source_target_pairs={{0,2},{2,4},{4,6},{6,8},{8,10},{10,12},{12,14},{14,16},{16,18},{18... | collective-permute-start | bytes 196616 | tf_op jit(solution)/shard_map/ppermute | solution.py:306
  3.0 0.0 collective-permute-done.2.refs_3_
  3.0 0.0 collective-permute-done.1.refs_1_
  3.0 0.0 copy-done
  3.1 0.6 %edge.2 = (f32[128,256]{1,0:T(8,128)S(1)}, f32[128,256]{1,0:T(8,128)S(1)}) custom-call(s32[8,128]{1,0:T(8,128)S(1)} %get-tuple-element.25.kinds_ref, f32[1024,256]{1,0:T(8,128)S(1)} %copy-done, f32[1,1024,128]{2,1,0:T(8,128)S(1)} %copy-done.1, f32[1,1024,128]{2,1,0:T(8,128)S(1)} %collective-permute-done.1.refs_1_, f32[1,4,128,128]{3,2,1,0:T(8,128)S(1)} %copy-done.2, ...), custom_call_target="tpu_custom_call" | custom-call | tf_op jit(solution)/shard_map/edge/pallas_call | solution.py:52
  3.6 0.6 %collective-permute-start.4 = (f32[128,256]{1,0:T(8,128)S(1)}, f32[128,256]{1,0:T(8,128)S(1)}, u32[]{:S(2)}, u32[]{:S(2)}) collective-permute-start(f32[128,256]{1,0:T(8,128)S(1)} %get-tuple-element.33.even_ref), channel_id=1, source_target_pairs={{0,2},{1,3},{2,0},{3,1},{4,6},{5,7},{6,4},{7,5},{8,10},{9,11},{10,... | collective-permute-start | bytes 393224 | tf_op jit(solution)/shard_map/ppermute | solution.py:296
  4.2 0.5 %edge.3 = (f32[128,256]{1,0:T(8,128)S(1)}, f32[128,256]{1,0:T(8,128)S(1)}) custom-call(s32[8,128]{1,0:T(8,128)S(1)} %get-tuple-element.25.kinds_ref, f32[1024,256]{1,0:T(8,128)S(1)} %copy-done, f32[1,1024,128]{2,1,0:T(8,128)S(1)} %copy-done.1, f32[1,1024,128]{2,1,0:T(8,128)S(1)} %collective-permute-done.1.refs_1_, f32[1,4,128,128]{3,2,1,0:T(8,128)S(1)} %copy-done.2, ...), custom_call_target="tpu_custom_call" | custom-call | tf_op jit(solution)/shard_map/edge/pallas_call | solution.py:52
  4.8 2.5 %collective-permute-start.5 = (f32[128,256]{1,0:T(8,128)S(1)}, f32[128,256]{1,0:T(8,128)S(1)}, u32[]{:S(2)}, u32[]{:S(2)}) collective-permute-start(f32[128,256]{1,0:T(8,128)S(1)} %get-tuple-element.34.odd_ref), channel_id=1, source_target_pairs={{0,1},{1,0},{2,4},{3,5},{4,2},{5,3},{6,8},{7,9},{8,6},{9,7},{10,12... | collective-permute-start | bytes 393224 | tf_op jit(solution)/shard_map/ppermute | solution.py:296
  7.3 1.7 %middle.1 = (f32[1024,256]{1,0:T(8,128)S(1)}, f32[128,256]{1,0:T(8,128)S(1)}, f32[128,256]{1,0:T(8,128)S(1)}) custom-call(s32[8,128]{1,0:T(8,128)S(1)} %get-tuple-element.25.kinds_ref, f32[1024,256]{1,0:T(8,128)S(1)} %copy-done, f32[128,256]{1,0:T(8,128)S(1)} %get-tuple-element.28.even_coeff, f32[128,256]{1,0:T(8,128)S(1)} %get-tuple-element.29.odd_coeff, ...), custom_call_target="tpu_custom_call" | custom-call | tf_op jit(solution)/shard_map/middle/pallas_call | solution.py:182
  8.9 0.0 collective-permute-done.refs_4_
  8.9 0.1 collective-permute-start.3
  9.0 0.9 %store.1.refs_8_ = f32[1024,256]{1,0:T(8,128)} custom-call(f32[1024,256]{1,0:T(8,128)S(1)} %get-tuple-element.42.work_ref), custom_call_target="tpu_custom_call" | custom-call | tf_op jit(solution)/shard_map/store/pallas_call | solution.py:202
  9.9 0.3 %collective-permute-done.3.refs_5_ = f32[1,128,128]{2,1,0:T(8,128)S(1)} collective-permute-done((f32[1,128,128]{2,1,0:T(8,128)S(1)}, f32[1,128,128]{2,1,0:T(8,128)S(1)}, u32[]{:S(2)}, u32[]{:S(2)}) %collective-permute-start.3) | collective-permute-done | bytes 65568 | tf_op jit(solution)/shard_map/ppermute | solution.py:287
  10.3 0.4 %prepare.1 = (f32[128,256]{1,0:T(8,128)S(1)}, f32[128,256]{1,0:T(8,128)S(1)}, bf16[128,128]{1,0:T(8,128)(2,1)S(1)}, bf16[128,128]{1,0:T(8,128)(2,1)S(1)}, bf16[1...) custom-call(s32[8,128]{1,0:T(8,128)S(1)} %get-tuple-element.25.kinds_ref, f32[128,256]{1,0:T(8,128)S(1)} %get-tuple-element.31.top_ref, ...), custom_call_target="tpu_custom_call" | custom-call | tf_op jit(solution)/shard_map/prepare/pallas_call | solution.py:52
  10.7 0.0 collective-permute-done.4.refs_6_
  10.7 2.1 %collective-permute-done.5.refs_7_ = f32[128,256]{1,0:T(8,128)S(1)} collective-permute-done((f32[128,256]{1,0:T(8,128)S(1)}, f32[128,256]{1,0:T(8,128)S(1)}, u32[]{:S(2)}, u32[]{:S(2)}) %collective-permute-start.5) | collective-permute-done | bytes 131104 | tf_op jit(solution)/shard_map/ppermute | solution.py:296
  12.8 1.0 %finish.1 = f32[1024,256]{1,0:T(8,128)} custom-call(f32[128,256]{1,0:T(8,128)S(1)} %get-tuple-element.36.refs_0_, f32[128,256]{1,0:T(8,128)S(1)} %get-tuple-element.37.refs_1_, bf16[128,128]{1,0:T(8,128)(2,1)S(1)} %get-tuple-element.38.refs_2_, bf16[128,128]{1,0:T(8,128)(2,1)S(1)} %get-tuple-element.39.refs_3_, ...), custom_call_target="tpu_custom_call", output_to_operand_aliasing={{}: (8, {})} | custom-call | tf_op jit(solution)/shard_map/finish/pallas_call | solution.py:270
  (4 shorter events, 0.0 us)
Async XLA Ops:
  0.0 3.0 %collective-permute-start.1 = (f32[1,1024,128]{2,1,0:T(8,128)}, f32[1,1024,128]{2,1,0:T(8,128)S(1)}, u32[]{:S(2)}, u32[]{:S(2)}) collective-permute-start(f32[1,1024,128]{2,1,0:T(8,128)} %refs_0_.7), channel_id=1, source_target_pairs={{0,1},{1,0},{2,3},{3,2},{4,5},{5,4},{6,7},{7,6},{8,9},{9,8},{10,11... | collective-permute-start | bytes 1572872 | tf_op jit(solution)/shard_map/ppermute | solution.py:287
  0.0 1.0 %copy-start.2 = (f32[1,4,128,128]{3,2,1,0:T(8,128)S(1)}, f32[1,4,128,128]{3,2,1,0:T(8,128)}, u32[]{:S(2)}) copy-start(f32[1,4,128,128]{3,2,1,0:T(8,128)} %refs_2_.9) | copy-start | bytes 786436
  0.0 1.5 %copy-start.3 = (s32[2]{0:T(128)S(1)}, s32[2]{0:T(128)}, u32[]{:S(2)}) copy-start(s32[2]{0:T(128)} %param.7) | copy-start | bytes 28
  0.0 3.0 %copy-start = (f32[1024,256]{1,0:T(8,128)S(1)}, f32[1024,256]{1,0:T(8,128)}, u32[]{:S(2)}) copy-start(f32[1024,256]{1,0:T(8,128)} %x_ref.5) | copy-start | bytes 3145732
  0.0 3.0 %copy-start.1 = (f32[1,1024,128]{2,1,0:T(8,128)S(1)}, f32[1,1024,128]{2,1,0:T(8,128)}, u32[]{:S(2)}) copy-start(f32[1,1024,128]{2,1,0:T(8,128)} %refs_0_.7) | copy-start | bytes 1572868
  1.0 2.1 %collective-permute-start.2 = (f32[1,4,128,128]{3,2,1,0:T(8,128)S(1)}, f32[1,4,128,128]{3,2,1,0:T(8,128)S(1)}, u32[]{:S(2)}, u32[]{:S(2)}) collective-permute-start(f32[1,4,128,128]{3,2,1,0:T(8,128)S(1)} %copy-done.2), channel_id=1, source_target_pairs={{0,1},{1,0},{2,3},{3,2},{4,5},{5,4},{6,7},{7,6},{8,9},{9,8},{10,11... | collective-permute-start | bytes 786440 | tf_op jit(solution)/shard_map/ppermute | solution.py:287
  1.5 7.4 %collective-permute-start = (f32[1,128,128]{2,1,0:T(8,128)S(1)}, f32[1,128,128]{2,1,0:T(8,128)S(1)}, u32[]{:S(2)}, u32[]{:S(2)}) collective-permute-start(f32[1,128,128]{2,1,0:T(8,128)S(1)} %get-tuple-element.26), channel_id=1, source_target_pairs={{0,2},{2,4},{4,6},{6,8},{8,10},{10,12},{12,14},{14,16},{16,18},{18... | collective-permute-start | bytes 196616 | tf_op jit(solution)/shard_map/ppermute | solution.py:306
  3.6 7.0 %collective-permute-start.4 = (f32[128,256]{1,0:T(8,128)S(1)}, f32[128,256]{1,0:T(8,128)S(1)}, u32[]{:S(2)}, u32[]{:S(2)}) collective-permute-start(f32[128,256]{1,0:T(8,128)S(1)} %get-tuple-element.33.even_ref), channel_id=1, source_target_pairs={{0,2},{1,3},{2,0},{3,1},{4,6},{5,7},{6,4},{7,5},{8,10},{9,11},{10,... | collective-permute-start | bytes 393224 | tf_op jit(solution)/shard_map/ppermute | solution.py:296
  4.8 8.0 %collective-permute-start.5 = (f32[128,256]{1,0:T(8,128)S(1)}, f32[128,256]{1,0:T(8,128)S(1)}, u32[]{:S(2)}, u32[]{:S(2)}) collective-permute-start(f32[128,256]{1,0:T(8,128)S(1)} %get-tuple-element.34.odd_ref), channel_id=1, source_target_pairs={{0,1},{1,0},{2,4},{3,5},{4,2},{5,3},{6,8},{7,9},{8,6},{9,7},{10,12... | collective-permute-start | bytes 393224 | tf_op jit(solution)/shard_map/ppermute | solution.py:296
  8.9 1.3 %collective-permute-start.3 = (f32[1,128,128]{2,1,0:T(8,128)S(1)}, f32[1,128,128]{2,1,0:T(8,128)S(1)}, u32[]{:S(2)}, u32[]{:S(2)}) collective-permute-start(f32[1,128,128]{2,1,0:T(8,128)S(1)} %collective-permute-done.refs_4_), channel_id=1, source_target_pairs={{0,1},{1,0},{2,3},{3,2},{4,5},{5,4},{6,7},{7,6},{8,9},{9,8},{10,11... | collective-permute-start | bytes 196616 | tf_op jit(solution)/shard_map/ppermute | solution.py:287

commit v10 on v9

--- a/solution.py
+++ b/solution.py
@@ -59,7 +59,7 @@
     )(*near(*args))
 
 
-def entry(*arrays):
+def entry(*arrays, after=()):
     lanes = (8, LANES)
 
     def body(*refs):
@@ -68,11 +68,11 @@
     return pl.pallas_call(
         body,
         out_shape=shape(*lanes),
-        in_specs=[HBM] * len(arrays),
+        in_specs=[VMEM] * len(after) + [HBM] * len(arrays),
         out_specs=VMEM,
         name="entry",
         compiler_params=LEAN,
-    )(*near(*arrays, space=pltpu.HBM))
+    )(*near(*after), *near(*arrays, space=pltpu.HBM))
 
 
 def tables(mark, tfactors, plan, columns):
@@ -298,10 +298,12 @@
     def everyone(piece, sent):
         return [piece, *(around(sent, shift) for shift in range(1, columns))]
 
+    factors = everyone(tfactors, tfactors)
     plan = plan.reshape(1, groups)
-    mark = entry(plan, vectors, reflectors, tfactors)
-    later, mark = lax.optimization_barrier((tfactors, mark))
-    refls, factors = everyone(reflectors, reflectors), everyone(tfactors, later)
+    mark = entry(plan, tfactors)
+    later, mark = lax.optimization_barrier((reflectors, mark))
+    refls = everyone(reflectors, later)
+    mark = entry(vectors, reflectors, after=(mark,))
     kinds, end = tables(mark, tfactors, plan, columns)
     behind = lax.ppermute(end, "row", [(r, (r + 1) % rows) for r in range(rows)])
     current, behinds = vectors, None

time: 13.9 us -> 13.7 us (0.986)
  the two profiles are of different devices: /device:TPU:18 before, /device:TPU:0 now
where the time goes in v10:
time: 13.7 us; the launch traced here: 13.5 us
  starting transfers between devices  5.21 us (38%)
  Pallas kernels  5.07 us (37%)
  waiting for transfers between devices  2.76 us (20%)
  local copies, waits for them, and re-layouts  0.38 us (3%)
    ppermute x1, starting transfers between devices, local(): lax.ppermute(end, 'row', [(r, (r + 1) % rows) for r in range(rows)])  2.48 us
    ppermute x1, waiting for transfers between devices, local(): lax.ppermute(end, 'row', [(r, (r + 1) % rows) for r in range(rows)])  2.39 us
    ppermute x2, starting transfers between devices, trade(): return lax.ppermute(block, ('row', 'col'), route)  1.67 us
    pallas_call x1, Pallas kernels, middle(): pl.pallas_call(body, out_shape=[shape(height, width)] + [shape(strip, wid...  1.66 us
    pallas_call x4, Pallas kernels, vmem_call(): pl.pallas_call(body, out_shape=outs, in_specs=[VMEM] * len(args), out_spe...  1.55 us
    ppermute x3, starting transfers between devices, around(): lax.ppermute(block, 'col', [(c, (c + shift) % columns) for c in range(col...  1.07 us
    pallas_call x1, Pallas kernels, finish(): pl.pallas_call(body, out_shape=jax.ShapeDtypeStruct((height, width), F32)...  0.97 us
    pallas_call x1, Pallas kernels, store(): pl.pallas_call(body, out_shape=jax.ShapeDtypeStruct((height, width), F32)...  0.89 us
  transfers between devices with their start and end apart: 6, of which 2 were waited for; matrix products, arithmetic and copies ran while one was open for 0% of the time, Pallas kernels for 30%

profile of v10, /device:TPU:0, one launch (start us, length us, event | category | flops | bytes accessed | tf_op | source)
XLA Modules:
  0.0 13.5 jit_solution(8074088458002588669)
XLA Ops:
  0.0 0.0 copy-start.2
  0.0 0.6 %collective-permute-start.1 = (f32[1,1024,128]{2,1,0:T(8,128)}, f32[1,1024,128]{2,1,0:T(8,128)S(1)}, u32[]{:S(2)}, u32[]{:S(2)}) collective-permute-start(f32[1,1024,128]{2,1,0:T(8,128)} %refs_0_.7), channel_id=1, source_target_pairs={{0,1},{1,0},{2,3},{3,2},{4,5},{5,4},{6,7},{7,6},{8,9},{9,8},{10,11... | collective-permute-start | bytes 1572872 | tf_op jit(solution)/shard_map/ppermute | solution.py:287
  0.6 0.4 %copy-done.2 = f32[1,4,128,128]{3,2,1,0:T(8,128)S(1)} copy-done((f32[1,4,128,128]{3,2,1,0:T(8,128)S(1)}, f32[1,4,128,128]{3,2,1,0:T(8,128)}, u32[]{:S(2)}) %copy-start.2) | copy-done | bytes 262168
  1.0 0.5 %collective-permute-start.2 = (f32[1,4,128,128]{3,2,1,0:T(8,128)S(1)}, f32[1,4,128,128]{3,2,1,0:T(8,128)S(1)}, u32[]{:S(2)}, u32[]{:S(2)}) collective-permute-start(f32[1,4,128,128]{3,2,1,0:T(8,128)S(1)} %copy-done.2), channel_id=1, source_target_pairs={{0,1},{1,0},{2,3},{3,2},{4,5},{5,4},{6,7},{7,6},{8,9},{9,8},{10,11... | collective-permute-start | bytes 786440 | tf_op jit(solution)/shard_map/ppermute | solution.py:287
  1.4 0.0 copy-done.3
  1.5 0.1 tables.1
  1.5 2.5 %collective-permute-start = (f32[1,128,128]{2,1,0:T(8,128)S(1)}, f32[1,128,128]{2,1,0:T(8,128)S(1)}, u32[]{:S(2)}, u32[]{:S(2)}) collective-permute-start(f32[1,128,128]{2,1,0:T(8,128)S(1)} %get-tuple-element.26), channel_id=1, source_target_pairs={{0,2},{2,4},{4,6},{6,8},{8,10},{10,12},{12,14},{14,16},{16,18},{18... | collective-permute-start | bytes 196616 | tf_op jit(solution)/shard_map/ppermute | solution.py:308
  4.0 0.0 collective-permute-done.2.refs_3_
  4.0 0.0 collective-permute-done.1.refs_1_
  4.0 0.0 copy-done
  4.0 0.0 copy-done.1
  4.0 0.6 %edge.2 = (f32[128,256]{1,0:T(8,128)S(1)}, f32[128,256]{1,0:T(8,128)S(1)}) custom-call(s32[8,128]{1,0:T(8,128)S(1)} %get-tuple-element.25.kinds_ref, f32[1024,256]{1,0:T(8,128)S(1)} %copy-done, f32[1,1024,128]{2,1,0:T(8,128)S(1)} %copy-done.1, f32[1,1024,128]{2,1,0:T(8,128)S(1)} %collective-permute-done.1.refs_1_, f32[1,4,128,128]{3,2,1,0:T(8,128)S(1)} %copy-done.2, ...), custom_call_target="tpu_custom_call" | custom-call | tf_op jit(solution)/shard_map/edge/pallas_call | solution.py:52
  4.6 1.6 %collective-permute-start.4 = (f32[128,256]{1,0:T(8,128)S(1)}, f32[128,256]{1,0:T(8,128)S(1)}, u32[]{:S(2)}, u32[]{:S(2)}) collective-permute-start(f32[128,256]{1,0:T(8,128)S(1)} %get-tuple-element.33.even_ref), channel_id=1, source_target_pairs={{0,2},{1,3},{2,0},{3,1},{4,6},{5,7},{6,4},{7,5},{8,10},{9,11},{10,... | collective-permute-start | bytes 393224 | tf_op jit(solution)/shard_map/ppermute | solution.py:296
  6.2 0.5 %edge.3 = (f32[128,256]{1,0:T(8,128)S(1)}, f32[128,256]{1,0:T(8,128)S(1)}) custom-call(s32[8,128]{1,0:T(8,128)S(1)} %get-tuple-element.25.kinds_ref, f32[1024,256]{1,0:T(8,128)S(1)} %copy-done, f32[1,1024,128]{2,1,0:T(8,128)S(1)} %copy-done.1, f32[1,1024,128]{2,1,0:T(8,128)S(1)} %collective-permute-done.1.refs_1_, f32[1,4,128,128]{3,2,1,0:T(8,128)S(1)} %copy-done.2, ...), custom_call_target="tpu_custom_call" | custom-call | tf_op jit(solution)/shard_map/edge/pallas_call | solution.py:52
  6.7 0.1 collective-permute-start.5
  6.8 1.7 %middle.1 = (f32[1024,256]{1,0:T(8,128)S(1)}, f32[128,256]{1,0:T(8,128)S(1)}, f32[128,256]{1,0:T(8,128)S(1)}) custom-call(s32[8,128]{1,0:T(8,128)S(1)} %get-tuple-element.25.kinds_ref, f32[1024,256]{1,0:T(8,128)S(1)} %copy-done, f32[128,256]{1,0:T(8,128)S(1)} %get-tuple-element.28.even_coeff, f32[128,256]{1,0:T(8,128)S(1)} %get-tuple-element.29.odd_coeff, ...), custom_call_target="tpu_custom_call" | custom-call | tf_op jit(solution)/shard_map/middle/pallas_call | solution.py:182
  8.5 2.4 %collective-permute-done.refs_4_ = f32[1,128,128]{2,1,0:T(8,128)S(1)} collective-permute-done((f32[1,128,128]{2,1,0:T(8,128)S(1)}, f32[1,128,128]{2,1,0:T(8,128)S(1)}, u32[]{:S(2)}, u32[]{:S(2)}) %collective-permute-start) | collective-permute-done | bytes 65568 | tf_op jit(solution)/shard_map/ppermute | solution.py:308
  10.9 0.0 collective-permute-start.3
  10.9 0.9 %store.1.refs_8_ = f32[1024,256]{1,0:T(8,128)} custom-call(f32[1024,256]{1,0:T(8,128)S(1)} %get-tuple-element.42.work_ref), custom_call_target="tpu_custom_call" | custom-call | tf_op jit(solution)/shard_map/store/pallas_call | solution.py:202
  11.8 0.4 %collective-permute-done.3.refs_5_ = f32[1,128,128]{2,1,0:T(8,128)S(1)} collective-permute-done((f32[1,128,128]{2,1,0:T(8,128)S(1)}, f32[1,128,128]{2,1,0:T(8,128)S(1)}, u32[]{:S(2)}, u32[]{:S(2)}) %collective-permute-start.3) | collective-permute-done | bytes 65568 | tf_op jit(solution)/shard_map/ppermute | solution.py:287
  12.1 0.4 %prepare.1 = (f32[128,256]{1,0:T(8,128)S(1)}, f32[128,256]{1,0:T(8,128)S(1)}, bf16[128,128]{1,0:T(8,128)(2,1)S(1)}, bf16[128,128]{1,0:T(8,128)(2,1)S(1)}, bf16[1...) custom-call(s32[8,128]{1,0:T(8,128)S(1)} %get-tuple-element.25.kinds_ref, f32[128,256]{1,0:T(8,128)S(1)} %get-tuple-element.31.top_ref, ...), custom_call_target="tpu_custom_call" | custom-call | tf_op jit(solution)/shard_map/prepare/pallas_call | solution.py:52
  12.5 0.0 collective-permute-done.4.refs_6_
  12.5 0.0 collective-permute-done.5.refs_7_
  12.5 1.0 %finish.1 = f32[1024,256]{1,0:T(8,128)} custom-call(f32[128,256]{1,0:T(8,128)S(1)} %get-tuple-element.36.refs_0_, f32[128,256]{1,0:T(8,128)S(1)} %get-tuple-element.37.refs_1_, bf16[128,128]{1,0:T(8,128)(2,1)S(1)} %get-tuple-element.38.refs_2_, bf16[128,128]{1,0:T(8,128)(2,1)S(1)} %get-tuple-element.39.refs_3_, ...), custom_call_target="tpu_custom_call", output_to_operand_aliasing={{}: (8, {})} | custom-call | tf_op jit(solution)/shard_map/finish/pallas_call | solution.py:270
  (5 shorter events, 0.0 us)
Async XLA Ops:
  0.0 0.9 %copy-start.2 = (f32[1,4,128,128]{3,2,1,0:T(8,128)S(1)}, f32[1,4,128,128]{3,2,1,0:T(8,128)}, u32[]{:S(2)}) copy-start(f32[1,4,128,128]{3,2,1,0:T(8,128)} %refs_2_.9) | copy-start | bytes 786436
  0.0 4.0 %copy-start = (f32[1024,256]{1,0:T(8,128)S(1)}, f32[1024,256]{1,0:T(8,128)}, u32[]{:S(2)}) copy-start(f32[1024,256]{1,0:T(8,128)} %x_ref.5) | copy-start | bytes 3145732
  0.0 1.4 %copy-start.3 = (s32[2]{0:T(128)S(1)}, s32[2]{0:T(128)}, u32[]{:S(2)}) copy-start(s32[2]{0:T(128)} %param.7) | copy-start | bytes 28
  0.0 4.0 %collective-permute-start.1 = (f32[1,1024,128]{2,1,0:T(8,128)}, f32[1,1024,128]{2,1,0:T(8,128)S(1)}, u32[]{:S(2)}, u32[]{:S(2)}) collective-permute-start(f32[1,1024,128]{2,1,0:T(8,128)} %refs_0_.7), channel_id=1, source_target_pairs={{0,1},{1,0},{2,3},{3,2},{4,5},{5,4},{6,7},{7,6},{8,9},{9,8},{10,11... | collective-permute-start | bytes 1572872 | tf_op jit(solution)/shard_map/ppermute | solution.py:287
  1.0 3.1 %collective-permute-start.2 = (f32[1,4,128,128]{3,2,1,0:T(8,128)S(1)}, f32[1,4,128,128]{3,2,1,0:T(8,128)S(1)}, u32[]{:S(2)}, u32[]{:S(2)}) collective-permute-start(f32[1,4,128,128]{3,2,1,0:T(8,128)S(1)} %copy-done.2), channel_id=1, source_target_pairs={{0,1},{1,0},{2,3},{3,2},{4,5},{5,4},{6,7},{7,6},{8,9},{9,8},{10,11... | collective-permute-start | bytes 786440 | tf_op jit(solution)/shard_map/ppermute | solution.py:287
  1.4 2.6 %copy-start.1 = (f32[1,1024,128]{2,1,0:T(8,128)S(1)}, f32[1,1024,128]{2,1,0:T(8,128)}, u32[]{:S(2)}) copy-start(f32[1,1024,128]{2,1,0:T(8,128)} %refs_0_.7) | copy-start | bytes 1572868
  1.5 9.3 %collective-permute-start = (f32[1,128,128]{2,1,0:T(8,128)S(1)}, f32[1,128,128]{2,1,0:T(8,128)S(1)}, u32[]{:S(2)}, u32[]{:S(2)}) collective-permute-start(f32[1,128,128]{2,1,0:T(8,128)S(1)} %get-tuple-element.26), channel_id=1, source_target_pairs={{0,2},{2,4},{4,6},{6,8},{8,10},{10,12},{12,14},{14,16},{16,18},{18... | collective-permute-start | bytes 196616 | tf_op jit(solution)/shard_map/ppermute | solution.py:308
  4.6 7.9 %collective-permute-start.4 = (f32[128,256]{1,0:T(8,128)S(1)}, f32[128,256]{1,0:T(8,128)S(1)}, u32[]{:S(2)}, u32[]{:S(2)}) collective-permute-start(f32[128,256]{1,0:T(8,128)S(1)} %get-tuple-element.33.even_ref), channel_id=1, source_target_pairs={{0,2},{1,3},{2,0},{3,1},{4,6},{5,7},{6,4},{7,5},{8,10},{9,11},{10,... | collective-permute-start | bytes 393224 | tf_op jit(solution)/shard_map/ppermute | solution.py:296
  6.7 5.8 %collective-permute-start.5 = (f32[128,256]{1,0:T(8,128)S(1)}, f32[128,256]{1,0:T(8,128)S(1)}, u32[]{:S(2)}, u32[]{:S(2)}) collective-permute-start(f32[128,256]{1,0:T(8,128)S(1)} %get-tuple-element.34.odd_ref), channel_id=1, source_target_pairs={{0,1},{1,0},{2,4},{3,5},{4,2},{5,3},{6,8},{7,9},{8,6},{9,7},{10,12... | collective-permute-start | bytes 393224 | tf_op jit(solution)/shard_map/ppermute | solution.py:296
  10.9 1.3 %collective-permute-start.3 = (f32[1,128,128]{2,1,0:T(8,128)S(1)}, f32[1,128,128]{2,1,0:T(8,128)S(1)}, u32[]{:S(2)}, u32[]{:S(2)}) collective-permute-start(f32[1,128,128]{2,1,0:T(8,128)S(1)} %collective-permute-done.refs_4_), channel_id=1, source_target_pairs={{0,1},{1,0},{2,3},{3,2},{4,5},{5,4},{6,7},{7,6},{8,9},{9,8},{10,11... | collective-permute-start | bytes 196616 | tf_op jit(solution)/shard_map/ppermute | solution.py:287

commit v11 on v10

--- a/solution.py
+++ b/solution.py
@@ -75,12 +75,36 @@
     )(*near(*after), *near(*arrays, space=pltpu.HBM))
 
 
+def fold(f):
+    size = f.shape[1]
+    part = size // 4
+    lane = lax.broadcasted_iota(jnp.int32, (part, size), 1)
+    rows = [f[at * part : (at + 1) * part] for at in range(4)]
+    mixed = jnp.where(lane < part, pltpu.roll(rows[3], part, 1), rows[1])
+    half = part // 2
+    halves = jnp.where(lane[:half] < 2 * part, pltpu.roll(rows[2][:half], 2 * part, 1), rows[2][half:])
+    return jnp.concatenate([rows[0], mixed, halves], 0)
+
+
+def unfold(f):
+    size = f.shape[1]
+    part = size // 4
+    half = part // 2
+    lane = lax.broadcasted_iota(jnp.int32, (part, size), 1)
+    mixed, halves = f[part : 2 * part], f[2 * part :]
+    second = jnp.where(lane < part, 0.0, mixed)
+    fourth = jnp.where(lane < 3 * part, 0.0, pltpu.roll(mixed, 3 * part, 1))
+    third = [jnp.where(lane[:half] < 2 * part, 0.0, v) for v in (pltpu.roll(halves, 2 * part, 1), halves)]
+    return jnp.concatenate([f[:part], second, *third, fourth], 0)
+
+
 def tables(mark, tfactors, plan, columns):
     held, count, lanes = tfactors.shape[:3]
     groups = plan.shape[1]
 
     def body(_, plan_ref, f_ref, kinds_ref, end_ref):
-        end_ref[...] = f_ref[:, count - 1]
+        for slot in range(held):
+            end_ref[slot] = fold(f_ref[slot, count - 1])
         me = lax.axis_index("col")
         kinds_ref[...] = jnp.zeros_like(kinds_ref)
         for step in range(groups):
@@ -91,7 +115,8 @@
             kinds_ref[step : step + 1, :] = gap * held + (group - home * held)
 
     table = shape(-(-groups // 8) * 8, lanes, dtype=jnp.int32)
-    return vmem_call(body, [table, shape(held, lanes, lanes)], "tables", mark, plan, tfactors)
+    folded = shape(held, 5 * lanes // 8, lanes)
+    return vmem_call(body, [table, folded], "tables", mark, plan, tfactors)
 
 
 def is_top(odd_round):
@@ -222,13 +247,15 @@
         row, last = lax.axis_index("row"), lax.axis_size("row") - 1
         projs = ordered(even_ref[...], odd_ref[...])
 
-        def weight(start, ends, present):
+        def weight(start, factor, present):
             refl = pick(kinds_ref, step + 1, [r[start : start + strip, :] for r in refl_refs])
-            value = product(split(refl), split(pick(kinds_ref, step + 1, ends)))
+            value = product(split(refl), split(factor))
             return jnp.where(present, value, jnp.zeros_like(value))
 
-        top = weight(0, [r[...] for r in behind_refs], row > 0)
-        low = weight(height - strip, [r[count - 1] for r in factor_refs], row < last)
+        before = unfold(pick(kinds_ref, step + 1, [r[...] for r in behind_refs]))
+        own = pick(kinds_ref, step + 1, [r[count - 1] for r in factor_refs])
+        top = weight(0, before, row > 0)
+        low = weight(height - strip, own, row < last)
         even, odd = ordered(top, low)
         highs[0][...], lows[0][...] = split(even)
         highs[1][...], lows[1][...] = split(odd)

time: 13.7 us -> 17.2 us (1.26)
  starting transfers between devices: 5.21 us -> 7.03 us
  waiting for transfers between devices: 2.76 us -> 4.52 us
    ppermute x2, starting transfers between devices: 1.67 us -> 2.99 us  [trade(): return lax.ppermute(block, ('row', 'col'), route)]
    ppermute x3, waiting for transfers between devices: 0.36 us -> 1.5 us  [around(): lax.ppermute(block, 'col', [(c, (c + shift) % columns) for c in range(col...]
    ppermute x1, waiting for transfers between devices: 2.39 us -> 3.02 us  [local(): lax.ppermute(end, 'row', [(r, (r + 1) % rows) for r in range(rows)])]
    ppermute x1, starting transfers between devices: 2.48 us -> 2.97 us  [local(): lax.ppermute(end, 'row', [(r, (r + 1) % rows) for r in range(rows)])]
  transfers between devices with their start and end apart: 6 -> 6, of which waited for: 2 -> 3; matrix products, arithmetic and copies ran while one was open for 0% -> 0% of each run, Pallas kernels for 30% -> 21%
where the time goes in v11:
time: 17.2 us; the launch traced here: 17.1 us
  starting transfers between devices  7.03 us (41%)
  Pallas kernels  5.09 us (30%)
  waiting for transfers between devices  4.52 us (26%)
  local copies, waits for them, and re-layouts  0.38 us (2%)
    ppermute x1, waiting for transfers between devices, local(): lax.ppermute(end, 'row', [(r, (r + 1) % rows) for r in range(rows)])  3.02 us
    ppermute x2, starting transfers between devices, trade(): return lax.ppermute(block, ('row', 'col'), route)  2.99 us
    ppermute x1, starting transfers between devices, local(): lax.ppermute(end, 'row', [(r, (r + 1) % rows) for r in range(rows)])  2.97 us
    pallas_call x1, Pallas kernels, middle(): pl.pallas_call(body, out_shape=[shape(height, width)] + [shape(strip, wid...  1.66 us
    pallas_call x4, Pallas kernels, vmem_call(): pl.pallas_call(body, out_shape=outs, in_specs=[VMEM] * len(args), out_spe...  1.56 us
    ppermute x3, waiting for transfers between devices, around(): lax.ppermute(block, 'col', [(c, (c + shift) % columns) for c in range(col...  1.5 us
    ppermute x3, starting transfers between devices, around(): lax.ppermute(block, 'col', [(c, (c + shift) % columns) for c in range(col...  1.07 us
    pallas_call x1, Pallas kernels, finish(): pl.pallas_call(body, out_shape=jax.ShapeDtypeStruct((height, width), F32)...  0.97 us
  transfers between devices with their start and end apart: 6, of which 3 were waited for; matrix products, arithmetic and copies ran while one was open for 0% of the time, Pallas kernels for 21%

profile of v11, /device:TPU:0, one launch (start us, length us, event | category | flops | bytes accessed | tf_op | source)
XLA Modules:
  0.0 17.1 jit_solution(17683590073757003490)
XLA Ops:
  0.0 0.0 copy-start.2
  0.0 0.6 %collective-permute-start.1 = (f32[1,1024,128]{2,1,0:T(8,128)}, f32[1,1024,128]{2,1,0:T(8,128)S(1)}, u32[]{:S(2)}, u32[]{:S(2)}) collective-permute-start(f32[1,1024,128]{2,1,0:T(8,128)} %refs_0_.7), channel_id=1, source_target_pairs={{0,1},{1,0},{2,3},{3,2},{4,5},{5,4},{6,7},{7,6},{8,9},{9,8},{10,11... | collective-permute-start | bytes 1572872 | tf_op jit(solution)/shard_map/ppermute | solution.py:314
  0.6 0.4 %copy-done.2 = f32[1,4,128,128]{3,2,1,0:T(8,128)S(1)} copy-done((f32[1,4,128,128]{3,2,1,0:T(8,128)S(1)}, f32[1,4,128,128]{3,2,1,0:T(8,128)}, u32[]{:S(2)}) %copy-start.2) | copy-done | bytes 262168
  1.0 0.5 %collective-permute-start.2 = (f32[1,4,128,128]{3,2,1,0:T(8,128)S(1)}, f32[1,4,128,128]{3,2,1,0:T(8,128)S(1)}, u32[]{:S(2)}, u32[]{:S(2)}) collective-permute-start(f32[1,4,128,128]{3,2,1,0:T(8,128)S(1)} %copy-done.2), channel_id=1, source_target_pairs={{0,1},{1,0},{2,3},{3,2},{4,5},{5,4},{6,7},{7,6},{8,9},{9,8},{10,11... | collective-permute-start | bytes 786440 | tf_op jit(solution)/shard_map/ppermute | solution.py:314
  1.4 0.0 copy-done.3
  1.5 0.1 tables.1
  1.5 1.2 %collective-permute-done.2.refs_3_ = f32[1,4,128,128]{3,2,1,0:T(8,128)S(1)} collective-permute-done((f32[1,4,128,128]{3,2,1,0:T(8,128)S(1)}, f32[1,4,128,128]{3,2,1,0:T(8,128)S(1)}, u32[]{:S(2)}, u32[]{:S(2)}) %collective-permute-start.2) | collective-permute-done | bytes 262176 | tf_op jit(solution)/shard_map/ppermute | solution.py:314
  2.7 0.0 collective-permute-done.1.refs_1_
  2.7 0.0 copy-done
  2.7 0.0 copy-done.1
  2.7 0.5 %edge.2 = (f32[128,256]{1,0:T(8,128)S(1)}, f32[128,256]{1,0:T(8,128)S(1)}) custom-call(s32[8,128]{1,0:T(8,128)S(1)} %get-tuple-element.25.kinds_ref, f32[1024,256]{1,0:T(8,128)S(1)} %copy-done, f32[1,1024,128]{2,1,0:T(8,128)S(1)} %copy-done.1, f32[1,1024,128]{2,1,0:T(8,128)S(1)} %collective-permute-done.1.refs_1_, f32[1,4,128,128]{3,2,1,0:T(8,128)S(1)} %copy-done.2, ...), custom_call_target="tpu_custom_call" | custom-call | tf_op jit(solution)/shard_map/edge/pallas_call | solution.py:52
  3.3 2.9 %collective-permute-start.4 = (f32[128,256]{1,0:T(8,128)S(1)}, f32[128,256]{1,0:T(8,128)S(1)}, u32[]{:S(2)}, u32[]{:S(2)}) collective-permute-start(f32[128,256]{1,0:T(8,128)S(1)} %get-tuple-element.33.even_ref), channel_id=1, source_target_pairs={{0,2},{1,3},{2,0},{3,1},{4,6},{5,7},{6,4},{7,5},{8,10},{9,11},{10,... | collective-permute-start | bytes 393224 | tf_op jit(solution)/shard_map/ppermute | solution.py:323
  6.2 0.5 %edge.3 = (f32[128,256]{1,0:T(8,128)S(1)}, f32[128,256]{1,0:T(8,128)S(1)}) custom-call(s32[8,128]{1,0:T(8,128)S(1)} %get-tuple-element.25.kinds_ref, f32[1024,256]{1,0:T(8,128)S(1)} %copy-done, f32[1,1024,128]{2,1,0:T(8,128)S(1)} %copy-done.1, f32[1,1024,128]{2,1,0:T(8,128)S(1)} %collective-permute-done.1.refs_1_, f32[1,4,128,128]{3,2,1,0:T(8,128)S(1)} %copy-done.2, ...), custom_call_target="tpu_custom_call" | custom-call | tf_op jit(solution)/shard_map/edge/pallas_call | solution.py:52
  6.7 0.1 collective-permute-start.5
  6.8 3.0 %collective-permute-start = (f32[1,80,128]{2,1,0:T(8,128)S(1)}, f32[1,80,128]{2,1,0:T(8,128)S(1)}, u32[]{:S(2)}, u32[]{:S(2)}) collective-permute-start(f32[1,80,128]{2,1,0:T(8,128)S(1)} %get-tuple-element.26), channel_id=1, source_target_pairs={{0,2},{2,4},{4,6},{6,8},{8,10},{10,12},{12,14},{14,16},{16,18},{18... | collective-permute-start | bytes 122888 | tf_op jit(solution)/shard_map/ppermute | solution.py:335
  9.8 1.7 %middle.1 = (f32[1024,256]{1,0:T(8,128)S(1)}, f32[128,256]{1,0:T(8,128)S(1)}, f32[128,256]{1,0:T(8,128)S(1)}) custom-call(s32[8,128]{1,0:T(8,128)S(1)} %get-tuple-element.25.kinds_ref, f32[1024,256]{1,0:T(8,128)S(1)} %copy-done, f32[128,256]{1,0:T(8,128)S(1)} %get-tuple-element.28.even_coeff, f32[128,256]{1,0:T(8,128)S(1)} %get-tuple-element.29.odd_coeff, ...), custom_call_target="tpu_custom_call" | custom-call | tf_op jit(solution)/shard_map/middle/pallas_call | solution.py:207
  11.4 3.0 %collective-permute-done.refs_4_ = f32[1,80,128]{2,1,0:T(8,128)S(1)} collective-permute-done((f32[1,80,128]{2,1,0:T(8,128)S(1)}, f32[1,80,128]{2,1,0:T(8,128)S(1)}, u32[]{:S(2)}, u32[]{:S(2)}) %collective-permute-start) | collective-permute-done | bytes 40992 | tf_op jit(solution)/shard_map/ppermute | solution.py:335
  14.5 0.0 collective-permute-start.3
  14.5 0.9 %store.1.refs_8_ = f32[1024,256]{1,0:T(8,128)} custom-call(f32[1024,256]{1,0:T(8,128)S(1)} %get-tuple-element.42.work_ref), custom_call_target="tpu_custom_call" | custom-call | tf_op jit(solution)/shard_map/store/pallas_call | solution.py:227
  15.4 0.3 %collective-permute-done.3.refs_5_ = f32[1,80,128]{2,1,0:T(8,128)S(1)} collective-permute-done((f32[1,80,128]{2,1,0:T(8,128)S(1)}, f32[1,80,128]{2,1,0:T(8,128)S(1)}, u32[]{:S(2)}, u32[]{:S(2)}) %collective-permute-start.3) | collective-permute-done | bytes 40992 | tf_op jit(solution)/shard_map/ppermute | solution.py:314
  15.7 0.4 %prepare.1 = (f32[128,256]{1,0:T(8,128)S(1)}, f32[128,256]{1,0:T(8,128)S(1)}, bf16[128,128]{1,0:T(8,128)(2,1)S(1)}, bf16[128,128]{1,0:T(8,128)(2,1)S(1)}, bf16[1...) custom-call(s32[8,128]{1,0:T(8,128)S(1)} %get-tuple-element.25.kinds_ref, f32[128,256]{1,0:T(8,128)S(1)} %get-tuple-element.31.top_ref, ...), custom_call_target="tpu_custom_call" | custom-call | tf_op jit(solution)/shard_map/prepare/pallas_call | solution.py:52
  16.1 0.0 collective-permute-done.4.refs_6_
  16.1 0.0 collective-permute-done.5.refs_7_
  16.1 1.0 %finish.1 = f32[1024,256]{1,0:T(8,128)} custom-call(f32[128,256]{1,0:T(8,128)S(1)} %get-tuple-element.36.refs_0_, f32[128,256]{1,0:T(8,128)S(1)} %get-tuple-element.37.refs_1_, bf16[128,128]{1,0:T(8,128)(2,1)S(1)} %get-tuple-element.38.refs_2_, bf16[128,128]{1,0:T(8,128)(2,1)S(1)} %get-tuple-element.39.refs_3_, ...), custom_call_target="tpu_custom_call", output_to_operand_aliasing={{}: (8, {})} | custom-call | tf_op jit(solution)/shard_map/finish/pallas_call | solution.py:297
  (5 shorter events, 0.0 us)
Async XLA Ops:
  0.0 0.9 %copy-start.2 = (f32[1,4,128,128]{3,2,1,0:T(8,128)S(1)}, f32[1,4,128,128]{3,2,1,0:T(8,128)}, u32[]{:S(2)}) copy-start(f32[1,4,128,128]{3,2,1,0:T(8,128)} %refs_2_.9) | copy-start | bytes 786436
  0.0 2.7 %copy-start = (f32[1024,256]{1,0:T(8,128)S(1)}, f32[1024,256]{1,0:T(8,128)}, u32[]{:S(2)}) copy-start(f32[1024,256]{1,0:T(8,128)} %x_ref.5) | copy-start | bytes 3145732
  0.0 1.4 %copy-start.3 = (s32[2]{0:T(128)S(1)}, s32[2]{0:T(128)}, u32[]{:S(2)}) copy-start(s32[2]{0:T(128)} %param.7) | copy-start | bytes 28
  0.0 2.7 %collective-permute-start.1 = (f32[1,1024,128]{2,1,0:T(8,128)}, f32[1,1024,128]{2,1,0:T(8,128)S(1)}, u32[]{:S(2)}, u32[]{:S(2)}) collective-permute-start(f32[1,1024,128]{2,1,0:T(8,128)} %refs_0_.7), channel_id=1, source_target_pairs={{0,1},{1,0},{2,3},{3,2},{4,5},{5,4},{6,7},{7,6},{8,9},{9,8},{10,11... | collective-permute-start | bytes 1572872 | tf_op jit(solution)/shard_map/ppermute | solution.py:314
  1.0 1.8 %collective-permute-start.2 = (f32[1,4,128,128]{3,2,1,0:T(8,128)S(1)}, f32[1,4,128,128]{3,2,1,0:T(8,128)S(1)}, u32[]{:S(2)}, u32[]{:S(2)}) collective-permute-start(f32[1,4,128,128]{3,2,1,0:T(8,128)S(1)} %copy-done.2), channel_id=1, source_target_pairs={{0,1},{1,0},{2,3},{3,2},{4,5},{5,4},{6,7},{7,6},{8,9},{9,8},{10,11... | collective-permute-start | bytes 786440 | tf_op jit(solution)/shard_map/ppermute | solution.py:314
  1.4 1.3 %copy-start.1 = (f32[1,1024,128]{2,1,0:T(8,128)S(1)}, f32[1,1024,128]{2,1,0:T(8,128)}, u32[]{:S(2)}) copy-start(f32[1,1024,128]{2,1,0:T(8,128)} %refs_0_.7) | copy-start | bytes 1572868
  3.3 12.8 %collective-permute-start.4 = (f32[128,256]{1,0:T(8,128)S(1)}, f32[128,256]{1,0:T(8,128)S(1)}, u32[]{:S(2)}, u32[]{:S(2)}) collective-permute-start(f32[128,256]{1,0:T(8,128)S(1)} %get-tuple-element.33.even_ref), channel_id=1, source_target_pairs={{0,2},{1,3},{2,0},{3,1},{4,6},{5,7},{6,4},{7,5},{8,10},{9,11},{10,... | collective-permute-start | bytes 393224 | tf_op jit(solution)/shard_map/ppermute | solution.py:323
  6.7 9.4 %collective-permute-start.5 = (f32[128,256]{1,0:T(8,128)S(1)}, f32[128,256]{1,0:T(8,128)S(1)}, u32[]{:S(2)}, u32[]{:S(2)}) collective-permute-start(f32[128,256]{1,0:T(8,128)S(1)} %get-tuple-element.34.odd_ref), channel_id=1, source_target_pairs={{0,1},{1,0},{2,4},{3,5},{4,2},{5,3},{6,8},{7,9},{8,6},{9,7},{10,12... | collective-permute-start | bytes 393224 | tf_op jit(solution)/shard_map/ppermute | solution.py:323
  6.8 7.7 %collective-permute-start = (f32[1,80,128]{2,1,0:T(8,128)S(1)}, f32[1,80,128]{2,1,0:T(8,128)S(1)}, u32[]{:S(2)}, u32[]{:S(2)}) collective-permute-start(f32[1,80,128]{2,1,0:T(8,128)S(1)} %get-tuple-element.26), channel_id=1, source_target_pairs={{0,2},{2,4},{4,6},{6,8},{8,10},{10,12},{12,14},{14,16},{16,18},{18... | collective-permute-start | bytes 122888 | tf_op jit(solution)/shard_map/ppermute | solution.py:335
  14.5 1.2 %collective-permute-start.3 = (f32[1,80,128]{2,1,0:T(8,128)S(1)}, f32[1,80,128]{2,1,0:T(8,128)S(1)}, u32[]{:S(2)}, u32[]{:S(2)}) collective-permute-start(f32[1,80,128]{2,1,0:T(8,128)S(1)} %collective-permute-done.refs_4_), channel_id=1, source_target_pairs={{0,1},{1,0},{2,3},{3,2},{4,5},{5,4},{6,7},{7,6},{8,9},{9,8},{10,11... | collective-permute-start | bytes 122888 | tf_op jit(solution)/shard_map/ppermute | solution.py:314

commit v12 on v11

--- a/solution.py
+++ b/solution.py
@@ -4,6 +4,7 @@
 from jax.experimental import pallas as pl
 from jax.experimental.pallas import tpu as pltpu
 from jax.sharding import PartitionSpec as P
+
 
 F32 = jnp.float32
 BF16 = jnp.bfloat16
@@ -48,14 +49,9 @@
     return [pltpu.with_memory_space_constraint(value, space) for value in values]
 
 
-def vmem_call(body, outs, name, *args):
-    return pl.pallas_call(
-        body,
-        out_shape=outs,
-        in_specs=[VMEM] * len(args),
-        out_specs=[VMEM] * len(outs),
-        name=name,
-        compiler_params=LEAN,
+def vmem_call(body, outs, *args):
+    return pl.pallas_call(
+        body, out_shape=outs, in_specs=[VMEM] * len(args), out_specs=[VMEM] * len(outs), compiler_params=LEAN
     )(*near(*args))
 
 
@@ -116,7 +112,7 @@
 
     table = shape(-(-groups // 8) * 8, lanes, dtype=jnp.int32)
     folded = shape(held, 5 * lanes // 8, lanes)
-    return vmem_call(body, [table, folded], "tables", mark, plan, tfactors)
+    return vmem_call(body, [table, folded], mark, plan, tfactors)
 
 
 def is_top(odd_round):
@@ -166,7 +162,7 @@
         pl.when(jnp.logical_not(top))(lambda: work(count - 1, strip))
 
     args = (kinds, x, *refls, *factors)
-    return vmem_call(body, [shape(strip, width)] * 2, "edge", *args)
+    return vmem_call(body, [shape(strip, width)] * 2, *args)
 
 
 def middle(x, refls, factors, kinds, step, coeffs):
@@ -264,12 +260,7 @@
         rests[0][...], rests[1][...] = ordered(top, low)
 
     rest, half = shape(strip, width), shape(strip, strip, dtype=BF16)
-    return vmem_call(
-        body,
-        [rest, rest, half, half, half, half],
-        "prepare",
-        *(kinds, *strips, *projs, *refls, *factors, *behind),
-    )
+    return vmem_call(body, [rest, rest, half, half, half, half], *(kinds, *strips, *projs, *refls, *factors, *behind))
 
 
 def finish(out, prepared, gots):

time: 17.2 us -> 17.2 us (level)
  no operation moved by 1% of the time
where the time goes in v12:
time: 17.2 us; the launch traced here: 17.1 us
  starting transfers between devices  7.03 us (41%)
  Pallas kernels  5.09 us (30%)
  waiting for transfers between devices  4.52 us (26%)
  local copies, waits for them, and re-layouts  0.38 us (2%)
    ppermute x1, waiting for transfers between devices, local(): lax.ppermute(end, 'row', [(r, (r + 1) % rows) for r in range(rows)])  3.02 us
    ppermute x2, starting transfers between devices, trade(): return lax.ppermute(block, ('row', 'col'), route)  2.99 us
    ppermute x1, starting transfers between devices, local(): lax.ppermute(end, 'row', [(r, (r + 1) % rows) for r in range(rows)])  2.97 us
    pallas_call x1, Pallas kernels, middle(): pl.pallas_call(body, out_shape=[shape(height, width)] + [shape(strip, wid...  1.66 us
    pallas_call x4, Pallas kernels, vmem_call(): pl.pallas_call(body, out_shape=outs, in_specs=[VMEM] * len(args), out_spe...  1.56 us
    ppermute x3, waiting for transfers between devices, around(): lax.ppermute(block, 'col', [(c, (c + shift) % columns) for c in range(col...  1.5 us
    ppermute x3, starting transfers between devices, around(): lax.ppermute(block, 'col', [(c, (c + shift) % columns) for c in range(col...  1.07 us
    pallas_call x1, Pallas kernels, finish(): pl.pallas_call(body, out_shape=jax.ShapeDtypeStruct((height, width), F32)...  0.97 us
  transfers between devices with their start and end apart: 6, of which 3 were waited for; matrix products, arithmetic and copies ran while one was open for 0% of the time, Pallas kernels for 21%

profile of v12, /device:TPU:0, one launch (start us, length us, event | category | flops | bytes accessed | tf_op | source)
XLA Modules:
  0.0 17.1 jit_solution(17683590073757003490)
XLA Ops:
  0.0 0.0 copy-start.2
  0.0 0.6 %collective-permute-start.1 = (f32[1,1024,128]{2,1,0:T(8,128)}, f32[1,1024,128]{2,1,0:T(8,128)S(1)}, u32[]{:S(2)}, u32[]{:S(2)}) collective-permute-start(f32[1,1024,128]{2,1,0:T(8,128)} %refs_0_.7), channel_id=1, source_target_pairs={{0,1},{1,0},{2,3},{3,2},{4,5},{5,4},{6,7},{7,6},{8,9},{9,8},{10,11... | collective-permute-start | bytes 1572872 | tf_op jit(solution)/shard_map/ppermute | solution.py:305
  0.6 0.4 %copy-done.2 = f32[1,4,128,128]{3,2,1,0:T(8,128)S(1)} copy-done((f32[1,4,128,128]{3,2,1,0:T(8,128)S(1)}, f32[1,4,128,128]{3,2,1,0:T(8,128)}, u32[]{:S(2)}) %copy-start.2) | copy-done | bytes 262168
  1.0 0.5 %collective-permute-start.2 = (f32[1,4,128,128]{3,2,1,0:T(8,128)S(1)}, f32[1,4,128,128]{3,2,1,0:T(8,128)S(1)}, u32[]{:S(2)}, u32[]{:S(2)}) collective-permute-start(f32[1,4,128,128]{3,2,1,0:T(8,128)S(1)} %copy-done.2), channel_id=1, source_target_pairs={{0,1},{1,0},{2,3},{3,2},{4,5},{5,4},{6,7},{7,6},{8,9},{9,8},{10,11... | collective-permute-start | bytes 786440 | tf_op jit(solution)/shard_map/ppermute | solution.py:305
  1.4 0.0 copy-done.3
  1.5 0.1 shard_map.46
  1.5 1.2 %collective-permute-done.2.refs_3_ = f32[1,4,128,128]{3,2,1,0:T(8,128)S(1)} collective-permute-done((f32[1,4,128,128]{3,2,1,0:T(8,128)S(1)}, f32[1,4,128,128]{3,2,1,0:T(8,128)S(1)}, u32[]{:S(2)}, u32[]{:S(2)}) %collective-permute-start.2) | collective-permute-done | bytes 262176 | tf_op jit(solution)/shard_map/ppermute | solution.py:305
  2.7 0.0 collective-permute-done.1.refs_1_
  2.7 0.0 copy-done
  2.7 0.0 copy-done.1
  2.7 0.5 %shard_map.47 = (f32[128,256]{1,0:T(8,128)S(1)}, f32[128,256]{1,0:T(8,128)S(1)}) custom-call(s32[8,128]{1,0:T(8,128)S(1)} %get-tuple-element.25.kinds_ref, f32[1024,256]{1,0:T(8,128)S(1)} %copy-done, f32[1,1024,128]{2,1,0:T(8,128)S(1)} %copy-done.1, f32[1,1024,128]{2,1,0:T(8,128)S(1)} %collective-permute-done.1.refs_1_, f32[1,4,128,128]{3,2,1,0:T(8,128)S(1)} %copy-done.2, ...), custom_call_target="tpu_custom_call" | custom-call | tf_op jit(solution)/shard_map/pallas_call | solution.py:53
  3.3 2.9 %collective-permute-start.4 = (f32[128,256]{1,0:T(8,128)S(1)}, f32[128,256]{1,0:T(8,128)S(1)}, u32[]{:S(2)}, u32[]{:S(2)}) collective-permute-start(f32[128,256]{1,0:T(8,128)S(1)} %get-tuple-element.33.even_ref), channel_id=1, source_target_pairs={{0,2},{1,3},{2,0},{3,1},{4,6},{5,7},{6,4},{7,5},{8,10},{9,11},{10,... | collective-permute-start | bytes 393224 | tf_op jit(solution)/shard_map/ppermute | solution.py:314
  6.2 0.5 %shard_map.48 = (f32[128,256]{1,0:T(8,128)S(1)}, f32[128,256]{1,0:T(8,128)S(1)}) custom-call(s32[8,128]{1,0:T(8,128)S(1)} %get-tuple-element.25.kinds_ref, f32[1024,256]{1,0:T(8,128)S(1)} %copy-done, f32[1,1024,128]{2,1,0:T(8,128)S(1)} %copy-done.1, f32[1,1024,128]{2,1,0:T(8,128)S(1)} %collective-permute-done.1.refs_1_, f32[1,4,128,128]{3,2,1,0:T(8,128)S(1)} %copy-done.2, ...), custom_call_target="tpu_custom_call" | custom-call | tf_op jit(solution)/shard_map/pallas_call | solution.py:53
  6.7 0.1 collective-permute-start.5
  6.8 3.0 %collective-permute-start = (f32[1,80,128]{2,1,0:T(8,128)S(1)}, f32[1,80,128]{2,1,0:T(8,128)S(1)}, u32[]{:S(2)}, u32[]{:S(2)}) collective-permute-start(f32[1,80,128]{2,1,0:T(8,128)S(1)} %get-tuple-element.26), channel_id=1, source_target_pairs={{0,2},{2,4},{4,6},{6,8},{8,10},{10,12},{12,14},{14,16},{16,18},{18... | collective-permute-start | bytes 122888 | tf_op jit(solution)/shard_map/ppermute | solution.py:326
  9.8 1.7 %middle.1 = (f32[1024,256]{1,0:T(8,128)S(1)}, f32[128,256]{1,0:T(8,128)S(1)}, f32[128,256]{1,0:T(8,128)S(1)}) custom-call(s32[8,128]{1,0:T(8,128)S(1)} %get-tuple-element.25.kinds_ref, f32[1024,256]{1,0:T(8,128)S(1)} %copy-done, f32[128,256]{1,0:T(8,128)S(1)} %get-tuple-element.28.even_coeff, f32[128,256]{1,0:T(8,128)S(1)} %get-tuple-element.29.odd_coeff, ...), custom_call_target="tpu_custom_call" | custom-call | tf_op jit(solution)/shard_map/middle/pallas_call | solution.py:203
  11.4 3.0 %collective-permute-done.refs_4_ = f32[1,80,128]{2,1,0:T(8,128)S(1)} collective-permute-done((f32[1,80,128]{2,1,0:T(8,128)S(1)}, f32[1,80,128]{2,1,0:T(8,128)S(1)}, u32[]{:S(2)}, u32[]{:S(2)}) %collective-permute-start) | collective-permute-done | bytes 40992 | tf_op jit(solution)/shard_map/ppermute | solution.py:326
  14.5 0.0 collective-permute-start.3
  14.5 0.9 %store.1.refs_8_ = f32[1024,256]{1,0:T(8,128)} custom-call(f32[1024,256]{1,0:T(8,128)S(1)} %get-tuple-element.42.work_ref), custom_call_target="tpu_custom_call" | custom-call | tf_op jit(solution)/shard_map/store/pallas_call | solution.py:223
  15.4 0.3 %collective-permute-done.3.refs_5_ = f32[1,80,128]{2,1,0:T(8,128)S(1)} collective-permute-done((f32[1,80,128]{2,1,0:T(8,128)S(1)}, f32[1,80,128]{2,1,0:T(8,128)S(1)}, u32[]{:S(2)}, u32[]{:S(2)}) %collective-permute-start.3) | collective-permute-done | bytes 40992 | tf_op jit(solution)/shard_map/ppermute | solution.py:305
  15.7 0.4 %shard_map.49 = (f32[128,256]{1,0:T(8,128)S(1)}, f32[128,256]{1,0:T(8,128)S(1)}, bf16[128,128]{1,0:T(8,128)(2,1)S(1)}, bf16[128,128]{1,0:T(8,128)(2,1)S(1)}, bf1...) custom-call(s32[8,128]{1,0:T(8,128)S(1)} %get-tuple-element.25.kinds_ref, ...), custom_call_target="tpu_custom_call" | custom-call | tf_op jit(solution)/shard_map/pallas_call | solution.py:53
  16.1 0.0 collective-permute-done.4.refs_6_
  16.1 0.0 collective-permute-done.5.refs_7_
  16.1 1.0 %finish.1 = f32[1024,256]{1,0:T(8,128)} custom-call(f32[128,256]{1,0:T(8,128)S(1)} %get-tuple-element.36.refs_0_, f32[128,256]{1,0:T(8,128)S(1)} %get-tuple-element.37.refs_1_, bf16[128,128]{1,0:T(8,128)(2,1)S(1)} %get-tuple-element.38.refs_2_, bf16[128,128]{1,0:T(8,128)(2,1)S(1)} %get-tuple-element.39.refs_3_, ...), custom_call_target="tpu_custom_call", output_to_operand_aliasing={{}: (8, {})} | custom-call | tf_op jit(solution)/shard_map/finish/pallas_call | solution.py:288
  (5 shorter events, 0.0 us)
Async XLA Ops:
  0.0 0.9 %copy-start.2 = (f32[1,4,128,128]{3,2,1,0:T(8,128)S(1)}, f32[1,4,128,128]{3,2,1,0:T(8,128)}, u32[]{:S(2)}) copy-start(f32[1,4,128,128]{3,2,1,0:T(8,128)} %refs_2_.9) | copy-start | bytes 786436
  0.0 2.7 %copy-start = (f32[1024,256]{1,0:T(8,128)S(1)}, f32[1024,256]{1,0:T(8,128)}, u32[]{:S(2)}) copy-start(f32[1024,256]{1,0:T(8,128)} %x_ref.5) | copy-start | bytes 3145732
  0.0 1.4 %copy-start.3 = (s32[2]{0:T(128)S(1)}, s32[2]{0:T(128)}, u32[]{:S(2)}) copy-start(s32[2]{0:T(128)} %param.7) | copy-start | bytes 28
  0.0 2.7 %collective-permute-start.1 = (f32[1,1024,128]{2,1,0:T(8,128)}, f32[1,1024,128]{2,1,0:T(8,128)S(1)}, u32[]{:S(2)}, u32[]{:S(2)}) collective-permute-start(f32[1,1024,128]{2,1,0:T(8,128)} %refs_0_.7), channel_id=1, source_target_pairs={{0,1},{1,0},{2,3},{3,2},{4,5},{5,4},{6,7},{7,6},{8,9},{9,8},{10,11... | collective-permute-start | bytes 1572872 | tf_op jit(solution)/shard_map/ppermute | solution.py:305
  1.0 1.8 %collective-permute-start.2 = (f32[1,4,128,128]{3,2,1,0:T(8,128)S(1)}, f32[1,4,128,128]{3,2,1,0:T(8,128)S(1)}, u32[]{:S(2)}, u32[]{:S(2)}) collective-permute-start(f32[1,4,128,128]{3,2,1,0:T(8,128)S(1)} %copy-done.2), channel_id=1, source_target_pairs={{0,1},{1,0},{2,3},{3,2},{4,5},{5,4},{6,7},{7,6},{8,9},{9,8},{10,11... | collective-permute-start | bytes 786440 | tf_op jit(solution)/shard_map/ppermute | solution.py:305
  1.4 1.3 %copy-start.1 = (f32[1,1024,128]{2,1,0:T(8,128)S(1)}, f32[1,1024,128]{2,1,0:T(8,128)}, u32[]{:S(2)}) copy-start(f32[1,1024,128]{2,1,0:T(8,128)} %refs_0_.7) | copy-start | bytes 1572868
  3.3 12.8 %collective-permute-start.4 = (f32[128,256]{1,0:T(8,128)S(1)}, f32[128,256]{1,0:T(8,128)S(1)}, u32[]{:S(2)}, u32[]{:S(2)}) collective-permute-start(f32[128,256]{1,0:T(8,128)S(1)} %get-tuple-element.33.even_ref), channel_id=1, source_target_pairs={{0,2},{1,3},{2,0},{3,1},{4,6},{5,7},{6,4},{7,5},{8,10},{9,11},{10,... | collective-permute-start | bytes 393224 | tf_op jit(solution)/shard_map/ppermute | solution.py:314
  6.7 9.4 %collective-permute-start.5 = (f32[128,256]{1,0:T(8,128)S(1)}, f32[128,256]{1,0:T(8,128)S(1)}, u32[]{:S(2)}, u32[]{:S(2)}) collective-permute-start(f32[128,256]{1,0:T(8,128)S(1)} %get-tuple-element.34.odd_ref), channel_id=1, source_target_pairs={{0,1},{1,0},{2,4},{3,5},{4,2},{5,3},{6,8},{7,9},{8,6},{9,7},{10,12... | collective-permute-start | bytes 393224 | tf_op jit(solution)/shard_map/ppermute | solution.py:314
  6.8 7.7 %collective-permute-start = (f32[1,80,128]{2,1,0:T(8,128)S(1)}, f32[1,80,128]{2,1,0:T(8,128)S(1)}, u32[]{:S(2)}, u32[]{:S(2)}) collective-permute-start(f32[1,80,128]{2,1,0:T(8,128)S(1)} %get-tuple-element.26), channel_id=1, source_target_pairs={{0,2},{2,4},{4,6},{6,8},{8,10},{10,12},{12,14},{14,16},{16,18},{18... | collective-permute-start | bytes 122888 | tf_op jit(solution)/shard_map/ppermute | solution.py:326
  14.5 1.2 %collective-permute-start.3 = (f32[1,80,128]{2,1,0:T(8,128)S(1)}, f32[1,80,128]{2,1,0:T(8,128)S(1)}, u32[]{:S(2)}, u32[]{:S(2)}) collective-permute-start(f32[1,80,128]{2,1,0:T(8,128)S(1)} %collective-permute-done.refs_4_), channel_id=1, source_target_pairs={{0,1},{1,0},{2,3},{3,2},{4,5},{5,4},{6,7},{7,6},{8,9},{9,8},{10,11... | collective-permute-start | bytes 122888 | tf_op jit(solution)/shard_map/ppermute | solution.py:305

commit v13 on v12

--- a/solution.py
+++ b/solution.py
@@ -263,38 +263,50 @@
     return vmem_call(body, [rest, rest, half, half, half, half], *(kinds, *strips, *projs, *refls, *factors, *behind))
 
 
-def finish(out, prepared, gots):
+def settled(odd_round, rest, high, low, got):
+    row, last = lax.axis_index("row"), lax.axis_size("row") - 1
+    present = jnp.where(is_top(odd_round), row > 0, row < last)
+    other = jnp.where(present, got[...], jnp.zeros_like(got))
+    return rest[...] - product((high[...], low[...]), split(other))
+
+
+def settle(rest, high, low, got):
+    def body(*refs):
+        refs[-1][...] = settled(False, *refs[:-1])
+
+    return vmem_call(body, [shape(*rest.shape)], rest, high, low, got)[0]
+
+
+def finish(out, even, rest, high, low, got):
     height, width = out.shape
-    strip = gots[0].shape[0]
-
-    def body(*refs):
-        rests, highs, lows, gots = refs[:2], refs[2:4], refs[4:6], refs[6:8]
-        out_ref, new_ref, sem = refs[9:]
-        row, last = lax.axis_index("row"), lax.axis_size("row") - 1
-        copies = []
-        for at in range(2):
-            top = is_top(at == 1)
-            present = jnp.where(top, row > 0, row < last)
-            other = jnp.where(present, gots[at][...], jnp.zeros_like(gots[at]))
-            weight = highs[at][...], lows[at][...]
-            new_ref[at] = rests[at][...] - product(weight, split(other))
-            start = pl.multiple_of(jnp.where(top, 0, height - strip), strip)
+    strip = rest.shape[0]
+
+    def body(even_ref, *refs):
+        out_ref, new_ref, sem = refs[5:]
+
+        def write(odd_round, source):
+            start = pl.multiple_of(jnp.where(is_top(odd_round), 0, height - strip), strip)
             rows = out_ref.at[pl.ds(start, strip), :]
-            copies.append(pltpu.make_async_copy(new_ref.at[at], rows, sem.at[at]))
-            copies[-1].start()
-        for copy in copies:
-            copy.wait()
+            copy = pltpu.make_async_copy(source, rows, sem.at[int(odd_round)])
+            copy.start()
+            return copy
+
+        first = write(False, even_ref)
+        new_ref[...] = settled(True, *refs[:4])
+        second = write(True, new_ref)
+        first.wait()
+        second.wait()
 
     return pl.pallas_call(
         body,
         out_shape=jax.ShapeDtypeStruct((height, width), F32),
-        in_specs=[VMEM] * 8 + [ANY],
+        in_specs=[VMEM] * 5 + [ANY],
         out_specs=ANY,
-        scratch_shapes=[pltpu.VMEM((2, strip, width), F32), pltpu.SemaphoreType.DMA((2,))],
-        input_output_aliases={8: 0},
+        scratch_shapes=[pltpu.VMEM((strip, width), F32), pltpu.SemaphoreType.DMA((2,))],
+        input_output_aliases={5: 0},
         name="finish",
         compiler_params=LEAN,
-    )(*near(*prepared, *gots), out)
+    )(*near(even, rest, high, low, got), out)
 
 
 def local(vectors, reflectors, tfactors, plan):
@@ -338,7 +350,8 @@
             behinds = everyone(behind, behind)
         out = store(work, strip)
         prepared = prepare(refls, factors, behinds, kinds, step, strips, projs)
-        current = finish(out, prepared, gots)
+        even = settle(*prepared[::2], gots[0])
+        current = finish(out, even, *prepared[1::2], gots[1])
     return current
 
 

time: 17.2 us -> 17.3 us (level)
    pallas_call x4 -> x5, Pallas kernels: 1.56 us -> 1.76 us  [vmem_call(): pl.pallas_call(body, out_shape=outs, in_specs=[VMEM] * len(args), out_spe...]
  transfers between devices with their start and end apart: 6 -> 6, of which waited for: 3 -> 3; matrix products, arithmetic and copies ran while one was open for 0% -> 0% of each run, Pallas kernels for 21% -> 22%
where the time goes in v13:
time: 17.3 us; the launch traced here: 17.2 us
  starting transfers between devices  7.03 us (41%)
  Pallas kernels  5.19 us (30%)
  waiting for transfers between devices  4.52 us (26%)
  local copies, waits for them, and re-layouts  0.38 us (2%)
    ppermute x1, waiting for transfers between devices, local(): lax.ppermute(end, 'row', [(r, (r + 1) % rows) for r in range(rows)])  3.02 us
    ppermute x2, starting transfers between devices, trade(): return lax.ppermute(block, ('row', 'col'), route)  2.99 us
    ppermute x1, starting transfers between devices, local(): lax.ppermute(end, 'row', [(r, (r + 1) % rows) for r in range(rows)])  2.97 us
    pallas_call x5, Pallas kernels, vmem_call(): pl.pallas_call(body, out_shape=outs, in_specs=[VMEM] * len(args), out_spe...  1.76 us
    pallas_call x1, Pallas kernels, middle(): pl.pallas_call(body, out_shape=[shape(height, width)] + [shape(strip, wid...  1.66 us
    ppermute x3, waiting for transfers between devices, around(): lax.ppermute(block, 'col', [(c, (c + shift) % columns) for c in range(col...  1.5 us
    ppermute x3, starting transfers between devices, around(): lax.ppermute(block, 'col', [(c, (c + shift) % columns) for c in range(col...  1.07 us
    pallas_call x1, Pallas kernels, store(): pl.pallas_call(body, out_shape=jax.ShapeDtypeStruct((height, width), F32)...  0.89 us
  transfers between devices with their start and end apart: 6, of which 3 were waited for; matrix products, arithmetic and copies ran while one was open for 0% of the time, Pallas kernels for 22%

profile of v13, /device:TPU:0, one launch (start us, length us, event | category | flops | bytes accessed | tf_op | source)
XLA Modules:
  0.0 17.2 jit_solution(3300339757098155615)
XLA Ops:
  0.0 0.6 %collective-permute-start.1 = (f32[1,1024,128]{2,1,0:T(8,128)}, f32[1,1024,128]{2,1,0:T(8,128)S(1)}, u32[]{:S(2)}, u32[]{:S(2)}) collective-permute-start(f32[1,1024,128]{2,1,0:T(8,128)} %refs_0_.7), channel_id=1, source_target_pairs={{0,1},{1,0},{2,3},{3,2},{4,5},{5,4},{6,7},{7,6},{8,9},{9,8},{10,11... | collective-permute-start | bytes 1572872 | tf_op jit(solution)/shard_map/ppermute | solution.py:317
  0.6 0.4 %copy-done.2 = f32[1,4,128,128]{3,2,1,0:T(8,128)S(1)} copy-done((f32[1,4,128,128]{3,2,1,0:T(8,128)S(1)}, f32[1,4,128,128]{3,2,1,0:T(8,128)}, u32[]{:S(2)}) %copy-start.2) | copy-done | bytes 262168
  1.0 0.5 %collective-permute-start.2 = (f32[1,4,128,128]{3,2,1,0:T(8,128)S(1)}, f32[1,4,128,128]{3,2,1,0:T(8,128)S(1)}, u32[]{:S(2)}, u32[]{:S(2)}) collective-permute-start(f32[1,4,128,128]{3,2,1,0:T(8,128)S(1)} %copy-done.2), channel_id=1, source_target_pairs={{0,1},{1,0},{2,3},{3,2},{4,5},{5,4},{6,7},{7,6},{8,9},{9,8},{10,11... | collective-permute-start | bytes 786440 | tf_op jit(solution)/shard_map/ppermute | solution.py:317
  1.4 0.0 copy-done.3
  1.5 0.1 shard_map.46
  1.5 1.2 %collective-permute-done.2.refs_3_ = f32[1,4,128,128]{3,2,1,0:T(8,128)S(1)} collective-permute-done((f32[1,4,128,128]{3,2,1,0:T(8,128)S(1)}, f32[1,4,128,128]{3,2,1,0:T(8,128)S(1)}, u32[]{:S(2)}, u32[]{:S(2)}) %collective-permute-start.2) | collective-permute-done | bytes 262176 | tf_op jit(solution)/shard_map/ppermute | solution.py:317
  2.7 0.0 collective-permute-done.1.refs_1_
  2.7 0.0 copy-done
  2.7 0.0 copy-done.1
  2.7 0.5 %shard_map.47 = (f32[128,256]{1,0:T(8,128)S(1)}, f32[128,256]{1,0:T(8,128)S(1)}) custom-call(s32[8,128]{1,0:T(8,128)S(1)} %get-tuple-element.25.kinds_ref, f32[1024,256]{1,0:T(8,128)S(1)} %copy-done, f32[1,1024,128]{2,1,0:T(8,128)S(1)} %copy-done.1, f32[1,1024,128]{2,1,0:T(8,128)S(1)} %collective-permute-done.1.refs_1_, f32[1,4,128,128]{3,2,1,0:T(8,128)S(1)} %copy-done.2, ...), custom_call_target="tpu_custom_call" | custom-call | tf_op jit(solution)/shard_map/pallas_call | solution.py:53
  3.3 2.9 %collective-permute-start.4 = (f32[128,256]{1,0:T(8,128)S(1)}, f32[128,256]{1,0:T(8,128)S(1)}, u32[]{:S(2)}, u32[]{:S(2)}) collective-permute-start(f32[128,256]{1,0:T(8,128)S(1)} %get-tuple-element.33.even_ref), channel_id=1, source_target_pairs={{0,2},{1,3},{2,0},{3,1},{4,6},{5,7},{6,4},{7,5},{8,10},{9,11},{10,... | collective-permute-start | bytes 393224 | tf_op jit(solution)/shard_map/ppermute | solution.py:326
  6.2 0.5 %shard_map.48 = (f32[128,256]{1,0:T(8,128)S(1)}, f32[128,256]{1,0:T(8,128)S(1)}) custom-call(s32[8,128]{1,0:T(8,128)S(1)} %get-tuple-element.25.kinds_ref, f32[1024,256]{1,0:T(8,128)S(1)} %copy-done, f32[1,1024,128]{2,1,0:T(8,128)S(1)} %copy-done.1, f32[1,1024,128]{2,1,0:T(8,128)S(1)} %collective-permute-done.1.refs_1_, f32[1,4,128,128]{3,2,1,0:T(8,128)S(1)} %copy-done.2, ...), custom_call_target="tpu_custom_call" | custom-call | tf_op jit(solution)/shard_map/pallas_call | solution.py:53
  6.7 0.1 collective-permute-start.5
  6.8 3.0 %collective-permute-start = (f32[1,80,128]{2,1,0:T(8,128)S(1)}, f32[1,80,128]{2,1,0:T(8,128)S(1)}, u32[]{:S(2)}, u32[]{:S(2)}) collective-permute-start(f32[1,80,128]{2,1,0:T(8,128)S(1)} %get-tuple-element.26), channel_id=1, source_target_pairs={{0,2},{2,4},{4,6},{6,8},{8,10},{10,12},{12,14},{14,16},{16,18},{18... | collective-permute-start | bytes 122888 | tf_op jit(solution)/shard_map/ppermute | solution.py:338
  9.8 1.7 %middle.1 = (f32[1024,256]{1,0:T(8,128)S(1)}, f32[128,256]{1,0:T(8,128)S(1)}, f32[128,256]{1,0:T(8,128)S(1)}) custom-call(s32[8,128]{1,0:T(8,128)S(1)} %get-tuple-element.25.kinds_ref, f32[1024,256]{1,0:T(8,128)S(1)} %copy-done, f32[128,256]{1,0:T(8,128)S(1)} %get-tuple-element.28.even_coeff, f32[128,256]{1,0:T(8,128)S(1)} %get-tuple-element.29.odd_coeff, ...), custom_call_target="tpu_custom_call" | custom-call | tf_op jit(solution)/shard_map/middle/pallas_call | solution.py:203
  11.4 3.0 %collective-permute-done.refs_4_ = f32[1,80,128]{2,1,0:T(8,128)S(1)} collective-permute-done((f32[1,80,128]{2,1,0:T(8,128)S(1)}, f32[1,80,128]{2,1,0:T(8,128)S(1)}, u32[]{:S(2)}, u32[]{:S(2)}) %collective-permute-start) | collective-permute-done | bytes 40992 | tf_op jit(solution)/shard_map/ppermute | solution.py:338
  14.5 0.0 collective-permute-start.3
  14.5 0.9 %store.1.refs_4_ = f32[1024,256]{1,0:T(8,128)} custom-call(f32[1024,256]{1,0:T(8,128)S(1)} %get-tuple-element.42.work_ref), custom_call_target="tpu_custom_call" | custom-call | tf_op jit(solution)/shard_map/store/pallas_call | solution.py:223
  15.4 0.3 %collective-permute-done.3.refs_5_ = f32[1,80,128]{2,1,0:T(8,128)S(1)} collective-permute-done((f32[1,80,128]{2,1,0:T(8,128)S(1)}, f32[1,80,128]{2,1,0:T(8,128)S(1)}, u32[]{:S(2)}, u32[]{:S(2)}) %collective-permute-start.3) | collective-permute-done | bytes 40992 | tf_op jit(solution)/shard_map/ppermute | solution.py:317
  15.7 0.4 %shard_map.49 = (f32[128,256]{1,0:T(8,128)S(1)}, f32[128,256]{1,0:T(8,128)S(1)}, bf16[128,128]{1,0:T(8,128)(2,1)S(1)}, bf16[128,128]{1,0:T(8,128)(2,1)S(1)}, bf1...) custom-call(s32[8,128]{1,0:T(8,128)S(1)} %get-tuple-element.25.kinds_ref, ...), custom_call_target="tpu_custom_call" | custom-call | tf_op jit(solution)/shard_map/pallas_call | solution.py:53
  16.1 0.0 collective-permute-done.4.refs_3_
  16.1 0.2 %shard_map.50.even_ref = f32[128,256]{1,0:T(8,128)S(1)} custom-call(f32[128,256]{1,0:T(8,128)S(1)} %get-tuple-element.36.refs_0_, bf16[128,128]{1,0:T(8,128)(2,1)S(1)} %get-tuple-element.37.refs_1_, bf16[128,128]{1,0:T(8,128)(2,1)S(1)} %get-tuple-element.38.refs_2_, f32[128,256]{1,0:T(8,128)S(1)} %collective-permute-done.4.refs_3_), custom_call_target="tpu_custom_call" | custom-call | tf_op jit(solution)/shard_map/pallas_call | solution.py:53
  16.3 0.0 collective-permute-done.5.refs_3_
  16.3 0.9 %finish.1 = f32[1024,256]{1,0:T(8,128)} custom-call(f32[128,256]{1,0:T(8,128)S(1)} %shard_map.50.even_ref, f32[128,256]{1,0:T(8,128)S(1)} %get-tuple-element.39.refs_0_, bf16[128,128]{1,0:T(8,128)(2,1)S(1)} %get-tuple-element.40.refs_1_, bf16[128,128]{1,0:T(8,128)(2,1)S(1)} %get-tuple-element.41.refs_2_, ...), custom_call_target="tpu_custom_call", output_to_operand_aliasing={{}: (5, {})} | custom-call | tf_op jit(solution)/shard_map/finish/pallas_call | solution.py:300
  (6 shorter events, 0.0 us)
Async XLA Ops:
  0.0 0.9 %copy-start.2 = (f32[1,4,128,128]{3,2,1,0:T(8,128)S(1)}, f32[1,4,128,128]{3,2,1,0:T(8,128)}, u32[]{:S(2)}) copy-start(f32[1,4,128,128]{3,2,1,0:T(8,128)} %refs_2_.9) | copy-start | bytes 786436
  0.0 2.7 %copy-start = (f32[1024,256]{1,0:T(8,128)S(1)}, f32[1024,256]{1,0:T(8,128)}, u32[]{:S(2)}) copy-start(f32[1024,256]{1,0:T(8,128)} %x_ref.5) | copy-start | bytes 3145732
  0.0 1.4 %copy-start.3 = (s32[2]{0:T(128)S(1)}, s32[2]{0:T(128)}, u32[]{:S(2)}) copy-start(s32[2]{0:T(128)} %param.7) | copy-start | bytes 28
  0.0 2.7 %collective-permute-start.1 = (f32[1,1024,128]{2,1,0:T(8,128)}, f32[1,1024,128]{2,1,0:T(8,128)S(1)}, u32[]{:S(2)}, u32[]{:S(2)}) collective-permute-start(f32[1,1024,128]{2,1,0:T(8,128)} %refs_0_.7), channel_id=1, source_target_pairs={{0,1},{1,0},{2,3},{3,2},{4,5},{5,4},{6,7},{7,6},{8,9},{9,8},{10,11... | collective-permute-start | bytes 1572872 | tf_op jit(solution)/shard_map/ppermute | solution.py:317
  1.0 1.8 %collective-permute-start.2 = (f32[1,4,128,128]{3,2,1,0:T(8,128)S(1)}, f32[1,4,128,128]{3,2,1,0:T(8,128)S(1)}, u32[]{:S(2)}, u32[]{:S(2)}) collective-permute-start(f32[1,4,128,128]{3,2,1,0:T(8,128)S(1)} %copy-done.2), channel_id=1, source_target_pairs={{0,1},{1,0},{2,3},{3,2},{4,5},{5,4},{6,7},{7,6},{8,9},{9,8},{10,11... | collective-permute-start | bytes 786440 | tf_op jit(solution)/shard_map/ppermute | solution.py:317
  1.4 1.3 %copy-start.1 = (f32[1,1024,128]{2,1,0:T(8,128)S(1)}, f32[1,1024,128]{2,1,0:T(8,128)}, u32[]{:S(2)}) copy-start(f32[1,1024,128]{2,1,0:T(8,128)} %refs_0_.7) | copy-start | bytes 1572868
  3.3 12.8 %collective-permute-start.4 = (f32[128,256]{1,0:T(8,128)S(1)}, f32[128,256]{1,0:T(8,128)S(1)}, u32[]{:S(2)}, u32[]{:S(2)}) collective-permute-start(f32[128,256]{1,0:T(8,128)S(1)} %get-tuple-element.33.even_ref), channel_id=1, source_target_pairs={{0,2},{1,3},{2,0},{3,1},{4,6},{5,7},{6,4},{7,5},{8,10},{9,11},{10,... | collective-permute-start | bytes 393224 | tf_op jit(solution)/shard_map/ppermute | solution.py:326
  6.7 9.6 %collective-permute-start.5 = (f32[128,256]{1,0:T(8,128)S(1)}, f32[128,256]{1,0:T(8,128)S(1)}, u32[]{:S(2)}, u32[]{:S(2)}) collective-permute-start(f32[128,256]{1,0:T(8,128)S(1)} %get-tuple-element.34.odd_ref), channel_id=1, source_target_pairs={{0,1},{1,0},{2,4},{3,5},{4,2},{5,3},{6,8},{7,9},{8,6},{9,7},{10,12... | collective-permute-start | bytes 393224 | tf_op jit(solution)/shard_map/ppermute | solution.py:326
  6.8 7.7 %collective-permute-start = (f32[1,80,128]{2,1,0:T(8,128)S(1)}, f32[1,80,128]{2,1,0:T(8,128)S(1)}, u32[]{:S(2)}, u32[]{:S(2)}) collective-permute-start(f32[1,80,128]{2,1,0:T(8,128)S(1)} %get-tuple-element.26), channel_id=1, source_target_pairs={{0,2},{2,4},{4,6},{6,8},{8,10},{10,12},{12,14},{14,16},{16,18},{18... | collective-permute-start | bytes 122888 | tf_op jit(solution)/shard_map/ppermute | solution.py:338
  14.5 1.2 %collective-permute-start.3 = (f32[1,80,128]{2,1,0:T(8,128)S(1)}, f32[1,80,128]{2,1,0:T(8,128)S(1)}, u32[]{:S(2)}, u32[]{:S(2)}) collective-permute-start(f32[1,80,128]{2,1,0:T(8,128)S(1)} %collective-permute-done.refs_4_), channel_id=1, source_target_pairs={{0,1},{1,0},{2,3},{3,2},{4,5},{5,4},{6,7},{7,6},{8,9},{9,8},{10,11... | collective-permute-start | bytes 122888 | tf_op jit(solution)/shard_map/ppermute | solution.py:317

commit v14 on v13

--- a/solution.py
+++ b/solution.py
@@ -284,25 +284,31 @@
     def body(even_ref, *refs):
         out_ref, new_ref, sem = refs[5:]
 
-        def write(odd_round, source):
+        def write(odd_round, source, lanes, at):
             start = pl.multiple_of(jnp.where(is_top(odd_round), 0, height - strip), strip)
-            rows = out_ref.at[pl.ds(start, strip), :]
-            copy = pltpu.make_async_copy(source, rows, sem.at[int(odd_round)])
+            rows = out_ref.at[pl.ds(start, strip), lanes]
+            copy = pltpu.make_async_copy(source.at[:, lanes], rows, sem.at[at])
             copy.start()
             return copy
 
-        first = write(False, even_ref)
-        new_ref[...] = settled(True, *refs[:4])
-        second = write(True, new_ref)
-        first.wait()
-        second.wait()
+        copies = [write(False, even_ref, pl.ds(0, width), 0)]
+        for at in range(width // LANES):
+            lanes = pl.ds(at * LANES, LANES)
+            got_ref = refs[3].at[:, lanes]
+            new_ref[:, lanes] = settled(True, refs[0].at[:, lanes], *refs[1:3], got_ref)
+            copies.append(write(True, new_ref, lanes, at + 1))
+        for copy in copies:
+            copy.wait()
 
     return pl.pallas_call(
         body,
         out_shape=jax.ShapeDtypeStruct((height, width), F32),
         in_specs=[VMEM] * 5 + [ANY],
         out_specs=ANY,
-        scratch_shapes=[pltpu.VMEM((strip, width), F32), pltpu.SemaphoreType.DMA((2,))],
+        scratch_shapes=[
+            pltpu.VMEM((strip, width), F32),
+            pltpu.SemaphoreType.DMA((1 + width // LANES,)),
+        ],
         input_output_aliases={5: 0},
         name="finish",
         compiler_params=LEAN,

time: 17.3 us -> 17.4 us (level)
  no operation moved by 1% of the time
where the time goes in v14:
time: 17.4 us; the launch traced here: 17.2 us
  starting transfers between devices  7.03 us (40%)
  Pallas kernels  5.22 us (30%)
  waiting for transfers between devices  4.52 us (26%)
  local copies, waits for them, and re-layouts  0.38 us (2%)
    ppermute x1, waiting for transfers between devices, local(): lax.ppermute(end, 'row', [(r, (r + 1) % rows) for r in range(rows)])  3.02 us
    ppermute x2, starting transfers between devices, trade(): return lax.ppermute(block, ('row', 'col'), route)  2.99 us
    ppermute x1, starting transfers between devices, local(): lax.ppermute(end, 'row', [(r, (r + 1) % rows) for r in range(rows)])  2.97 us
    pallas_call x5, Pallas kernels, vmem_call(): pl.pallas_call(body, out_shape=outs, in_specs=[VMEM] * len(args), out_spe...  1.76 us
    pallas_call x1, Pallas kernels, middle(): pl.pallas_call(body, out_shape=[shape(height, width)] + [shape(strip, wid...  1.66 us
    ppermute x3, waiting for transfers between devices, around(): lax.ppermute(block, 'col', [(c, (c + shift) % columns) for c in range(col...  1.5 us
    ppermute x3, starting transfers between devices, around(): lax.ppermute(block, 'col', [(c, (c + shift) % columns) for c in range(col...  1.07 us
    pallas_call x1, Pallas kernels, finish(): pl.pallas_call(body, out_shape=jax.ShapeDtypeStruct((height, width), F32)...  0.9 us
  transfers between devices with their start and end apart: 6, of which 3 were waited for; matrix products, arithmetic and copies ran while one was open for 0% of the time, Pallas kernels for 22%

profile of v14, /device:TPU:0, one launch (start us, length us, event | category | flops | bytes accessed | tf_op | source)
XLA Modules:
  0.0 17.2 jit_solution(6694091999191029256)
XLA Ops:
  0.0 0.6 %collective-permute-start.1 = (f32[1,1024,128]{2,1,0:T(8,128)}, f32[1,1024,128]{2,1,0:T(8,128)S(1)}, u32[]{:S(2)}, u32[]{:S(2)}) collective-permute-start(f32[1,1024,128]{2,1,0:T(8,128)} %refs_0_.7), channel_id=1, source_target_pairs={{0,1},{1,0},{2,3},{3,2},{4,5},{5,4},{6,7},{7,6},{8,9},{9,8},{10,11... | collective-permute-start | bytes 1572872 | tf_op jit(solution)/shard_map/ppermute | solution.py:323
  0.6 0.4 %copy-done.2 = f32[1,4,128,128]{3,2,1,0:T(8,128)S(1)} copy-done((f32[1,4,128,128]{3,2,1,0:T(8,128)S(1)}, f32[1,4,128,128]{3,2,1,0:T(8,128)}, u32[]{:S(2)}) %copy-start.2) | copy-done | bytes 262168
  1.0 0.5 %collective-permute-start.2 = (f32[1,4,128,128]{3,2,1,0:T(8,128)S(1)}, f32[1,4,128,128]{3,2,1,0:T(8,128)S(1)}, u32[]{:S(2)}, u32[]{:S(2)}) collective-permute-start(f32[1,4,128,128]{3,2,1,0:T(8,128)S(1)} %copy-done.2), channel_id=1, source_target_pairs={{0,1},{1,0},{2,3},{3,2},{4,5},{5,4},{6,7},{7,6},{8,9},{9,8},{10,11... | collective-permute-start | bytes 786440 | tf_op jit(solution)/shard_map/ppermute | solution.py:323
  1.4 0.0 copy-done.3
  1.5 0.1 shard_map.46
  1.5 1.2 %collective-permute-done.2.refs_3_ = f32[1,4,128,128]{3,2,1,0:T(8,128)S(1)} collective-permute-done((f32[1,4,128,128]{3,2,1,0:T(8,128)S(1)}, f32[1,4,128,128]{3,2,1,0:T(8,128)S(1)}, u32[]{:S(2)}, u32[]{:S(2)}) %collective-permute-start.2) | collective-permute-done | bytes 262176 | tf_op jit(solution)/shard_map/ppermute | solution.py:323
  2.7 0.0 collective-permute-done.1.refs_1_
  2.7 0.0 copy-done
  2.7 0.0 copy-done.1
  2.7 0.5 %shard_map.47 = (f32[128,256]{1,0:T(8,128)S(1)}, f32[128,256]{1,0:T(8,128)S(1)}) custom-call(s32[8,128]{1,0:T(8,128)S(1)} %get-tuple-element.25.kinds_ref, f32[1024,256]{1,0:T(8,128)S(1)} %copy-done, f32[1,1024,128]{2,1,0:T(8,128)S(1)} %copy-done.1, f32[1,1024,128]{2,1,0:T(8,128)S(1)} %collective-permute-done.1.refs_1_, f32[1,4,128,128]{3,2,1,0:T(8,128)S(1)} %copy-done.2, ...), custom_call_target="tpu_custom_call" | custom-call | tf_op jit(solution)/shard_map/pallas_call | solution.py:53
  3.3 2.9 %collective-permute-start.4 = (f32[128,256]{1,0:T(8,128)S(1)}, f32[128,256]{1,0:T(8,128)S(1)}, u32[]{:S(2)}, u32[]{:S(2)}) collective-permute-start(f32[128,256]{1,0:T(8,128)S(1)} %get-tuple-element.33.even_ref), channel_id=1, source_target_pairs={{0,2},{1,3},{2,0},{3,1},{4,6},{5,7},{6,4},{7,5},{8,10},{9,11},{10,... | collective-permute-start | bytes 393224 | tf_op jit(solution)/shard_map/ppermute | solution.py:332
  6.2 0.5 %shard_map.48 = (f32[128,256]{1,0:T(8,128)S(1)}, f32[128,256]{1,0:T(8,128)S(1)}) custom-call(s32[8,128]{1,0:T(8,128)S(1)} %get-tuple-element.25.kinds_ref, f32[1024,256]{1,0:T(8,128)S(1)} %copy-done, f32[1,1024,128]{2,1,0:T(8,128)S(1)} %copy-done.1, f32[1,1024,128]{2,1,0:T(8,128)S(1)} %collective-permute-done.1.refs_1_, f32[1,4,128,128]{3,2,1,0:T(8,128)S(1)} %copy-done.2, ...), custom_call_target="tpu_custom_call" | custom-call | tf_op jit(solution)/shard_map/pallas_call | solution.py:53
  6.7 0.1 collective-permute-start.5
  6.8 3.0 %collective-permute-start = (f32[1,80,128]{2,1,0:T(8,128)S(1)}, f32[1,80,128]{2,1,0:T(8,128)S(1)}, u32[]{:S(2)}, u32[]{:S(2)}) collective-permute-start(f32[1,80,128]{2,1,0:T(8,128)S(1)} %get-tuple-element.26), channel_id=1, source_target_pairs={{0,2},{2,4},{4,6},{6,8},{8,10},{10,12},{12,14},{14,16},{16,18},{18... | collective-permute-start | bytes 122888 | tf_op jit(solution)/shard_map/ppermute | solution.py:344
  9.8 1.7 %middle.1 = (f32[1024,256]{1,0:T(8,128)S(1)}, f32[128,256]{1,0:T(8,128)S(1)}, f32[128,256]{1,0:T(8,128)S(1)}) custom-call(s32[8,128]{1,0:T(8,128)S(1)} %get-tuple-element.25.kinds_ref, f32[1024,256]{1,0:T(8,128)S(1)} %copy-done, f32[128,256]{1,0:T(8,128)S(1)} %get-tuple-element.28.even_coeff, f32[128,256]{1,0:T(8,128)S(1)} %get-tuple-element.29.odd_coeff, ...), custom_call_target="tpu_custom_call" | custom-call | tf_op jit(solution)/shard_map/middle/pallas_call | solution.py:203
  11.4 3.0 %collective-permute-done.refs_4_ = f32[1,80,128]{2,1,0:T(8,128)S(1)} collective-permute-done((f32[1,80,128]{2,1,0:T(8,128)S(1)}, f32[1,80,128]{2,1,0:T(8,128)S(1)}, u32[]{:S(2)}, u32[]{:S(2)}) %collective-permute-start) | collective-permute-done | bytes 40992 | tf_op jit(solution)/shard_map/ppermute | solution.py:344
  14.5 0.0 collective-permute-start.3
  14.5 0.9 %store.1.refs_4_ = f32[1024,256]{1,0:T(8,128)} custom-call(f32[1024,256]{1,0:T(8,128)S(1)} %get-tuple-element.42.work_ref), custom_call_target="tpu_custom_call" | custom-call | tf_op jit(solution)/shard_map/store/pallas_call | solution.py:223
  15.4 0.3 %collective-permute-done.3.refs_5_ = f32[1,80,128]{2,1,0:T(8,128)S(1)} collective-permute-done((f32[1,80,128]{2,1,0:T(8,128)S(1)}, f32[1,80,128]{2,1,0:T(8,128)S(1)}, u32[]{:S(2)}, u32[]{:S(2)}) %collective-permute-start.3) | collective-permute-done | bytes 40992 | tf_op jit(solution)/shard_map/ppermute | solution.py:323
  15.7 0.4 %shard_map.49 = (f32[128,256]{1,0:T(8,128)S(1)}, f32[128,256]{1,0:T(8,128)S(1)}, bf16[128,128]{1,0:T(8,128)(2,1)S(1)}, bf16[128,128]{1,0:T(8,128)(2,1)S(1)}, bf1...) custom-call(s32[8,128]{1,0:T(8,128)S(1)} %get-tuple-element.25.kinds_ref, ...), custom_call_target="tpu_custom_call" | custom-call | tf_op jit(solution)/shard_map/pallas_call | solution.py:53
  16.1 0.0 collective-permute-done.4.refs_3_
  16.1 0.2 %shard_map.50.even_ref = f32[128,256]{1,0:T(8,128)S(1)} custom-call(f32[128,256]{1,0:T(8,128)S(1)} %get-tuple-element.36.refs_0_, bf16[128,128]{1,0:T(8,128)(2,1)S(1)} %get-tuple-element.37.refs_1_, bf16[128,128]{1,0:T(8,128)(2,1)S(1)} %get-tuple-element.38.refs_2_, f32[128,256]{1,0:T(8,128)S(1)} %collective-permute-done.4.refs_3_), custom_call_target="tpu_custom_call" | custom-call | tf_op jit(solution)/shard_map/pallas_call | solution.py:53
  16.3 0.0 collective-permute-done.5.refs_3_
  16.3 0.9 %finish.1 = f32[1024,256]{1,0:T(8,128)} custom-call(f32[128,256]{1,0:T(8,128)S(1)} %shard_map.50.even_ref, f32[128,256]{1,0:T(8,128)S(1)} %get-tuple-element.39.refs_0_, bf16[128,128]{1,0:T(8,128)(2,1)S(1)} %get-tuple-element.40.refs_1_, bf16[128,128]{1,0:T(8,128)(2,1)S(1)} %get-tuple-element.41.refs_2_, ...), custom_call_target="tpu_custom_call", output_to_operand_aliasing={{}: (5, {})} | custom-call | tf_op jit(solution)/shard_map/finish/pallas_call | solution.py:303
  (6 shorter events, 0.0 us)
Async XLA Ops:
  0.0 0.9 %copy-start.2 = (f32[1,4,128,128]{3,2,1,0:T(8,128)S(1)}, f32[1,4,128,128]{3,2,1,0:T(8,128)}, u32[]{:S(2)}) copy-start(f32[1,4,128,128]{3,2,1,0:T(8,128)} %refs_2_.9) | copy-start | bytes 786436
  0.0 2.7 %copy-start = (f32[1024,256]{1,0:T(8,128)S(1)}, f32[1024,256]{1,0:T(8,128)}, u32[]{:S(2)}) copy-start(f32[1024,256]{1,0:T(8,128)} %x_ref.5) | copy-start | bytes 3145732
  0.0 1.4 %copy-start.3 = (s32[2]{0:T(128)S(1)}, s32[2]{0:T(128)}, u32[]{:S(2)}) copy-start(s32[2]{0:T(128)} %param.7) | copy-start | bytes 28
  0.0 2.7 %collective-permute-start.1 = (f32[1,1024,128]{2,1,0:T(8,128)}, f32[1,1024,128]{2,1,0:T(8,128)S(1)}, u32[]{:S(2)}, u32[]{:S(2)}) collective-permute-start(f32[1,1024,128]{2,1,0:T(8,128)} %refs_0_.7), channel_id=1, source_target_pairs={{0,1},{1,0},{2,3},{3,2},{4,5},{5,4},{6,7},{7,6},{8,9},{9,8},{10,11... | collective-permute-start | bytes 1572872 | tf_op jit(solution)/shard_map/ppermute | solution.py:323
  1.0 1.8 %collective-permute-start.2 = (f32[1,4,128,128]{3,2,1,0:T(8,128)S(1)}, f32[1,4,128,128]{3,2,1,0:T(8,128)S(1)}, u32[]{:S(2)}, u32[]{:S(2)}) collective-permute-start(f32[1,4,128,128]{3,2,1,0:T(8,128)S(1)} %copy-done.2), channel_id=1, source_target_pairs={{0,1},{1,0},{2,3},{3,2},{4,5},{5,4},{6,7},{7,6},{8,9},{9,8},{10,11... | collective-permute-start | bytes 786440 | tf_op jit(solution)/shard_map/ppermute | solution.py:323
  1.4 1.3 %copy-start.1 = (f32[1,1024,128]{2,1,0:T(8,128)S(1)}, f32[1,1024,128]{2,1,0:T(8,128)}, u32[]{:S(2)}) copy-start(f32[1,1024,128]{2,1,0:T(8,128)} %refs_0_.7) | copy-start | bytes 1572868
  3.3 12.8 %collective-permute-start.4 = (f32[128,256]{1,0:T(8,128)S(1)}, f32[128,256]{1,0:T(8,128)S(1)}, u32[]{:S(2)}, u32[]{:S(2)}) collective-permute-start(f32[128,256]{1,0:T(8,128)S(1)} %get-tuple-element.33.even_ref), channel_id=1, source_target_pairs={{0,2},{1,3},{2,0},{3,1},{4,6},{5,7},{6,4},{7,5},{8,10},{9,11},{10,... | collective-permute-start | bytes 393224 | tf_op jit(solution)/shard_map/ppermute | solution.py:332
  6.7 9.6 %collective-permute-start.5 = (f32[128,256]{1,0:T(8,128)S(1)}, f32[128,256]{1,0:T(8,128)S(1)}, u32[]{:S(2)}, u32[]{:S(2)}) collective-permute-start(f32[128,256]{1,0:T(8,128)S(1)} %get-tuple-element.34.odd_ref), channel_id=1, source_target_pairs={{0,1},{1,0},{2,4},{3,5},{4,2},{5,3},{6,8},{7,9},{8,6},{9,7},{10,12... | collective-permute-start | bytes 393224 | tf_op jit(solution)/shard_map/ppermute | solution.py:332
  6.8 7.7 %collective-permute-start = (f32[1,80,128]{2,1,0:T(8,128)S(1)}, f32[1,80,128]{2,1,0:T(8,128)S(1)}, u32[]{:S(2)}, u32[]{:S(2)}) collective-permute-start(f32[1,80,128]{2,1,0:T(8,128)S(1)} %get-tuple-element.26), channel_id=1, source_target_pairs={{0,2},{2,4},{4,6},{6,8},{8,10},{10,12},{12,14},{14,16},{16,18},{18... | collective-permute-start | bytes 122888 | tf_op jit(solution)/shard_map/ppermute | solution.py:344
  14.5 1.2 %collective-permute-start.3 = (f32[1,80,128]{2,1,0:T(8,128)S(1)}, f32[1,80,128]{2,1,0:T(8,128)S(1)}, u32[]{:S(2)}, u32[]{:S(2)}) collective-permute-start(f32[1,80,128]{2,1,0:T(8,128)S(1)} %collective-permute-done.refs_4_), channel_id=1, source_target_pairs={{0,1},{1,0},{2,3},{3,2},{4,5},{5,4},{6,7},{7,6},{8,9},{9,8},{10,11... | collective-permute-start | bytes 122888 | tf_op jit(solution)/shard_map/ppermute | solution.py:323
